TPU v7x, 32 devices: a whole 2x2x4 slice. The times are simulated.
32 devices in a mesh: dp: 4 (over x, core), seq: 4 (over z), tensor: 2 (over y).
Axes of the slice: x: 2, y: 2, z: 4, core: 2. Of those that a mesh axis runs over, the one named last changes fastest.
Arguments:
- tokens: bfloat16 [4, 4096, 2048], P('dp', ('seq', 'tensor')), may hold values from -6 to 6
- doc_lengths: int32 [4, 8], P('dp'), may hold values from 1 to 2048, 4096 in all within a row
- w_query: bfloat16 [2048, 2048], P(None, 'tensor'), may hold values from -0.125 to 0.125
- w_key: bfloat16 [2048, 1024], P(None, 'tensor'), may hold values from -0.125 to 0.125
- w_value: bfloat16 [2048, 1024], P(None, 'tensor'), may hold values from -0.125 to 0.125
- w_out: bfloat16 [2048, 2048], P('tensor'), may hold values from -0.5 to 0.5
- w_gate: bfloat16 [2048, 6144], P(None, 'tensor'), may hold values from -0.125 to 0.125
- w_up: bfloat16 [2048, 6144], P(None, 'tensor'), may hold values from -0.125 to 0.125
- w_down: bfloat16 [6144, 2048], P('tensor'), may hold values from -0.078125 to 0.078125
- norm_attn: float32 [2048], replicated, may hold values from 0.25 to 1.75
- norm_mlp: float32 [2048], replicated, may hold values from 0.25 to 1.75
- query_norm: float32 [128], replicated, may hold values from 0.8 to 1.8
- key_norm: float32 [128], replicated, may hold values from 0.8 to 1.8
- cotangent: bfloat16 [4, 4096, 2048], P('dp', ('seq', 'tensor')), may hold values from -6 to 6
Outputs:
- output: bfloat16 [4, 4096, 2048], P('dp', ('seq', 'tensor'))
- grad_tokens: bfloat16 [4, 4096, 2048], P('dp', ('seq', 'tensor'))
- grad_w_query: float32 [2048, 2048], P(('dp', 'seq'), 'tensor')
- grad_w_key: float32 [2048, 1024], P(('dp', 'seq'), 'tensor')
- grad_w_value: float32 [2048, 1024], P(('dp', 'seq'), 'tensor')
- grad_w_out: float32 [2048, 2048], P('tensor', ('dp', 'seq'))
- grad_w_gate: float32 [2048, 6144], P(('dp', 'seq'), 'tensor')
- grad_w_up: float32 [2048, 6144], P(('dp', 'seq'), 'tensor')
- grad_w_down: float32 [6144, 2048], P('tensor', ('dp', 'seq'))
- grad_norm_attn: float32 [2048], replicated
- grad_norm_mlp: float32 [2048], replicated
- grad_query_norm: float32 [128], replicated
- grad_key_norm: float32 [128], replicated
Inputs may be any that keep to these rules, and one draw needn't show every extreme that they name: `doc_lengths`: each row holds the lengths of the 8 documents of one sequence, in order; they sum to 4096, and the longest in each row is exactly 2048.
All inputs are finite; a program needn't handle non-finite values.
Results may differ from a plain program's by a relative error of at most 0.028.
Values may be sent and summed in bfloat16 or wider, within the bound.
A program may use at most 320 MiB of HBM per device.

v0:
```python
import functools
import math

import jax
import jax.numpy as jnp
from jax import lax
from jax.experimental import pallas as pl
from jax.experimental.pallas import tpu as pltpu
from jax.sharding import PartitionSpec as P

HD = 128
LONGEST = 2048
eps_norm = 1e-06
rope_base = 1000000.0
score_scale = HD ** (-0.5)
log2e = math.log2(math.e)
exp_scale = score_scale * log2e
BF = jnp.bfloat16
F32 = jnp.float32
MIB = 1 << 20


def params(limit=56, **kw):
    return pltpu.CompilerParams(vmem_limit_bytes=limit * MIB, **kw)


def cost(flops, bytes_accessed, transcendentals=0):
    return pl.CostEstimate(
        flops=int(flops), bytes_accessed=int(bytes_accessed), transcendentals=int(transcendentals)
    )


def dot(a, b, ca=1, cb=0):
    return lax.dot_general(a, b, (((ca,), (cb,)), ((), ())), preferred_element_type=F32)


def fixed(shape):
    zeros = (0,) * len(shape)
    return pl.BlockSpec(shape, lambda *_: zeros, pipeline_mode=pl.Buffered(1))


def grid_spec(scalars, grid, ins, outs, scratch=()):
    return pltpu.PrefetchScalarGridSpec(
        num_scalar_prefetch=scalars, grid=grid, in_specs=ins, out_specs=outs, scratch_shapes=scratch
    )


def sds(shape, dtype):
    return jax.ShapeDtypeStruct(shape, dtype)


def rms(x):
    return lax.rsqrt(jnp.mean(x * x, axis=-1, keepdims=True) + eps_norm)


def fold_rows(v):
    return jnp.sum(v.reshape(v.shape[0] // 8, 8, v.shape[1]), axis=0)


def kv_kernel(s_ref, x_ref, gain_ref, wk_ref, wv_ref, cos_ref, sin_ref, hg_ref, kv_ref, raw_ref):
    x = x_ref[...].astype(F32)
    a = (x * rms(x) * gain_ref[...]).astype(BF)
    k = dot(a, wk_ref[...])
    v = dot(a, wv_ref[...]).astype(BF)
    raw_ref[...] = k
    cosine, sine, hg = cos_ref[...], sin_ref[...], hg_ref[...]
    for h in range(k.shape[1] // HD):
        kh = k[:, h * HD : (h + 1) * HD]
        u = kh * rms(kh) * hg
        r = u * cosine + pltpu.roll(u, HD // 2, 1) * sine
        kv_ref[:, 2 * h * HD : (2 * h + 1) * HD] = r.astype(BF)
        kv_ref[:, (2 * h + 1) * HD : (2 * h + 2) * HD] = v[:, h * HD : (h + 1) * HD]


def project_kv(x, base_tile, gain, wk, wv, cosine, sine, hg, tm):
    rows, d = x.shape
    n = wk.shape[1]
    return pl.pallas_call(
        kv_kernel,
        grid_spec=grid_spec(
            1,
            (rows // tm,),
            [
                pl.BlockSpec((tm, d), lambda i, s: (i, 0)),
                fixed((1, d)),
                fixed((d, n)),
                fixed((d, n)),
                pl.BlockSpec((tm, HD), lambda i, s: (s[0] + i, 0)),
                pl.BlockSpec((tm, HD), lambda i, s: (s[0] + i, 0)),
                fixed((1, HD)),
            ],
            [
                pl.BlockSpec((tm, 2 * n), lambda i, s: (i, 0)),
                pl.BlockSpec((tm, n), lambda i, s: (i, 0)),
            ],
        ),
        out_shape=[sds((rows, 2 * n), BF), sds((rows, n), F32)],
        compiler_params=params(),
        cost_estimate=cost(4 * rows * d * n, 2 * rows * d + 4 * d * n + 8 * rows * n),
        name="project_kv",
    )(jnp.reshape(base_tile, (1,)), x, gain, wk, wv, cosine, sine, hg)


def q_kernel(
    s_ref, xa_ref, xb_ref, gain_ref, w_ref, cos_ref, sin_ref, hg_ref, x_ref, a_ref, q_ref, raw_ref,
    *, half,
):
    xin = jnp.where(pl.program_id(0) < half, xa_ref[...].astype(F32), xb_ref[...].astype(F32))
    x_ref[...] = xin.astype(BF)
    a = (xin * rms(xin) * gain_ref[...]).astype(BF)
    a_ref[...] = a
    q = dot(a, w_ref[...])
    raw_ref[...] = q
    cosine, sine, hg = cos_ref[...], sin_ref[...], hg_ref[...]
    for h in range(q.shape[1] // HD):
        qh = q[:, h * HD : (h + 1) * HD]
        u = qh * rms(qh) * hg
        r = u * cosine + pltpu.roll(u, HD // 2, 1) * sine
        q_ref[:, h * HD : (h + 1) * HD] = (r * exp_scale).astype(BF)


def project_q(xa, xb, bases, gain, w, cosine, sine, hg, tm):
    rows, d = xa.shape
    n = w.shape[1]
    half = rows // tm
    out_at = lambda i, s: (s[i // half] + i % half, 0)
    total = 2 * rows
    return pl.pallas_call(
        functools.partial(q_kernel, half=half),
        grid_spec=grid_spec(
            1,
            (2 * half,),
            [
                pl.BlockSpec((tm, d), lambda i, s: (jnp.minimum(i, half - 1), 0)),
                pl.BlockSpec((tm, d), lambda i, s: (jnp.maximum(i - half, 0), 0)),
                fixed((1, d)),
                fixed((d, n)),
                pl.BlockSpec((tm, HD), out_at),
                pl.BlockSpec((tm, HD), out_at),
                fixed((1, HD)),
            ],
            [
                pl.BlockSpec((tm, d), out_at),
                pl.BlockSpec((tm, d), out_at),
                pl.BlockSpec((tm, n), out_at),
                pl.BlockSpec((tm, n), out_at),
            ],
        ),
        out_shape=[
            sds((total, d), BF), sds((total, d), BF), sds((total, n), BF), sds((total, n), F32)
        ],
        compiler_params=params(),
        cost_estimate=cost(2 * total * d * n, 6 * total * d + 2 * d * n + 6 * total * n),
        name="project_q",
    )(bases, xa, xb, gain, w, cosine, sine, hg)


def fill_window(s_ref, at, segs, kwin, vwin):
    for n, seg in enumerate(segs):
        rows = seg.shape[0]
        base = pl.multiple_of(s_ref[at + n], math.gcd(rows, 256))
        kwin[pl.ds(base, rows), :HD] = seg[:, :HD]
        vwin[pl.ds(base, rows), :HD] = seg[:, HD:]


def flash_fwd_kernel(s_ref, q_ref, st_ref, *rest, nq, tq, tk, gs, row0, at_bases):
    segs, (o_ref, aug_ref, kwin, vwin, acc) = rest[:-5], rest[-5:]
    i = pl.program_id(1)

    @pl.when(i == 0)
    def _():
        fill_window(s_ref, at_bases, segs, kwin, vwin)
        vwin[:, HD:] = jnp.ones(vwin[:, HD:].shape, BF)

    q2 = jnp.concatenate([q_ref[:, g * HD : (g + 1) * HD] for g in range(gs)], axis=0)
    acc[...] = jnp.zeros_like(acc)
    lo, hi, flo, fhi = [s_ref[n * nq + i] for n in range(4)]

    def step(kt, masked):
        at = pl.multiple_of(kt * tk, tk)
        p = jnp.exp2(dot(q2, kwin[pl.ds(at, tk), :], 1, 1))
        if masked:
            st = st_ref[:, :1]
            j = at + lax.broadcasted_iota(jnp.int32, (tq, tk), 1)
            t = row0 + i * tq + lax.broadcasted_iota(jnp.int32, (tq, tk), 0)
            keep = (j >= st) & (j <= t)
            p = jnp.where(jnp.concatenate([keep] * gs, axis=0), p, 0.0)
        acc[...] += dot(p.astype(BF), vwin[pl.ds(at, tk), :])

    def body(kt, carry):
        inside = (kt >= flo) & (kt < fhi)

        @pl.when(inside)
        def _():
            step(kt, False)

        @pl.when(jnp.logical_not(inside))
        def _():
            step(kt, True)

        return carry

    lax.fori_loop(lo, hi, body, 0)
    total = acc[:, HD:]
    out = (acc[:, :HD] / total).astype(BF)
    neg = -jnp.log2(total)
    first = neg.astype(BF)
    rest_one = neg - first.astype(F32)
    second = rest_one.astype(BF)
    third = (rest_one - second.astype(F32)).astype(BF)
    lane = lax.broadcasted_iota(jnp.int32, total.shape, 1)
    aug = jnp.where(
        lane == 0,
        first.astype(F32),
        jnp.where(lane == 1, second.astype(F32), jnp.where(lane == 2, third.astype(F32), 0.0)),
    ).astype(BF)
    for g in range(gs):
        o_ref[:, g * HD : (g + 1) * HD] = out[g * tq : (g + 1) * tq]
        aug_ref[:, g * HD : (g + 1) * HD] = aug[g * tq : (g + 1) * tq]


def flash_fwd(scalars, q, starts_col, segs, window, chunk, rows, gs, tq, tk):
    width = gs * HD
    heads = q.shape[1] // width
    nq = rows // tq
    off = chunk * nq
    seg_specs = [pl.BlockSpec((seg.shape[0], 2 * HD), lambda h, i, s: (0, h)) for seg in segs]
    pairs = rows * (window // 2)
    return pl.pallas_call(
        functools.partial(
            flash_fwd_kernel, nq=nq, tq=tq, tk=tk, gs=gs,
            row0=window - q.shape[0] + chunk * rows, at_bases=4 * nq,
        ),
        grid_spec=grid_spec(
            1,
            (heads, nq),
            [
                pl.BlockSpec((tq, width), lambda h, i, s: (off + i, h)),
                pl.BlockSpec((tq, HD), lambda h, i, s: (off + i, 0)),
                *seg_specs,
            ],
            [
                pl.BlockSpec((tq, width), lambda h, i, s: (i, h)),
                pl.BlockSpec((tq, width), lambda h, i, s: (i, h)),
            ],
            [
                pltpu.VMEM((window, HD), BF),
                pltpu.VMEM((window, 2 * HD), BF),
                pltpu.VMEM((gs * tq, 2 * HD), F32),
            ],
        ),
        out_shape=[sds((rows, q.shape[1]), BF), sds((rows, q.shape[1]), BF)],
        compiler_params=params(),
        cost_estimate=cost(
            heads * gs * pairs * 8 * HD, 8 * q.size + sum(2 * x.size for x in segs),
            heads * gs * pairs,
        ),
        name="flash_fwd",
    )(scalars, q, starts_col, *segs)


def flash_bwd_kernel(s_ref, q_ref, st_ref, *rest, nc, ns, nb, nq, tq, tk, gs, row0, at_bases):
    das, outs, augs = rest[:nc], rest[nc : 2 * nc], rest[2 * nc : 3 * nc]
    segs = rest[3 * nc : 3 * nc + ns]
    dq_ref = rest[3 * nc + ns]
    dkvs = rest[3 * nc + ns + 1 : 3 * nc + ns + 1 + nb]
    kwin, vwin, dk, dv, dqs = rest[3 * nc + ns + 1 + nb :]
    span = dkvs[0].shape[0]

    fill_window(s_ref, at_bases, segs, kwin, vwin)
    lane = lax.broadcasted_iota(jnp.int32, (kwin.shape[0], HD), 1)
    marks = jnp.where(lane < 3, 1.0, 0.0).astype(BF)
    kwin[:, HD:] = marks
    vwin[:, HD:] = marks
    dk[...] = jnp.zeros_like(dk)
    dv[...] = jnp.zeros_like(dv)

    for i in range(nq):
        per = nq // nc
        c, r = i // per, i % per
        rows = slice(r * tq, (r + 1) * tq)
        heads = [slice(g * HD, (g + 1) * HD) for g in range(gs)]
        pile = lambda ref, rr: jnp.concatenate([ref[rr, hh] for hh in heads], axis=0)
        q2 = pile(q_ref, slice(i * tq, (i + 1) * tq))
        qa = jnp.concatenate([q2, pile(augs[c], rows)], axis=1)
        do2 = pile(das[c], rows)
        neg = -jnp.sum(
            do2.astype(F32) * pile(outs[c], rows).astype(F32), axis=1, keepdims=True
        )
        first = neg.astype(BF).astype(F32)
        second = (neg - first).astype(BF).astype(F32)
        third = neg - first - second
        ln = lax.broadcasted_iota(jnp.int32, (gs * tq, HD), 1)
        daug = jnp.where(
            ln == 0, first, jnp.where(ln == 1, second, jnp.where(ln == 2, third, 0.0))
        ).astype(BF)
        da = jnp.concatenate([do2, daug], axis=1)
        dqs[...] = jnp.zeros_like(dqs)
        lo, hi, flo, fhi = [s_ref[n * nq + i] for n in range(4)]

        def step(kt, masked, i=i, q2=q2, qa=qa, do2=do2, da=da):
            at = pl.multiple_of(kt * tk, tk)
            ka = kwin[pl.ds(at, tk), :]
            p = jnp.exp2(dot(ka, qa, 1, 1))
            if masked:
                st = st_ref[:1, i * tq : (i + 1) * tq]
                j = at + lax.broadcasted_iota(jnp.int32, (tk, tq), 0)
                t = row0 + i * tq + lax.broadcasted_iota(jnp.int32, (tk, tq), 1)
                keep = (j >= st) & (j <= t)
                p = jnp.where(jnp.concatenate([keep] * gs, axis=1), p, 0.0)
            grad = (p * dot(vwin[pl.ds(at, tk), :], da, 1, 1)).astype(BF)
            dv[pl.ds(at, tk), :] += dot(p.astype(BF), do2)
            dk[pl.ds(at, tk), :] += dot(grad, q2)
            dqs[...] += dot(grad, ka[:, :HD], 0, 0)

        def body(kt, carry, step=step, flo=flo, fhi=fhi):
            inside = (kt >= flo) & (kt < fhi)

            @pl.when(inside)
            def _():
                step(kt, False)

            @pl.when(jnp.logical_not(inside))
            def _():
                step(kt, True)

            return carry

        lax.fori_loop(lo, hi, body, 0)
        for g in range(gs):
            dq_ref[i * tq : (i + 1) * tq, heads[g]] = dqs[g * tq : (g + 1) * tq] * score_scale

    for b in range(nb):
        part = slice(b * span, (b + 1) * span)
        dkvs[b][:, :HD] = (dk[part, :] * (1.0 / log2e)).astype(BF)
        dkvs[b][:, HD:] = dv[part, :].astype(BF)


def flash_bwd(scalars, q, starts_row, das, outs, augs, segs, window, gs, tq, tk):
    span, total = q.shape
    width = gs * HD
    heads = total // width
    nc, nb, nq = len(das), window // span, span // tq
    rows = das[0].shape[0]
    chunk = pl.BlockSpec((rows, width), lambda h, s: (0, h))
    seg_specs = [pl.BlockSpec((seg.shape[0], 2 * HD), lambda h, s: (0, h)) for seg in segs]
    pairs = span * (window // 2)
    return pl.pallas_call(
        functools.partial(
            flash_bwd_kernel, nc=nc, ns=len(segs), nb=nb, nq=nq, tq=tq, tk=tk, gs=gs,
            row0=window - span, at_bases=4 * nq,
        ),
        grid_spec=grid_spec(
            1,
            (heads,),
            [
                pl.BlockSpec((span, width), lambda h, s: (0, h)),
                pl.BlockSpec((8, span), lambda h, s: (0, 0)),
                *([chunk] * (3 * nc)),
                *seg_specs,
            ],
            [
                pl.BlockSpec((span, width), lambda h, s: (0, h)),
                *([pl.BlockSpec((span, 2 * HD), lambda h, s: (0, h))] * nb),
            ],
            [
                pltpu.VMEM((window, 2 * HD), BF),
                pltpu.VMEM((window, 2 * HD), BF),
                pltpu.VMEM((window, HD), F32),
                pltpu.VMEM((window, HD), F32),
                pltpu.VMEM((gs * tq, HD), F32),
            ],
        ),
        out_shape=[sds((span, total), F32)] + [sds((span, heads * 2 * HD), BF)] * nb,
        compiler_params=params(),
        cost_estimate=cost(
            heads * gs * pairs * 14 * HD, 20 * q.size + sum(2 * x.size for x in segs),
            heads * gs * pairs,
        ),
        name="flash_bwd",
    )(scalars, q, starts_row, *das, *outs, *augs, *segs)


def mlp_kernel(*refs, np_):
    x_ref, parts = refs[0], refs[1 : 1 + np_]
    (gain_ref, cot_ref, wg_ref, wu_ref, wd_ref, m_ref, h_ref, dg_ref, du_ref, gm_ref, acc) = refs[
        1 + np_ :
    ]
    j = pl.program_id(0)

    @pl.when(j == 0)
    def _():
        rows = x_ref.shape[0]
        for r in range(0, rows, 128):
            at = slice(r, r + 128)
            h1 = x_ref[at, :].astype(F32)
            for part in parts:
                h1 = h1 + part[at, :].astype(F32)
            m_ref[at, :] = (h1 * rms(h1) * gain_ref[...]).astype(BF)

    m = m_ref[...]
    gate = dot(m, wg_ref[...])
    up = dot(m, wu_ref[...])
    gh = dot(cot_ref[...], wd_ref[...], 1, 1)
    sig = jax.nn.sigmoid(gate)
    silu = gate * sig
    h_ref[...] = (silu * up).astype(BF)
    dg = (gh * up * sig * (1.0 + gate * (1.0 - sig))).astype(BF)
    du = (gh * silu).astype(BF)
    dg_ref[...] = dg
    du_ref[...] = du
    add = dot(dg, wg_ref[...], 1, 1) + dot(du, wu_ref[...], 1, 1)

    @pl.when(j == 0)
    def _():
        acc[...] = add

    @pl.when(j > 0)
    def _():
        acc[...] += add

    @pl.when(j == pl.num_programs(0) - 1)
    def _():
        gm_ref[...] = acc[...].astype(BF)


def mlp(x, parts, cot, gain, wg, wu, wd, chunk, tf):
    rows, d = parts[0].shape
    ff = wg.shape[1]
    once = pl.Buffered(1)
    at_chunk = pl.BlockSpec((rows, d), lambda j: (chunk, 0), pipeline_mode=once)
    whole = pl.BlockSpec((rows, d), lambda j: (0, 0), pipeline_mode=once)
    tile = pl.BlockSpec((rows, tf), lambda j: (0, j))
    return pl.pallas_call(
        functools.partial(mlp_kernel, np_=len(parts)),
        grid=(ff // tf,),
        in_specs=[
            at_chunk,
            *([whole] * len(parts)),
            pl.BlockSpec((1, d), lambda j: (0, 0)),
            at_chunk,
            pl.BlockSpec((d, tf), lambda j: (0, j)),
            pl.BlockSpec((d, tf), lambda j: (0, j)),
            pl.BlockSpec((tf, d), lambda j: (j, 0)),
        ],
        out_specs=[
            pl.BlockSpec((rows, d), lambda j: (0, 0)), tile, tile, tile,
            pl.BlockSpec((rows, d), lambda j: (0, 0)),
        ],
        scratch_shapes=[pltpu.VMEM((rows, d), F32)],
        out_shape=[
            sds((rows, d), BF), sds((rows, ff), BF), sds((rows, ff), BF), sds((rows, ff), BF),
            sds((rows, d), BF),
        ],
        compiler_params=params(),
        cost_estimate=cost(10 * rows * d * ff, 6 * d * ff + 6 * rows * ff + 10 * rows * d),
        name="mlp",
    )(x, *parts, gain, cot, wg, wu, wd)


def mid_kernel(*refs, np_, ng):
    x_ref, parts, grads = refs[0], refs[1 : 1 + np_], refs[1 + np_ : 1 + np_ + ng]
    gain_ref, cot_ref, w_ref, gh_ref, ga_ref, gn_ref = refs[1 + np_ + ng :]
    h1 = x_ref[...].astype(F32)
    for part in parts:
        h1 = h1 + part[...].astype(F32)
    inv = rms(h1)
    n2 = h1 * inv
    gm = grads[0][...].astype(F32)
    for grad in grads[1:]:
        gm = gm + grad[...].astype(F32)
    g2 = gm * gain_ref[...]
    gh = cot_ref[...].astype(F32) + inv * (g2 - n2 * jnp.mean(g2 * n2, axis=1, keepdims=True))
    low = gh.astype(BF)
    gh_ref[...] = low
    ga_ref[...] = dot(low, w_ref[...], 1, 1).astype(BF)
    add = fold_rows(gm * n2)

    @pl.when(pl.program_id(0) == 0)
    def _():
        gn_ref[...] = add

    @pl.when(pl.program_id(0) > 0)
    def _():
        gn_ref[...] += add


def mid_backward(x, parts, grads, cot, gain, w_out, chunk, tm):
    rows, d = parts[0].shape
    n = w_out.shape[0]
    tiles = rows // tm
    at_chunk = pl.BlockSpec((tm, d), lambda i: (chunk * tiles + i, 0))
    tile = pl.BlockSpec((tm, d), lambda i: (i, 0))
    return pl.pallas_call(
        functools.partial(mid_kernel, np_=len(parts), ng=len(grads)),
        grid=(tiles,),
        in_specs=[
            at_chunk, *([tile] * (len(parts) + len(grads))), fixed((1, d)), at_chunk, fixed((n, d))
        ],
        out_specs=[tile, pl.BlockSpec((tm, n), lambda i: (i, 0)), pl.BlockSpec((8, d), lambda i: (0, 0))],
        out_shape=[sds((rows, d), BF), sds((rows, n), BF), sds((8, d), F32)],
        compiler_params=params(),
        cost_estimate=cost(2 * rows * d * n, 14 * rows * d + 2 * d * n),
        name="mid_backward",
    )(x, *parts, *grads, gain, cot, w_out)


def head_back(grad, raw, hg, cosine, sine):
    inv = rms(raw)
    n = raw * inv
    du = grad * cosine + pltpu.roll(grad * sine, HD // 2, 1)
    dn = du * hg
    return inv * (dn - n * jnp.mean(dn * n, axis=1, keepdims=True)), fold_rows(du * n)


def add_out(ref, value):
    @pl.when(pl.program_id(0) == 0)
    def _():
        ref[...] = value

    @pl.when(pl.program_id(0) > 0)
    def _():
        ref[...] += value


def q_back_kernel(dq_ref, raw_ref, cos_ref, sin_ref, hg_ref, low_ref, gain_ref):
    total = jnp.zeros(gain_ref.shape, F32)
    for h in range(dq_ref.shape[1] // HD):
        at = slice(h * HD, (h + 1) * HD)
        back, part = head_back(dq_ref[:, at], raw_ref[:, at], hg_ref[...], cos_ref[...], sin_ref[...])
        low_ref[:, at] = back.astype(BF)
        total = total + part
    add_out(gain_ref, total)


def q_back(dq, raw, cosine, sine, hg, tm):
    rows, n = dq.shape
    tile = pl.BlockSpec((tm, n), lambda i: (i, 0))
    table = pl.BlockSpec((tm, HD), lambda i: (i, 0))
    return pl.pallas_call(
        q_back_kernel,
        grid=(rows // tm,),
        in_specs=[tile, tile, table, table, fixed((1, HD))],
        out_specs=[tile, pl.BlockSpec((8, HD), lambda i: (0, 0))],
        out_shape=[sds((rows, n), BF), sds((8, HD), F32)],
        compiler_params=params(),
        cost_estimate=cost(30 * rows * n, 10 * rows * n),
        name="q_back",
    )(dq, raw, cosine, sine, hg)


def in_kernel(s_ref, *refs, nk):
    dkvs = refs[:nk]
    (raw_ref, dq_ref, x_ref, cos_ref, sin_ref, hg_ref, wq_ref, wk_ref, wv_ref,
     low_ref, ga_ref, gain_ref, gn_ref) = refs[nk:]
    heads = raw_ref.shape[1] // HD
    total = jnp.zeros(gain_ref.shape, F32)
    for h in range(heads):
        dk = dkvs[0][:, 2 * h * HD : (2 * h + 1) * HD].astype(F32)
        dv = dkvs[0][:, (2 * h + 1) * HD : (2 * h + 2) * HD].astype(F32)
        for ref in dkvs[1:]:
            dk = dk + ref[:, 2 * h * HD : (2 * h + 1) * HD].astype(F32)
            dv = dv + ref[:, (2 * h + 1) * HD : (2 * h + 2) * HD].astype(F32)
        at = slice(h * HD, (h + 1) * HD)
        back, part = head_back(dk, raw_ref[:, at], hg_ref[...], cos_ref[...], sin_ref[...])
        low_ref[:, at] = back.astype(BF)
        low_ref[:, (heads + h) * HD : (heads + h + 1) * HD] = dv.astype(BF)
        total = total + part
    add_out(gain_ref, total)
    low = low_ref[...]
    ga = (
        dot(dq_ref[...], wq_ref[...], 1, 1)
        + dot(low[:, : heads * HD], wk_ref[...], 1, 1)
        + dot(low[:, heads * HD :], wv_ref[...], 1, 1)
    )
    ga_ref[...] = ga.astype(BF)
    x = x_ref[...].astype(F32)
    add_out(gn_ref, fold_rows(ga * (x * rms(x))))


def in_back(dkvs, raw, dq_low, x, base_tile, cosine, sine, hg, wq, wk, wv, tm):
    rows, n = raw.shape
    d = x.shape[1]
    nq = wq.shape[1]
    moved = lambda width: pl.BlockSpec((tm, width), lambda i, s: (s[0] + i, 0))
    tile = lambda width: pl.BlockSpec((tm, width), lambda i, s: (i, 0))
    return pl.pallas_call(
        functools.partial(in_kernel, nk=len(dkvs)),
        grid_spec=grid_spec(
            1,
            (rows // tm,),
            [
                *([moved(2 * n)] * len(dkvs)), tile(n), moved(nq), moved(d), moved(HD), moved(HD),
                fixed((1, HD)), fixed((d, nq)), fixed((d, n)), fixed((d, n)),
            ],
            [
                tile(2 * n), tile(d),
                pl.BlockSpec((8, HD), lambda i, s: (0, 0)), pl.BlockSpec((8, d), lambda i, s: (0, 0)),
            ],
        ),
        out_shape=[sds((rows, 2 * n), BF), sds((rows, d), BF), sds((8, HD), F32), sds((8, d), F32)],
        compiler_params=params(),
        cost_estimate=cost(
            2 * rows * d * (nq + 2 * n), 4 * rows * d + 2 * d * (nq + 2 * n) + 12 * rows * n
        ),
        name="in_back",
    )(jnp.reshape(base_tile, (1,)), *dkvs, raw, dq_low, x, cosine, sine, hg, wq, wk, wv)


def wgrad_kernel(s_ref, *refs, nt, na, row_type, ns):
    out_ref, aside = refs[2 * nt + na], refs[2 * nt + na + 1 :]
    if row_type:
        turned = aside[0]

        @pl.when(pl.program_id(1) == 0)
        def _():
            for n in range(nt):
                turned[n] = refs[2 * n][...].T

        total = dot(turned[0], refs[1][...])
        for n in range(1, nt):
            total = total + dot(turned[n], refs[2 * n + 1][...])
    else:
        total = dot(refs[0][...], refs[1][...], 0, 0)
        for n in range(1, nt):
            total = total + dot(refs[2 * n][...], refs[2 * n + 1][...], 0, 0)
    for n in range(ns):
        if row_type:
            size = total.shape[0] // ns
            piece = total[n * size : (n + 1) * size]
        else:
            size = total.shape[1] // ns
            piece = total[:, n * size : (n + 1) * size]
        for add in refs[2 * nt : 2 * nt + na]:
            piece = piece + add[0, n].astype(F32)
        out_ref[0, n] = piece.astype(BF)


def wgrad(terms, blocks, addends, row_type, nd, ns, rows):
    nb, nt = len(blocks), len(terms)
    scalars = jnp.stack(
        [jnp.asarray(v, jnp.int32) for v in blocks]
        + [jnp.asarray(v, jnp.int32) for t in terms for v in (t[1], t[3])]
    )
    left, right = terms[0][0].shape[1], terms[0][2].shape[1]
    ins = []
    if row_type:
        bw = left // nd
        tile = min(512, right)
        steps = right // tile
        for n in range(nt):
            ins.append(pl.BlockSpec((rows, bw), lambda b, t, s, n=n: (s[nb + 2 * n], s[b])))
            ins.append(pl.BlockSpec((rows, tile), lambda b, t, s, n=n: (s[nb + 2 * n + 1], t)))
        out_dims = (ns, bw // ns, right)
        block = (1, ns, bw // ns, tile)
        at = lambda b, t, s: (b, 0, 0, t)
        add_at = lambda k: lambda b, t, s: (k, 0, 0, t)
        scratch = [pltpu.VMEM((nt, bw, rows), BF)]
        flops = 2 * nb * nt * rows * bw * right
    else:
        bw = right // nd
        tile = min(512, left)
        steps = left // tile
        for n in range(nt):
            ins.append(pl.BlockSpec((rows, tile), lambda b, t, s, n=n: (s[nb + 2 * n], t)))
            ins.append(pl.BlockSpec((rows, bw), lambda b, t, s, n=n: (s[nb + 2 * n + 1], s[b])))
        out_dims = (ns, left, bw // ns)
        block = (1, ns, tile, bw // ns)
        at = lambda b, t, s: (b, 0, t, 0)
        add_at = lambda k: lambda b, t, s: (k, 0, t, 0)
        scratch = []
        flops = 2 * nb * nt * rows * bw * left
    operands = [v for t in terms for v in (t[0], t[2])]
    for arr, k in addends:
        ins.append(pl.BlockSpec(block, add_at(k)))
        operands.append(arr)
    size = nb * math.prod(out_dims)
    return pl.pallas_call(
        functools.partial(wgrad_kernel, nt=nt, na=len(addends), row_type=row_type, ns=ns),
        grid_spec=grid_spec(1, (nb, steps), ins, pl.BlockSpec(block, at), scratch),
        out_shape=sds((nb, *out_dims), BF),
        compiler_params=params(),
        cost_estimate=cost(
            flops, 2 * size * (1 + len(addends)) + 2 * nt * rows * (left + right)
        ),
        name="wgrad",
    )(scalars, *operands)


def reduce_weights(terms, row_type, nd, ns, rows, z):
    d = lax.axis_index("dp")
    make = lambda blocks, adds: wgrad(terms, blocks, adds, row_type, nd, ns, rows)
    side = [(k, k ^ 1) for k in range(nd)]
    across = [(k, k ^ 2) for k in range(nd)]
    got = lax.ppermute(make([d ^ 1, d ^ 3], []), "dp", side)
    far = make([d ^ 2], [(got, 1)])
    near = make([d], [(got, 0)])
    come = lax.ppermute(far, "dp", across)

    def piece(j):
        j = jnp.clip(j, 0, ns - 1)
        take = lambda v: lax.dynamic_index_in_dim(v[0], j, 0, keepdims=False).astype(F32)
        return take(near) + take(come)

    total, right, left = piece(z), None, None
    for s in range(1, ns):
        send_right, send_left = piece(ns - s + z), piece(z + s - ns)
        if right is not None:
            send_right, send_left = send_right + right.astype(F32), send_left + left.astype(F32)
        right = lax.ppermute(send_right.astype(BF), "seq", [(k, k + 1) for k in range(s)])
        left = lax.ppermute(
            send_left.astype(BF), "seq", [(ns - 1 - k, ns - 2 - k) for k in range(s)]
        )
    return total + right.astype(F32) + left.astype(F32)


def final_kernel(x_ref, ga_ref, gb_ref, h0_ref, h1_ref, gain_ref, s_ref, out_ref):
    x = x_ref[...].astype(F32)
    inv = rms(x)
    n1 = x * inv
    g1 = (ga_ref[...].astype(F32) + gb_ref[...].astype(F32)) * gain_ref[...]
    gh = jnp.where(s_ref[0] == 0, h0_ref[...].astype(F32), h1_ref[...].astype(F32))
    out_ref[...] = (gh + inv * (g1 - n1 * jnp.mean(g1 * n1, axis=1, keepdims=True))).astype(BF)


def final(x, ga, gb, h0, h1, gain, y, tm):
    rows, d = x.shape
    tile = pl.BlockSpec((tm, d), lambda i: (i, 0))
    return pl.pallas_call(
        final_kernel,
        grid=(rows // tm,),
        in_specs=[tile] * 5 + [fixed((1, d)), pl.BlockSpec(memory_space=pltpu.SMEM)],
        out_specs=tile,
        out_shape=sds((rows, d), BF),
        compiler_params=params(),
        cost_estimate=cost(20 * rows * d, 12 * rows * d),
        name="final",
    )(x, ga, gb, h0, h1, gain, jnp.reshape(y, (1,)))


def per_device(
    tokens, doc_lengths, w_query, w_key, w_value, w_out, w_gate, w_up, w_down,
    norm_attn, norm_mlp, query_norm, key_norm, cotangent, *, nd, ns, nt,
):
    tokens, cotangent = tokens[0], cotangent[0]
    own_rows, d = tokens.shape
    span = own_rows * nt
    rows = span // 2
    heads_kv = w_key.shape[1] // HD
    gs = w_query.shape[1] // w_key.shape[1]
    z, y = lax.axis_index("seq"), lax.axis_index("tensor")
    row = lambda v: v[None, :]
    tm = 256
    tq, tk = 256, 512
    swap = lambda v: lax.ppermute(v, "tensor", [(0, 1), (1, 0)])
    pick = lambda a, b: jnp.where(y == 0, a, b)

    back = min(ns - 1, -(-(LONGEST - 1) // span))
    window = (back + 1) * span
    ends = jnp.cumsum(doc_lengths[0])
    positions = z * span + jnp.arange(span, dtype=jnp.int32)
    starts = jnp.max(jnp.where(ends[None, :] <= positions[:, None], ends[None, :], 0), axis=1)
    half = HD // 2
    inverse = rope_base ** (-(jnp.arange(half, dtype=F32) * 2.0 / HD))
    angles = (positions - starts).astype(F32)[:, None] * inverse[None, :]
    cosine = jnp.tile(jnp.cos(angles), (1, 2))
    sine = jnp.sin(angles)
    sine = jnp.concatenate([-sine, sine], axis=1)
    rel = jnp.clip(starts - (z - back) * span, 0, window - 1)
    starts_col = jnp.broadcast_to(rel[:, None], (span, HD))
    starts_row = jnp.broadcast_to(rel[None, :], (8, span))

    def bounds(first_row, count):
        heads = rel[first_row : first_row + count : tq]
        tails = rel[first_row + tq - 1 : first_row + count : tq]
        at = window - span + first_row + tq * jnp.arange(count // tq, dtype=jnp.int32)
        return [heads // tk, (at + tq - 1) // tk + 1, (tails + tk - 1) // tk, (at + 1) // tk]

    if nt == 2:
        other = swap(tokens)
        cot_in, other = lax.optimization_barrier((cotangent, other))
        cot_other = swap(cot_in)
        pieces, bases = [tokens, other], [y * rows, (1 - y) * rows]
        cot = jnp.concatenate([pick(cotangent, cot_other), pick(cot_other, cotangent)], axis=0)
    else:
        everything = lax.all_gather(tokens, "tensor", axis=0, tiled=True)
        cot = lax.all_gather(cotangent, "tensor", axis=0, tiled=True)
        pieces, bases = [everything[:rows], everything[rows:]], [0, rows]
    bases = [jnp.asarray(b, jnp.int32) for b in bases]
    base_tiles = [b // tm for b in bases]

    hops, raws, seg_bases = [], [], []
    ahead = [(k, k + 1) for k in range(ns - 1)]
    for x_piece, base, base_tile in zip(pieces, bases, base_tiles):
        kv, raw = project_kv(
            x_piece, base_tile, row(norm_attn), w_key, w_value, cosine, sine, row(key_norm), tm
        )
        raws.append(raw)
        for hop in range(back + 1):
            hops.append(kv)
            seg_bases.append((back - hop) * span + base)
            if hop < back:
                kv = lax.ppermute(kv, "seq", ahead)
    x_all, attn_in, query, q_raw = project_q(
        pieces[0], pieces[1], jnp.stack(base_tiles), row(norm_attn), w_query, cosine, sine,
        row(query_norm), tm,
    )

    outs, augs, parts = [], [], []
    for c in range(2):
        scalars = jnp.concatenate([*bounds(c * rows, rows), jnp.stack(seg_bases)])
        out, aug = flash_fwd(scalars, query, starts_col, hops, window, c, rows, gs, tq, tk)
        outs.append(out)
        augs.append(aug)
        partial = dot(out, w_out).astype(BF)
        parts.append([partial, swap(partial)] if nt == 2 else [lax.psum(partial, "tensor")])

    low_mlp, hidden, d_gate, d_up, grads = [], [], [], [], []
    tf = min(256, w_gate.shape[1])
    for c in range(2):
        m, h, dg, du, gm = mlp(x_all, parts[c], cot, row(norm_mlp), w_gate, w_up, w_down, c, tf)
        low_mlp.append(m)
        hidden.append(h)
        d_gate.append(dg)
        d_up.append(du)
        grads.append([gm, swap(gm)] if nt == 2 else [lax.psum(gm, "tensor")])
    shrink = functools.partial(reduce_weights, nd=nd, ns=ns, rows=rows, z=z)
    g_down = shrink([(hidden[c], 0, cot, c) for c in range(2)], False)
    g_gate = shrink([(low_mlp[c], 0, d_gate[c], 0) for c in range(2)], True)
    g_up = shrink([(low_mlp[c], 0, d_up[c], 0) for c in range(2)], True)

    gh, g_att, g_norm_two = [], [], []
    for c in range(2):
        low, ga, gn = mid_backward(x_all, parts[c], grads[c], cot, row(norm_mlp), w_out, c, tm)
        gh.append(low)
        g_att.append(ga)
        g_norm_two.append(gn)
    g_out = shrink([(outs[c], 0, gh[c], 0) for c in range(2)], False)
    scalars = jnp.concatenate([*bounds(0, span), jnp.stack(seg_bases)])
    dq, *dkvs = flash_bwd(
        scalars, query, starts_row, g_att, outs, augs, hops, window, gs, tq, tk
    )
    behind = [(k + 1, k) for k in range(ns - 1)]
    come = None
    for b in range(back):
        send = dkvs[b]
        if come is not None:
            send = (send.astype(F32) + come.astype(F32)).astype(BF)
        come = lax.ppermute(send, "seq", behind)
    dkv = [dkvs[back]] + ([come] if come is not None else [])

    dq_low, g_qn = q_back(dq, q_raw, cosine, sine, row(query_norm), tm)
    g_query = shrink([(attn_in, c, dq_low, c) for c in range(2)], True)
    lows, gas, g_kn, g_norm_one = [None] * 2, [None] * 2, [], []
    for n in (1, 0):
        lows[n], gas[n], gain_part, norm_part = in_back(
            dkv, raws[n], dq_low, x_all, base_tiles[n], cosine, sine, row(key_norm),
            w_query, w_key, w_value, tm,
        )
        g_kn.append(gain_part)
        g_norm_one.append(norm_part)
    kv_cut = heads_kv * HD
    g_kv = shrink([(attn_in, bases[n] // rows, lows[n], 0) for n in range(2)], True)

    downs = [dot(hidden[c], w_down).astype(BF) for c in range(2)]
    up32 = lambda v: v.astype(F32)
    if nt == 2:
        come_down = swap(pick(downs[1], downs[0]))
        result = up32(tokens) + up32(pick(downs[0], downs[1])) + up32(come_down)
        for n in range(2):
            result = result + up32(pick(parts[0][n], parts[1][n]))
        grad_tokens = final(tokens, gas[0], swap(gas[1]), gh[0], gh[1], row(norm_attn), y, tm)
    else:
        scatter = lambda v: lax.psum_scatter(v, "tensor", scatter_dimension=0, tiled=True)
        mine = lambda pair: lax.dynamic_slice_in_dim(
            jnp.concatenate(pair, axis=0), y * own_rows, own_rows
        )
        result = up32(tokens) + up32(scatter(jnp.concatenate(downs, axis=0)))
        result = result + up32(mine([parts[0][0], parts[1][0]]))
        x32 = up32(tokens)
        inv = rms(x32)
        n1 = x32 * inv
        g1 = up32(scatter(jnp.concatenate(gas, axis=0))) * row(norm_attn)
        moved = inv * (g1 - n1 * jnp.mean(g1 * n1, axis=1, keepdims=True))
        grad_tokens = (up32(mine(gh)) + moved).astype(BF)

    share = 1.0 / nt
    fold = lambda pair: jnp.sum(pair[0] + pair[1], axis=0)
    packed = jnp.concatenate(
        [fold(g_norm_one), fold(g_norm_two) * share, jnp.sum(g_qn, axis=0), fold(g_kn)]
    )
    packed = lax.psum(packed, ("dp", "seq", "tensor"))
    return (
        result.astype(BF)[None], grad_tokens[None], g_query, g_kv[:, :kv_cut], g_kv[:, kv_cut:],
        g_out, g_gate, g_up, g_down,
        packed[:d], packed[d : 2 * d], packed[2 * d : 2 * d + HD], packed[2 * d + HD :],
    )


def solution(mesh):
    sizes = dict(nd=mesh.shape["dp"], ns=mesh.shape["seq"], nt=mesh.shape["tensor"])
    rows, cols, both = P("dp", ("seq", "tensor"), None), P(None, "tensor"), ("dp", "seq")
    return jax.shard_map(
        functools.partial(per_device, **sizes),
        mesh=mesh,
        in_specs=(
            rows, P("dp", None), cols, cols, cols, P("tensor", None), cols, cols, P("tensor", None),
            P(), P(), P(), P(), rows,
        ),
        out_specs=(
            rows, rows, P(both, "tensor"), P(both, "tensor"), P(both, "tensor"), P("tensor", both),
            P(both, "tensor"), P(both, "tensor"), P("tensor", both), P(), P(), P(), P(),
        ),
        check_vma=False,
    )
```

profile of v0, /device:TPU:0, one launch (start us, length us, event | category | flops | bytes accessed | tf_op | source)
XLA Modules:
  0.0 1162.9 jit_solution(8009187186435205763)
XLA Ops:
  8.8 6.5 project_kv.2
  18.9 30.8 %collective-permute-done.xb_ref.x_ref = bf16[512,2048]{1,0:T(8,128)(2,1)} collective-permute-done((bf16[512,2048]{1,0:T(8,128)(2,1)}, bf16[512,2048]{1,0:T(8,128)(2,1)}, u32[]{:S(2)}, u32[]{:S(2)}) %collective-permute-start) | collective-permute-done | bytes 2097184 | tf_op jit(solution)/shard_map/ppermute | solution.py:755
  49.6 6.5 project_kv.3
  64.9 18.9 %collective-permute-done.3.rest_4_.rest_10_ = bf16[512,1024]{1,0:T(8,128)(2,1)S(1)} collective-permute-done((bf16[512,1024]{1,0:T(8,128)(2,1)}, bf16[512,1024]{1,0:T(8,128)(2,1)S(1)}, u32[]{:S(2)}, u32[]{:S(2)}) %collective-permute-start.3) | collective-permute-done | bytes 1048608 | tf_op jit(solution)/shard_map/ppermute | solution.py:803
  92.7 13.2 %project_q.1 = (bf16[1024,2048]{1,0:T(8,128)(2,1)}, bf16[1024,2048]{1,0:T(8,128)(2,1)}, bf16[1024,1024]{1,0:T(8,128)(2,1)}, f32[1024,1024]{1,0:T(8,128)}) custom-call(s32[2]{0:T(128)} %pad_add_fusion.10.s_ref, bf16[512,2048]{1,0:T(8,128)(2,1)} %bitcast.184, bf16[512,2048]{1,0:T(8,128)(2,1)} %collective-permute-done.xb_ref.x_ref, f32[1,2048]{1,0:T(1,128)} %bitcast.194, ...), custom_call_target="tpu_custom_call" | custom-call | flops 4294967296 | bytes 23068672 | tf_op jit(solution)/shard_map/project_q/pallas_call | solution.py:128
  106.1 20.4 %collective-permute-done.4.rest_5_.rest_11_ = bf16[512,1024]{1,0:T(8,128)(2,1)} collective-permute-done((bf16[512,1024]{1,0:T(8,128)(2,1)S(1)}, bf16[512,1024]{1,0:T(8,128)(2,1)}, u32[]{:S(2)}, u32[]{:S(2)}) %collective-permute-start.4) | collective-permute-done | bytes 1048608 | tf_op jit(solution)/shard_map/ppermute | solution.py:803
  127.5 13.3 %flash_fwd.2 = (bf16[512,1024]{1,0:T(8,128)(2,1)}, bf16[512,1024]{1,0:T(8,128)(2,1)}) custom-call(s32[14]{0:T(128)} %concatenate.19.s_ref, bf16[1024,1024]{1,0:T(8,128)(2,1)} %get-tuple-element.59.q_ref, s32[1024,128]{1,0:T(8,128)} %broadcast_in_dim.29.st_ref, bf16[512,1024]{1,0:T(8,128)(2,1)} %get-tuple-element.60.rest_0_.rest_6_, ...), custom_call_target="tpu_custom_call" | custom-call | flops 6442450944 | bytes 14680064 | tf_op jit(solution)/shard_map/flash_fwd/pallas_call | solution.py:229
  146.0 15.0 %flash_fwd.3 = (bf16[512,1024]{1,0:T(8,128)(2,1)}, bf16[512,1024]{1,0:T(8,128)(2,1)}) custom-call(s32[14]{0:T(128)} %concatenate.21.s_ref, bf16[1024,1024]{1,0:T(8,128)(2,1)} %get-tuple-element.59.q_ref, s32[1024,128]{1,0:T(8,128)} %broadcast_in_dim.29.st_ref, bf16[512,1024]{1,0:T(8,128)(2,1)} %get-tuple-element.60.rest_0_.rest_6_, ...), custom_call_target="tpu_custom_call" | custom-call | flops 6442450944 | bytes 14680064 | tf_op jit(solution)/shard_map/flash_fwd/pallas_call | solution.py:229
  171.5 21.6 %collective-permute-done.5.refs_2_ = bf16[512,2048]{1,0:T(8,128)(2,1)} collective-permute-done((bf16[512,2048]{1,0:T(8,128)(2,1)S(1)}, bf16[512,2048]{1,0:T(8,128)(2,1)}, u32[]{:S(2)}, u32[]{:S(2)}) %collective-permute-start.5) | collective-permute-done | bytes 2097184 | tf_op jit(solution)/shard_map/ppermute | solution.py:755
  193.1 75.4 %mlp.2 = (bf16[512,2048]{1,0:T(8,128)(2,1)}, bf16[512,3072]{1,0:T(8,128)(2,1)}, bf16[512,3072]{1,0:T(8,128)(2,1)}, bf16[512,3072]{1,0:T(8,128)(2,1)}, bf16[512,2048]{1,0:T(8,128)(2,1)}) custom-call(bf16[1024,2048]{1,0:T(8,128)(2,1)} %get-tuple-element.58.refs_0_.refs_4_, bf16[512,2048]{1,0:T(8,128)(2,1)} %copy-done.6, ...), custom_call_target="tpu_custom_call" | custom-call | flops 32212254720 | bytes 57671680 | tf_op jit(solution)/shard_map/mlp/pallas_call | solution.py:434
  271.5 75.4 %mlp.3 = (bf16[512,2048]{1,0:T(8,128)(2,1)}, bf16[512,3072]{1,0:T(8,128)(2,1)}, bf16[512,3072]{1,0:T(8,128)(2,1)}, bf16[512,3072]{1,0:T(8,128)(2,1)}, bf16[512,2048]{1,0:T(8,128)(2,1)}) custom-call(bf16[1024,2048]{1,0:T(8,128)(2,1)} %get-tuple-element.58.refs_0_.refs_4_, bf16[512,2048]{1,0:T(8,128)(2,1)} %convolution_convert_fusion.2.refs_1_, ...), custom_call_target="tpu_custom_call" | custom-call | flops 32212254720 | bytes 57671680 | tf_op jit(solution)/shard_map/mlp/pallas_call | solution.py:434
  349.3 9.6 convolution_convert_fusion.1
  359.0 12.0 %mid_backward.2 = (bf16[512,2048]{1,0:T(8,128)(2,1)}, bf16[512,1024]{1,0:T(8,128)(2,1)}, f32[8,2048]{1,0:T(8,128)}) custom-call(bf16[1024,2048]{1,0:T(8,128)(2,1)} %get-tuple-element.58.refs_0_.refs_4_, bf16[512,2048]{1,0:T(8,128)(2,1)} %copy-done.6, bf16[512,2048]{1,0:T(8,128)(2,1)} %collective-permute-done.5.refs_2_, ...), custom_call_target="tpu_custom_call" | custom-call | flops 2147483648 | bytes 18874368 | tf_op jit(solution)/shard_map/mid_backward/pallas_call | solution.py:494
  370.9 17.7 %collective-permute-done.10.refs_4_ = bf16[512,2048]{1,0:T(8,128)(2,1)} collective-permute-done((bf16[512,2048]{1,0:T(8,128)(2,1)}, bf16[512,2048]{1,0:T(8,128)(2,1)}, u32[]{:S(2)}, u32[]{:S(2)}) %collective-permute-start.10) | collective-permute-done | bytes 2097184 | tf_op jit(solution)/shard_map/ppermute | solution.py:755
  388.6 11.4 mid_backward.3
  400.6 30.5 %flash_bwd.1 = (f32[1024,1024]{1,0:T(8,128)}, bf16[1024,1024]{1,0:T(8,128)(2,1)}, bf16[1024,1024]{1,0:T(8,128)(2,1)}, bf16[1024,1024]{1,0:T(8,128)(2,1)}) custom-call(s32[22]{0:T(128)} %concatenate.22.s_ref, bf16[1024,1024]{1,0:T(8,128)(2,1)} %get-tuple-element.59.q_ref, s32[8,1024]{1,0:T(8,128)} %broadcast_in_dim.33.st_ref, ...), custom_call_target="tpu_custom_call" | custom-call | flops 22548578304 | bytes 27262976 | tf_op jit(solution)/shard_map/flash_bwd/pallas_call | solution.py:348
  431.1 9.0 q_back.1
  440.1 7.7 wgrad.18
  447.9 7.3 wgrad.24
  455.7 10.9 broadcast_select_fusion
  468.8 16.3 %wgrad.27 = bf16[2,4,128,3072]{3,2,1,0:T(8,128)(2,1)} custom-call(s32[6]{0:T(128)} %pad_add_fusion.13.s_ref, bf16[512,2048]{1,0:T(8,128)(2,1)} %get-tuple-element.88.refs_0_, bf16[512,3072]{1,0:T(8,128)(2,1)} %get-tuple-element.89.refs_1_, bf16[512,2048]{1,0:T(8,128)(2,1)} %get-tuple-element.90.refs_2_, bf16[512,3072]{1,0:T(8,128)(2,1)} %get-tuple-element.91.refs_3_), custom_call_target="tpu_custom_call" | custom-call | flops 6442450944 | bytes 16777216 | tf_op jit(solution)/shard_map/wgrad/pallas_call | solution.py:678
  493.2 16.3 %wgrad.30 = bf16[2,4,128,3072]{3,2,1,0:T(8,128)(2,1)} custom-call(s32[6]{0:T(128)} %pad_add_fusion.13.s_ref, bf16[512,2048]{1,0:T(8,128)(2,1)} %get-tuple-element.88.refs_0_, bf16[512,3072]{1,0:T(8,128)(2,1)} %get-tuple-element.92.refs_1_, bf16[512,2048]{1,0:T(8,128)(2,1)} %get-tuple-element.90.refs_2_, bf16[512,3072]{1,0:T(8,128)(2,1)} %get-tuple-element.93.refs_3_), custom_call_target="tpu_custom_call" | custom-call | flops 6442450944 | bytes 16777216 | tf_op jit(solution)/shard_map/wgrad/pallas_call | solution.py:678
  516.1 15.8 %wgrad.33 = bf16[2,4,3072,128]{3,2,1,0:T(8,128)(2,1)} custom-call(s32[6]{0:T(128)} %stack.148.s_ref, bf16[512,3072]{1,0:T(8,128)(2,1)} %get-tuple-element.64.refs_0_, bf16[1024,2048]{1,0:T(8,128)(2,1)} %pad_maximum_fusion.refs_4_.refs_6_.refs_1_.refs_3_, bf16[512,3072]{1,0:T(8,128)(2,1)} %get-tuple-element.66.refs_2_, ...), custom_call_target="tpu_custom_call" | custom-call | flops 6442450944 | bytes 16777216 | tf_op jit(solution)/shard_map/wgrad/pallas_call | solution.py:678
  539.1 7.4 collective-permute-done.11
  546.6 22.7 %collective-permute-start.16 = (bf16[128,1024]{1,0:T(8,128)(2,1)}, bf16[128,1024]{1,0:T(8,128)(2,1)S(1)}, u32[]{:S(2)}, u32[]{:S(2)}) collective-permute-start(bf16[128,1024]{1,0:T(8,128)(2,1)} %get-tuple-element.125), channel_id=1, source_target_pairs={{0,2},{1,3},{8,10},{9,11},{16,18},{17,19},{24,26},{25,27}} | collective-permute-start | bytes 786440 | tf_op jit(solution)/shard_map/ppermute | solution.py:710
  594.2 7.5 fusion
  602.8 23.7 %collective-permute-start.33 = (bf16[1024,128]{1,0:T(8,128)(2,1)S(1)}, bf16[1024,128]{1,0:T(8,128)(2,1)S(1)}, u32[]{:S(2)}, u32[]{:S(2)}) collective-permute-start(bf16[1024,128]{1,0:T(8,128)(2,1)S(1)} %fusion.24), channel_id=1, source_target_pairs={{0,2},{2,4},{1,3},{3,5},{8,10},{10,12},{9,11},{11,13},{16,18},{18,... | collective-permute-start | bytes 786440 | tf_op jit(solution)/shard_map/ppermute | solution.py:710
  634.6 28.0 %collective-permute-start.18 = (bf16[128,1024]{1,0:T(8,128)(2,1)S(1)}, bf16[128,1024]{1,0:T(8,128)(2,1)S(1)}, u32[]{:S(2)}, u32[]{:S(2)}) collective-permute-start(bf16[128,1024]{1,0:T(8,128)(2,1)S(1)} %copy-done.25), channel_id=1, source_target_pairs={{0,2},{2,4},{4,6},{1,3},{3,5},{5,7},{8,10},{10,12},{12,14},{9,11},... | collective-permute-start | bytes 786440 | tf_op jit(solution)/shard_map/ppermute | solution.py:710
  665.1 12.5 %in_back.2 = (bf16[512,1024]{1,0:T(8,128)(2,1)}, bf16[512,2048]{1,0:T(8,128)(2,1)}, f32[8,128]{1,0:T(8,128)}, f32[8,2048]{1,0:T(8,128)}) custom-call(s32[1]{0:T(128)} %bitcast.1.s_ref, bf16[1024,1024]{1,0:T(8,128)(2,1)} %get-tuple-element.73.refs_0_, bf16[1024,1024]{1,0:T(8,128)(2,1)} %copy-done.11, f32[512,512]{1,0:T(8,128)} %get-tuple-element.76.refs_2_, ...), custom_call_target="tpu_custom_call" | custom-call | flops 4294967296 | bytes 15728640 | tf_op jit(solution)/shard_map/in_back/pallas_call | solution.py:587
  677.6 12.5 %in_back.3 = (bf16[512,1024]{1,0:T(8,128)(2,1)}, bf16[512,2048]{1,0:T(8,128)(2,1)}, f32[8,128]{1,0:T(8,128)}, f32[8,2048]{1,0:T(8,128)}) custom-call(s32[1]{0:T(128)} %bitcast.2.s_ref, bf16[1024,1024]{1,0:T(8,128)(2,1)} %get-tuple-element.73.refs_0_, bf16[1024,1024]{1,0:T(8,128)(2,1)} %copy-done.11, f32[512,512]{1,0:T(8,128)} %get-tuple-element.81.refs_2_, ...), custom_call_target="tpu_custom_call" | custom-call | flops 4294967296 | bytes 15728640 | tf_op jit(solution)/shard_map/in_back/pallas_call | solution.py:587
  690.1 7.7 wgrad.21
  697.9 10.0 wgrad.29
  711.7 6.5 collective-permute-start.34
  718.3 10.0 wgrad.32
  728.6 10.0 wgrad.28
  741.5 9.6 wgrad.35
  752.9 10.0 wgrad.31
  762.9 9.7 wgrad.34
  772.7 178.3 %psum.7 = f32[4352]{0:T(1024)S(1)} all-reduce(f32[4352]{0:T(1024)S(1)} %pad_maximum_fusion.2), channel_id=1, replica_groups=mesh['dp'=4,'seq'=4,'tensor'=2] {'dp','seq','tensor'}, use_global_device_ids=true, to_apply=%region_6.7 | all-reduce | flops 4352 | bytes 34816 | tf_op jit(solution)/shard_map/psum | solution.py:892
  966.2 7.9 final.1
  992.7 15.0 %collective-permute-done.24 = bf16[128,1024]{1,0:T(8,128)(2,1)S(1)} collective-permute-done((bf16[128,1024]{1,0:T(8,128)(2,1)S(1)}, bf16[128,1024]{1,0:T(8,128)(2,1)S(1)}, u32[]{:S(2)}, u32[]{:S(2)}) %collective-permute-start.24) | collective-permute-done | bytes 262176 | tf_op jit(solution)/shard_map/ppermute | solution.py:710
  1016.5 9.8 collective-permute-done.25
  1042.6 6.0 collective-permute-done.56
  1065.2 5.9 collective-permute-done.41
  1077.6 10.3 collective-permute-done.49
  1096.1 8.7 collective-permute-done.57
  1122.9 12.9 %collective-permute-done.45 = bf16[128,3072]{1,0:T(8,128)(2,1)S(1)} collective-permute-done((bf16[128,3072]{1,0:T(8,128)(2,1)S(1)}, bf16[128,3072]{1,0:T(8,128)(2,1)S(1)}, u32[]{:S(2)}, u32[]{:S(2)}) %collective-permute-start.45) | collective-permute-done | bytes 786464 | tf_op jit(solution)/shard_map/ppermute | solution.py:711
  1138.5 13.1 %collective-permute-done.53 = bf16[128,3072]{1,0:T(8,128)(2,1)S(1)} collective-permute-done((bf16[128,3072]{1,0:T(8,128)(2,1)S(1)}, bf16[128,3072]{1,0:T(8,128)(2,1)S(1)}, u32[]{:S(2)}, u32[]{:S(2)}) %collective-permute-start.53) | collective-permute-done | bytes 786464 | tf_op jit(solution)/shard_map/ppermute | solution.py:711
  (271 shorter events, 243.4 us)
Async XLA Ops:
  0.6 49.0 %collective-permute-start = (bf16[512,2048]{1,0:T(8,128)(2,1)}, bf16[512,2048]{1,0:T(8,128)(2,1)}, u32[]{:S(2)}, u32[]{:S(2)}) collective-permute-start(bf16[512,2048]{1,0:T(8,128)(2,1)} %bitcast.182), channel_id=1, source_target_pairs={{0,1},{1,0},{2,3},{3,2},{4,5},{5,4},{6,7},{7,6},{8,9},{9,8},{10,11... | collective-permute-start | bytes 6291464 | tf_op jit(solution)/shard_map/ppermute | solution.py:755
  15.3 45.2 %collective-permute-start.1 = (bf16[512,1024]{1,0:T(8,128)(2,1)}, bf16[512,1024]{1,0:T(8,128)(2,1)S(1)}, u32[]{:S(2)}, u32[]{:S(2)}) collective-permute-start(bf16[512,1024]{1,0:T(8,128)(2,1)} %get-tuple-element.60.rest_0_.rest_6_), channel_id=1, source_target_pairs={{0,2},{2,4},{4,6},{1,3},{3,5},{5,7},{8,10},{10,12},{12,14},{9,11},... | collective-permute-start | bytes 3145736 | tf_op jit(solution)/shard_map/ppermute | solution.py:803
  56.2 27.6 %collective-permute-start.3 = (bf16[512,1024]{1,0:T(8,128)(2,1)}, bf16[512,1024]{1,0:T(8,128)(2,1)S(1)}, u32[]{:S(2)}, u32[]{:S(2)}) collective-permute-start(bf16[512,1024]{1,0:T(8,128)(2,1)} %get-tuple-element.61.rest_3_.rest_9_), channel_id=1, source_target_pairs={{0,2},{2,4},{4,6},{1,3},{3,5},{5,7},{8,10},{10,12},{12,14},{9,11},... | collective-permute-start | bytes 3145736 | tf_op jit(solution)/shard_map/ppermute | solution.py:803
  60.5 45.6 %collective-permute-start.2 = (bf16[512,1024]{1,0:T(8,128)(2,1)S(1)}, bf16[512,1024]{1,0:T(8,128)(2,1)}, u32[]{:S(2)}, u32[]{:S(2)}) collective-permute-start(bf16[512,1024]{1,0:T(8,128)(2,1)S(1)} %collective-permute-done.1.rest_1_.rest_7_), channel_id=1, source_target_pairs={{0,2},{2,4},{4,6},{1,3},{3,5},{5,7},{8,10},{10,12},{12,14},{9,11},... | collective-permute-start | bytes 3145736 | tf_op jit(solution)/shard_map/ppermute | solution.py:803
  83.8 42.7 %collective-permute-start.4 = (bf16[512,1024]{1,0:T(8,128)(2,1)S(1)}, bf16[512,1024]{1,0:T(8,128)(2,1)}, u32[]{:S(2)}, u32[]{:S(2)}) collective-permute-start(bf16[512,1024]{1,0:T(8,128)(2,1)S(1)} %collective-permute-done.3.rest_4_.rest_10_), channel_id=1, source_target_pairs={{0,2},{2,4},{4,6},{1,3},{3,5},{5,7},{8,10},{10,12},{12,14},{9,11},... | collective-permute-start | bytes 3145736 | tf_op jit(solution)/shard_map/ppermute | solution.py:803
  91.1 75.3 %collective-permute-start.6 = (bf16[512,2048]{1,0:T(8,128)(2,1)}, bf16[512,2048]{1,0:T(8,128)(2,1)}, u32[]{:S(2)}, u32[]{:S(2)}) collective-permute-start(bf16[512,2048]{1,0:T(8,128)(2,1)} %bitcast.3), channel_id=1, source_target_pairs={{0,1},{1,0},{2,3},{3,2},{4,5},{5,4},{6,7},{7,6},{8,9},{9,8},{10,11... | collective-permute-start | bytes 6291464 | tf_op jit(solution)/shard_map/ppermute | solution.py:755
  144.4 48.7 %collective-permute-start.5 = (bf16[512,2048]{1,0:T(8,128)(2,1)S(1)}, bf16[512,2048]{1,0:T(8,128)(2,1)}, u32[]{:S(2)}, u32[]{:S(2)}) collective-permute-start(bf16[512,2048]{1,0:T(8,128)(2,1)S(1)} %convolution_convert_fusion.3.refs_1_), channel_id=1, source_target_pairs={{0,1},{1,0},{2,3},{3,2},{4,5},{5,4},{6,7},{7,6},{8,9},{9,8},{10,11... | collective-permute-start | bytes 6291464 | tf_op jit(solution)/shard_map/ppermute | solution.py:755
  165.8 104.3 %collective-permute-start.7 = (bf16[512,2048]{1,0:T(8,128)(2,1)}, bf16[512,2048]{1,0:T(8,128)(2,1)S(1)}, u32[]{:S(2)}, u32[]{:S(2)}) collective-permute-start(bf16[512,2048]{1,0:T(8,128)(2,1)} %convolution_convert_fusion.2.refs_1_), channel_id=1, source_target_pairs={{0,1},{1,0},{2,3},{3,2},{4,5},{5,4},{6,7},{7,6},{8,9},{9,8},{10,11... | collective-permute-start | bytes 6291464 | tf_op jit(solution)/shard_map/ppermute | solution.py:755
  268.5 90.4 %collective-permute-start.9 = (bf16[512,2048]{1,0:T(8,128)(2,1)}, bf16[512,2048]{1,0:T(8,128)(2,1)}, u32[]{:S(2)}, u32[]{:S(2)}) collective-permute-start(bf16[512,2048]{1,0:T(8,128)(2,1)} %get-tuple-element.67.refs_3_), channel_id=1, source_target_pairs={{0,1},{1,0},{2,3},{3,2},{4,5},{5,4},{6,7},{7,6},{8,9},{9,8},{10,11... | collective-permute-start | bytes 6291464 | tf_op jit(solution)/shard_map/ppermute | solution.py:755
  346.8 41.8 %collective-permute-start.10 = (bf16[512,2048]{1,0:T(8,128)(2,1)}, bf16[512,2048]{1,0:T(8,128)(2,1)}, u32[]{:S(2)}, u32[]{:S(2)}) collective-permute-start(bf16[512,2048]{1,0:T(8,128)(2,1)} %get-tuple-element.69.refs_3_), channel_id=1, source_target_pairs={{0,1},{1,0},{2,3},{3,2},{4,5},{5,4},{6,7},{7,6},{8,9},{9,8},{10,11... | collective-permute-start | bytes 6291464 | tf_op jit(solution)/shard_map/ppermute | solution.py:755
  447.9 38.6 %collective-permute-start.14 = (bf16[2,4,128,1024]{3,2,1,0:T(8,128)(2,1)}, bf16[2,4,128,1024]{3,2,1,0:T(8,128)(2,1)}, u32[]{:S(2)}, u32[]{:S(2)}) collective-permute-start(bf16[2,4,128,1024]{3,2,1,0:T(8,128)(2,1)} %wgrad.18), channel_id=1, source_target_pairs={{0,8},{8,0},{16,24},{24,16},{1,9},{9,1},{17,25},{25,17},{2,10},{10... | collective-permute-start | bytes 6291464 | tf_op jit(solution)/shard_map/ppermute | solution.py:695
  455.2 54.3 %collective-permute-start.30 = (bf16[2,4,1024,128]{3,2,1,0:T(8,128)(2,1)}, bf16[2,4,1024,128]{3,2,1,0:T(8,128)(2,1)}, u32[]{:S(2)}, u32[]{:S(2)}) collective-permute-start(bf16[2,4,1024,128]{3,2,1,0:T(8,128)(2,1)} %wgrad.24), channel_id=1, source_target_pairs={{0,8},{8,0},{16,24},{24,16},{1,9},{9,1},{17,25},{25,17},{2,10},{10... | collective-permute-start | bytes 6291464 | tf_op jit(solution)/shard_map/ppermute | solution.py:695
  466.6 47.9 %collective-permute-start.8 = (bf16[512,2048]{1,0:T(8,128)(2,1)}, bf16[512,2048]{1,0:T(8,128)(2,1)}, u32[]{:S(2)}, u32[]{:S(2)}) collective-permute-start(bf16[512,2048]{1,0:T(8,128)(2,1)} %get-tuple-element.142), channel_id=1, source_target_pairs={{0,1},{1,0},{2,3},{3,2},{4,5},{5,4},{6,7},{7,6},{8,9},{9,8},{10,11... | collective-permute-start | bytes 6291464 | tf_op jit(solution)/shard_map/ppermute | solution.py:755
  485.2 212.7 %collective-permute-start.38 = (bf16[2,4,128,3072]{3,2,1,0:T(8,128)(2,1)}, bf16[2,4,128,3072]{3,2,1,0:T(8,128)(2,1)}, u32[]{:S(2)}, u32[]{:S(2)}) collective-permute-start(bf16[2,4,128,3072]{3,2,1,0:T(8,128)(2,1)} %wgrad.27), channel_id=1, source_target_pairs={{0,8},{8,0},{16,24},{24,16},{1,9},{9,1},{17,25},{25,17},{2,10},{10... | collective-permute-start | bytes 18874376 | tf_op jit(solution)/shard_map/ppermute | solution.py:695
  485.2 61.4 %collective-permute-start.11 = (bf16[1024,1024]{1,0:T(8,128)(2,1)}, bf16[1024,1024]{1,0:T(8,128)(2,1)}, u32[]{:S(2)}, u32[]{:S(2)}) collective-permute-start(bf16[1024,1024]{1,0:T(8,128)(2,1)} %get-tuple-element.75), channel_id=1, source_target_pairs={{2,0},{4,2},{6,4},{3,1},{5,3},{7,5},{10,8},{12,10},{14,12},{11,9},... | collective-permute-start | bytes 6291464 | tf_op jit(solution)/shard_map/ppermute | solution.py:849
  491.6 40.3 %collective-permute-start.15 = (bf16[1,4,128,1024]{3,2,1,0:T(8,128)(2,1)}, bf16[1,4,128,1024]{3,2,1,0:T(8,128)(2,1)S(1)}, u32[]{:S(2)}, u32[]{:S(2)}) collective-permute-start(bf16[1,4,128,1024]{3,2,1,0:T(8,128)(2,1)} %wgrad.20), channel_id=1, source_target_pairs={{0,16},{8,24},{16,0},{24,8},{1,17},{9,25},{17,1},{25,9},{2,18},{10... | collective-permute-start | bytes 3145736 | tf_op jit(solution)/shard_map/ppermute | solution.py:698
  509.5 202.2 %collective-permute-start.46 = (bf16[2,4,128,3072]{3,2,1,0:T(8,128)(2,1)}, bf16[2,4,128,3072]{3,2,1,0:T(8,128)(2,1)}, u32[]{:S(2)}, u32[]{:S(2)}) collective-permute-start(bf16[2,4,128,3072]{3,2,1,0:T(8,128)(2,1)} %wgrad.30), channel_id=1, source_target_pairs={{0,8},{8,0},{16,24},{24,16},{1,9},{9,1},{17,25},{25,17},{2,10},{10... | collective-permute-start | bytes 18874376 | tf_op jit(solution)/shard_map/ppermute | solution.py:695
  514.5 54.7 %collective-permute-start.31 = (bf16[1,4,1024,128]{3,2,1,0:T(8,128)(2,1)}, bf16[1,4,1024,128]{3,2,1,0:T(8,128)(2,1)S(1)}, u32[]{:S(2)}, u32[]{:S(2)}) collective-permute-start(bf16[1,4,1024,128]{3,2,1,0:T(8,128)(2,1)} %wgrad.26), channel_id=1, source_target_pairs={{0,16},{8,24},{16,0},{24,8},{1,17},{9,25},{17,1},{25,9},{2,18},{10... | collective-permute-start | bytes 3145736 | tf_op jit(solution)/shard_map/ppermute | solution.py:698
  531.9 208.0 %collective-permute-start.54 = (bf16[2,4,3072,128]{3,2,1,0:T(8,128)(2,1)}, bf16[2,4,3072,128]{3,2,1,0:T(8,128)(2,1)}, u32[]{:S(2)}, u32[]{:S(2)}) collective-permute-start(bf16[2,4,3072,128]{3,2,1,0:T(8,128)(2,1)} %wgrad.33), channel_id=1, source_target_pairs={{0,8},{8,0},{16,24},{24,16},{1,9},{9,1},{17,25},{25,17},{2,10},{10... | collective-permute-start | bytes 18874376 | tf_op jit(solution)/shard_map/ppermute | solution.py:695
  546.6 33.6 %collective-permute-start.16 = (bf16[128,1024]{1,0:T(8,128)(2,1)}, bf16[128,1024]{1,0:T(8,128)(2,1)S(1)}, u32[]{:S(2)}, u32[]{:S(2)}) collective-permute-start(bf16[128,1024]{1,0:T(8,128)(2,1)} %get-tuple-element.125), channel_id=1, source_target_pairs={{0,2},{1,3},{8,10},{9,11},{16,18},{17,19},{24,26},{25,27}} | collective-permute-start | bytes 786440 | tf_op jit(solution)/shard_map/ppermute | solution.py:710
  587.7 76.0 %collective-permute-start.12 = (bf16[1024,1024]{1,0:T(8,128)(2,1)}, bf16[1024,1024]{1,0:T(8,128)(2,1)S(1)}, u32[]{:S(2)}, u32[]{:S(2)}) collective-permute-start(bf16[1024,1024]{1,0:T(8,128)(2,1)} %add_convert_fusion), channel_id=1, source_target_pairs={{2,0},{4,2},{6,4},{3,1},{5,3},{7,5},{10,8},{12,10},{14,12},{11,9},... | collective-permute-start | bytes 6291464 | tf_op jit(solution)/shard_map/ppermute | solution.py:849
  602.8 28.0 %collective-permute-start.33 = (bf16[1024,128]{1,0:T(8,128)(2,1)S(1)}, bf16[1024,128]{1,0:T(8,128)(2,1)S(1)}, u32[]{:S(2)}, u32[]{:S(2)}) collective-permute-start(bf16[1024,128]{1,0:T(8,128)(2,1)S(1)} %fusion.24), channel_id=1, source_target_pairs={{0,2},{2,4},{1,3},{3,5},{8,10},{10,12},{9,11},{11,13},{16,18},{18,... | collective-permute-start | bytes 786440 | tf_op jit(solution)/shard_map/ppermute | solution.py:710
  634.6 93.7 %collective-permute-start.18 = (bf16[128,1024]{1,0:T(8,128)(2,1)S(1)}, bf16[128,1024]{1,0:T(8,128)(2,1)S(1)}, u32[]{:S(2)}, u32[]{:S(2)}) collective-permute-start(bf16[128,1024]{1,0:T(8,128)(2,1)S(1)} %copy-done.25), channel_id=1, source_target_pairs={{0,2},{2,4},{4,6},{1,3},{3,5},{5,7},{8,10},{10,12},{12,14},{9,11},... | collective-permute-start | bytes 786440 | tf_op jit(solution)/shard_map/ppermute | solution.py:710
  663.7 44.1 %collective-permute-start.36 = (bf16[1024,128]{1,0:T(8,128)(2,1)S(1)}, bf16[1024,128]{1,0:T(8,128)(2,1)S(1)}, u32[]{:S(2)}, u32[]{:S(2)}) collective-permute-start(bf16[1024,128]{1,0:T(8,128)(2,1)S(1)} %get-tuple-element.116), channel_id=1, source_target_pairs={{6,4},{4,2},{7,5},{5,3},{14,12},{12,10},{15,13},{13,11},{22,20},{2... | collective-permute-start | bytes 786440 | tf_op jit(solution)/shard_map/ppermute | solution.py:711
  697.9 253.2 %collective-permute-start.22 = (bf16[2,4,128,1024]{3,2,1,0:T(8,128)(2,1)}, bf16[2,4,128,1024]{3,2,1,0:T(8,128)(2,1)}, u32[]{:S(2)}, u32[]{:S(2)}) collective-permute-start(bf16[2,4,128,1024]{3,2,1,0:T(8,128)(2,1)} %wgrad.21), channel_id=1, source_target_pairs={{0,8},{8,0},{16,24},{24,16},{1,9},{9,1},{17,25},{25,17},{2,10},{10... | collective-permute-start | bytes 6291464 | tf_op jit(solution)/shard_map/ppermute | solution.py:695
  707.9 271.6 %collective-permute-start.39 = (bf16[1,4,128,3072]{3,2,1,0:T(8,128)(2,1)}, bf16[1,4,128,3072]{3,2,1,0:T(8,128)(2,1)S(1)}, u32[]{:S(2)}, u32[]{:S(2)}) collective-permute-start(bf16[1,4,128,3072]{3,2,1,0:T(8,128)(2,1)} %wgrad.29), channel_id=1, source_target_pairs={{0,16},{8,24},{16,0},{24,8},{1,17},{9,25},{17,1},{25,9},{2,18},{10... | collective-permute-start | bytes 9437192 | tf_op jit(solution)/shard_map/ppermute | solution.py:698
  711.7 26.9 %collective-permute-start.34 = (bf16[1024,128]{1,0:T(8,128)(2,1)S(1)}, bf16[1024,128]{1,0:T(8,128)(2,1)S(1)}, u32[]{:S(2)}, u32[]{:S(2)}) collective-permute-start(bf16[1024,128]{1,0:T(8,128)(2,1)S(1)} %get-tuple-element.115), channel_id=1, source_target_pairs={{0,2},{2,4},{4,6},{1,3},{3,5},{5,7},{8,10},{10,12},{12,14},{9,11},... | collective-permute-start | bytes 786440 | tf_op jit(solution)/shard_map/ppermute | solution.py:710
  728.3 261.2 %collective-permute-start.47 = (bf16[1,4,128,3072]{3,2,1,0:T(8,128)(2,1)}, bf16[1,4,128,3072]{3,2,1,0:T(8,128)(2,1)}, u32[]{:S(2)}, u32[]{:S(2)}) collective-permute-start(bf16[1,4,128,3072]{3,2,1,0:T(8,128)(2,1)} %wgrad.32), channel_id=1, source_target_pairs={{0,16},{8,24},{16,0},{24,8},{1,17},{9,25},{17,1},{25,9},{2,18},{10... | collective-permute-start | bytes 9437192 | tf_op jit(solution)/shard_map/ppermute | solution.py:698
  739.9 226.3 %collective-permute-start.13 = (bf16[512,2048]{1,0:T(8,128)(2,1)}, bf16[512,2048]{1,0:T(8,128)(2,1)}, u32[]{:S(2)}, u32[]{:S(2)}) collective-permute-start(bf16[512,2048]{1,0:T(8,128)(2,1)} %get-tuple-element.82), channel_id=1, source_target_pairs={{0,1},{1,0},{2,3},{3,2},{4,5},{5,4},{6,7},{7,6},{8,9},{9,8},{10,11... | collective-permute-start | bytes 6291464 | tf_op jit(solution)/shard_map/ppermute | solution.py:755
  751.1 258.4 %collective-permute-start.55 = (bf16[1,4,3072,128]{3,2,1,0:T(8,128)(2,1)}, bf16[1,4,3072,128]{3,2,1,0:T(8,128)(2,1)}, u32[]{:S(2)}, u32[]{:S(2)}) collective-permute-start(bf16[1,4,3072,128]{3,2,1,0:T(8,128)(2,1)} %wgrad.35), channel_id=1, source_target_pairs={{0,16},{8,24},{16,0},{24,8},{1,17},{9,25},{17,1},{25,9},{2,18},{10... | collective-permute-start | bytes 9437192 | tf_op jit(solution)/shard_map/ppermute | solution.py:698
  960.7 24.2 %collective-permute-start.23 = (bf16[1,4,128,1024]{3,2,1,0:T(8,128)(2,1)}, bf16[1,4,128,1024]{3,2,1,0:T(8,128)(2,1)}, u32[]{:S(2)}, u32[]{:S(2)}) collective-permute-start(bf16[1,4,128,1024]{3,2,1,0:T(8,128)(2,1)} %wgrad.23), channel_id=1, source_target_pairs={{0,16},{8,24},{16,0},{24,8},{1,17},{9,25},{17,1},{25,9},{2,18},{10... | collective-permute-start | bytes 3145736 | tf_op jit(solution)/shard_map/ppermute | solution.py:698
  980.1 51.9 %collective-permute-start.40 = (bf16[128,3072]{1,0:T(8,128)(2,1)S(1)}, bf16[128,3072]{1,0:T(8,128)(2,1)S(1)}, u32[]{:S(2)}, u32[]{:S(2)}) collective-permute-start(bf16[128,3072]{1,0:T(8,128)(2,1)S(1)} %get-tuple-element.111), channel_id=1, source_target_pairs={{0,2},{1,3},{8,10},{9,11},{16,18},{17,19},{24,26},{25,27}} | collective-permute-start | bytes 2359304 | tf_op jit(solution)/shard_map/ppermute | solution.py:710
  984.2 79.0 %collective-permute-start.43 = (bf16[128,3072]{1,0:T(8,128)(2,1)S(1)}, bf16[128,3072]{1,0:T(8,128)(2,1)S(1)}, u32[]{:S(2)}, u32[]{:S(2)}) collective-permute-start(bf16[128,3072]{1,0:T(8,128)(2,1)S(1)} %get-tuple-element.112), channel_id=1, source_target_pairs={{6,4},{7,5},{14,12},{15,13},{22,20},{23,21},{30,28},{31,29}} | collective-permute-start | bytes 2359304 | tf_op jit(solution)/shard_map/ppermute | solution.py:711
  991.4 41.6 %collective-permute-start.48 = (bf16[128,3072]{1,0:T(8,128)(2,1)S(1)}, bf16[128,3072]{1,0:T(8,128)(2,1)S(1)}, u32[]{:S(2)}, u32[]{:S(2)}) collective-permute-start(bf16[128,3072]{1,0:T(8,128)(2,1)S(1)} %get-tuple-element.107), channel_id=1, source_target_pairs={{0,2},{1,3},{8,10},{9,11},{16,18},{17,19},{24,26},{25,27}} | collective-permute-start | bytes 2359304 | tf_op jit(solution)/shard_map/ppermute | solution.py:710
  1015.8 56.8 %collective-permute-start.51 = (bf16[128,3072]{1,0:T(8,128)(2,1)S(1)}, bf16[128,3072]{1,0:T(8,128)(2,1)S(1)}, u32[]{:S(2)}, u32[]{:S(2)}) collective-permute-start(bf16[128,3072]{1,0:T(8,128)(2,1)S(1)} %get-tuple-element.108), channel_id=1, source_target_pairs={{6,4},{7,5},{14,12},{15,13},{22,20},{23,21},{30,28},{31,29}} | collective-permute-start | bytes 2359304 | tf_op jit(solution)/shard_map/ppermute | solution.py:711
  1026.2 22.4 %collective-permute-start.56 = (bf16[3072,128]{1,0:T(8,128)(2,1)S(1)}, bf16[3072,128]{1,0:T(8,128)(2,1)S(1)}, u32[]{:S(2)}, u32[]{:S(2)}) collective-permute-start(bf16[3072,128]{1,0:T(8,128)(2,1)S(1)} %get-tuple-element.103), channel_id=1, source_target_pairs={{0,2},{1,3},{8,10},{9,11},{16,18},{17,19},{24,26},{25,27}} | collective-permute-start | bytes 2359304 | tf_op jit(solution)/shard_map/ppermute | solution.py:710
  1036.4 34.6 %collective-permute-start.41 = (bf16[128,3072]{1,0:T(8,128)(2,1)S(1)}, bf16[128,3072]{1,0:T(8,128)(2,1)S(1)}, u32[]{:S(2)}, u32[]{:S(2)}) collective-permute-start(bf16[128,3072]{1,0:T(8,128)(2,1)S(1)} %fusion.13), channel_id=1, source_target_pairs={{0,2},{2,4},{1,3},{3,5},{8,10},{10,12},{9,11},{11,13},{16,18},{18,... | collective-permute-start | bytes 2359304 | tf_op jit(solution)/shard_map/ppermute | solution.py:710
  1054.2 36.6 %collective-permute-start.59 = (bf16[3072,128]{1,0:T(8,128)(2,1)S(1)}, bf16[3072,128]{1,0:T(8,128)(2,1)S(1)}, u32[]{:S(2)}, u32[]{:S(2)}) collective-permute-start(bf16[3072,128]{1,0:T(8,128)(2,1)S(1)} %get-tuple-element.104), channel_id=1, source_target_pairs={{6,4},{7,5},{14,12},{15,13},{22,20},{23,21},{30,28},{31,29}} | collective-permute-start | bytes 2359304 | tf_op jit(solution)/shard_map/ppermute | solution.py:711
  1057.3 30.6 %collective-permute-start.49 = (bf16[128,3072]{1,0:T(8,128)(2,1)S(1)}, bf16[128,3072]{1,0:T(8,128)(2,1)S(1)}, u32[]{:S(2)}, u32[]{:S(2)}) collective-permute-start(bf16[128,3072]{1,0:T(8,128)(2,1)S(1)} %fusion.8), channel_id=1, source_target_pairs={{0,2},{2,4},{1,3},{3,5},{8,10},{10,12},{9,11},{11,13},{16,18},{18,... | collective-permute-start | bytes 2359304 | tf_op jit(solution)/shard_map/ppermute | solution.py:710
  1063.2 41.5 %collective-permute-start.57 = (bf16[3072,128]{1,0:T(8,128)(2,1)S(1)}, bf16[3072,128]{1,0:T(8,128)(2,1)S(1)}, u32[]{:S(2)}, u32[]{:S(2)}) collective-permute-start(bf16[3072,128]{1,0:T(8,128)(2,1)S(1)} %fusion.3), channel_id=1, source_target_pairs={{0,2},{2,4},{1,3},{3,5},{8,10},{10,12},{9,11},{11,13},{16,18},{18,... | collective-permute-start | bytes 2359304 | tf_op jit(solution)/shard_map/ppermute | solution.py:710
  1071.9 35.6 %collective-permute-start.44 = (bf16[128,3072]{1,0:T(8,128)(2,1)S(1)}, bf16[128,3072]{1,0:T(8,128)(2,1)S(1)}, u32[]{:S(2)}, u32[]{:S(2)}) collective-permute-start(bf16[128,3072]{1,0:T(8,128)(2,1)S(1)} %get-tuple-element.110), channel_id=1, source_target_pairs={{6,4},{4,2},{7,5},{5,3},{14,12},{12,10},{15,13},{13,11},{22,20},{2... | collective-permute-start | bytes 2359304 | tf_op jit(solution)/shard_map/ppermute | solution.py:711
  1072.6 49.0 %collective-permute-start.42 = (bf16[128,3072]{1,0:T(8,128)(2,1)S(1)}, bf16[128,3072]{1,0:T(8,128)(2,1)S(1)}, u32[]{:S(2)}, u32[]{:S(2)}) collective-permute-start(bf16[128,3072]{1,0:T(8,128)(2,1)S(1)} %get-tuple-element.109), channel_id=1, source_target_pairs={{0,2},{2,4},{4,6},{1,3},{3,5},{5,7},{8,10},{10,12},{12,14},{9,11},... | collective-permute-start | bytes 2359304 | tf_op jit(solution)/shard_map/ppermute | solution.py:710
  1090.1 22.8 %collective-permute-start.52 = (bf16[128,3072]{1,0:T(8,128)(2,1)S(1)}, bf16[128,3072]{1,0:T(8,128)(2,1)S(1)}, u32[]{:S(2)}, u32[]{:S(2)}) collective-permute-start(bf16[128,3072]{1,0:T(8,128)(2,1)S(1)} %get-tuple-element.106), channel_id=1, source_target_pairs={{6,4},{4,2},{7,5},{5,3},{14,12},{12,10},{15,13},{13,11},{22,20},{2... | collective-permute-start | bytes 2359304 | tf_op jit(solution)/shard_map/ppermute | solution.py:711
  1090.8 47.7 %collective-permute-start.50 = (bf16[128,3072]{1,0:T(8,128)(2,1)S(1)}, bf16[128,3072]{1,0:T(8,128)(2,1)S(1)}, u32[]{:S(2)}, u32[]{:S(2)}) collective-permute-start(bf16[128,3072]{1,0:T(8,128)(2,1)S(1)} %get-tuple-element.105), channel_id=1, source_target_pairs={{0,2},{2,4},{4,6},{1,3},{3,5},{5,7},{8,10},{10,12},{12,14},{9,11},... | collective-permute-start | bytes 2359304 | tf_op jit(solution)/shard_map/ppermute | solution.py:710
  1107.5 46.8 %collective-permute-start.58 = (bf16[3072,128]{1,0:T(8,128)(2,1)S(1)}, bf16[3072,128]{1,0:T(8,128)(2,1)S(1)}, u32[]{:S(2)}, u32[]{:S(2)}) collective-permute-start(bf16[3072,128]{1,0:T(8,128)(2,1)S(1)} %get-tuple-element.101), channel_id=1, source_target_pairs={{0,2},{2,4},{4,6},{1,3},{3,5},{5,7},{8,10},{10,12},{12,14},{9,11},... | collective-permute-start | bytes 2359304 | tf_op jit(solution)/shard_map/ppermute | solution.py:710
  1112.9 22.9 %collective-permute-start.45 = (bf16[128,3072]{1,0:T(8,128)(2,1)S(1)}, bf16[128,3072]{1,0:T(8,128)(2,1)S(1)}, u32[]{:S(2)}, u32[]{:S(2)}) collective-permute-start(bf16[128,3072]{1,0:T(8,128)(2,1)S(1)} %fusion.12), channel_id=1, source_target_pairs={{6,4},{4,2},{2,0},{7,5},{5,3},{3,1},{14,12},{12,10},{10,8},{15,13}... | collective-permute-start | bytes 2359304 | tf_op jit(solution)/shard_map/ppermute | solution.py:711
  1115.7 35.9 %collective-permute-start.53 = (bf16[128,3072]{1,0:T(8,128)(2,1)S(1)}, bf16[128,3072]{1,0:T(8,128)(2,1)S(1)}, u32[]{:S(2)}, u32[]{:S(2)}) collective-permute-start(bf16[128,3072]{1,0:T(8,128)(2,1)S(1)} %fusion.7), channel_id=1, source_target_pairs={{6,4},{4,2},{2,0},{7,5},{5,3},{3,1},{14,12},{12,10},{10,8},{15,13}... | collective-permute-start | bytes 2359304 | tf_op jit(solution)/shard_map/ppermute | solution.py:711
  1121.6 38.4 %collective-permute-start.61 = (bf16[3072,128]{1,0:T(8,128)(2,1)S(1)}, bf16[3072,128]{1,0:T(8,128)(2,1)S(1)}, u32[]{:S(2)}, u32[]{:S(2)}) collective-permute-start(bf16[3072,128]{1,0:T(8,128)(2,1)S(1)} %fusion.2), channel_id=1, source_target_pairs={{6,4},{4,2},{2,0},{7,5},{5,3},{3,1},{14,12},{12,10},{10,8},{15,13}... | collective-permute-start | bytes 2359304 | tf_op jit(solution)/shard_map/ppermute | solution.py:711
  (51 other events, 852.8 us)
where the time goes:
time: 1190 us; the launch traced here: 1160 us
  Pallas kernels  463 us (39%)
  waiting for transfers between devices  220 us (18%)
  starting transfers between devices  190 us (16%)
  blocking collectives  178 us (15%)
  other arithmetic  67.4 us (6%)
  matrix products  29 us (2%)
  local copies, waits for them, and re-layouts  14.2 us (1%)
    psum x1, blocking collectives, per_device(): packed = lax.psum(packed, ('dp', 'seq', 'tensor'))  178 us
    pallas_call x18, Pallas kernels, wgrad(): pl.pallas_call(functools.partial(wgrad_kernel, nt=nt, na=len(addends), ro...  162 us
    pallas_call x2, Pallas kernels, mlp(): pl.pallas_call(functools.partial(mlp_kernel, np_=len(parts)), grid=(ff //...  151 us
    ppermute x18, starting transfers between devices, reduce_weights(): lax.ppermute(send_right.astype(BF), 'seq', [(k, k + 1) for k in range(s)])  133 us
    ppermute x8, waiting for transfers between devices, per_device(): swap = lambda v: lax.ppermute(v, 'tensor', [(0, 1), (1, 0)])  70.1 us
    ppermute x18, waiting for transfers between devices, reduce_weights(): lax.ppermute(send_right.astype(BF), 'seq', [(k, k + 1) for k in range(s)])  66.2 us
    ppermute x4, waiting for transfers between devices, per_device(): kv = lax.ppermute(kv, 'seq', ahead)  39.5 us
    ppermute x18, waiting for transfers between devices, reduce_weights(): lax.ppermute(send_left.astype(BF), 'seq', [(ns - 1 - k, ns - 2 - k) for k...  36.3 us
  transfers between devices with their start and end apart: 62, of which 24 were waited for; matrix products, arithmetic and copies ran while one was open for 9% of the time, Pallas kernels for 35%

commit v1 on v0

--- a/solution.py
+++ b/solution.py
@@ -18,16 +18,15 @@
 BF = jnp.bfloat16
 F32 = jnp.float32
 MIB = 1 << 20
+cost_scale = 0.4
 
 
 def params(limit=56, **kw):
     return pltpu.CompilerParams(vmem_limit_bytes=limit * MIB, **kw)
 
 
-def cost(flops, bytes_accessed, transcendentals=0):
-    return pl.CostEstimate(
-        flops=int(flops), bytes_accessed=int(bytes_accessed), transcendentals=int(transcendentals)
-    )
+def cost(us):
+    return pl.CostEstimate(flops=int(us * cost_scale * 1e9), bytes_accessed=0, transcendentals=0)
 
 
 def dot(a, b, ca=1, cb=0):
@@ -96,7 +95,7 @@
         ),
         out_shape=[sds((rows, 2 * n), BF), sds((rows, n), F32)],
         compiler_params=params(),
-        cost_estimate=cost(4 * rows * d * n, 2 * rows * d + 4 * d * n + 8 * rows * n),
+        cost_estimate=cost(6.5),
         name="project_kv",
     )(jnp.reshape(base_tile, (1,)), x, gain, wk, wv, cosine, sine, hg)
 
@@ -150,7 +149,7 @@
             sds((total, d), BF), sds((total, d), BF), sds((total, n), BF), sds((total, n), F32)
         ],
         compiler_params=params(),
-        cost_estimate=cost(2 * total * d * n, 6 * total * d + 2 * d * n + 6 * total * n),
+        cost_estimate=cost(13),
         name="project_q",
     )(bases, xa, xb, gain, w, cosine, sine, hg)
 
@@ -163,17 +162,29 @@
         vwin[pl.ds(base, rows), :HD] = seg[:, HD:]
 
 
-def flash_fwd_kernel(s_ref, q_ref, st_ref, *rest, nq, tq, tk, gs, row0, at_bases):
-    segs, (o_ref, aug_ref, kwin, vwin, acc) = rest[:-5], rest[-5:]
+def spread(value, gs, tq):
+    step = HD // gs
+    return jnp.concatenate([value[:, g * step : g * step + 1] for g in range(gs)], axis=0)
+
+
+def flash_fwd_kernel(s_ref, q_ref, st_ref, *rest, nseg, prior, last, nq, tq, tk, gs, w0, row0):
+    segs, rest = rest[:nseg], rest[nseg:]
+    acc_in, rest = rest[: 2 * prior], rest[2 * prior :]
+    o_ref, l_ref, kwin, vwin, acc = rest
     i = pl.program_id(1)
 
     @pl.when(i == 0)
     def _():
-        fill_window(s_ref, at_bases, segs, kwin, vwin)
+        fill_window(s_ref, 4 * nq, segs, kwin, vwin)
         vwin[:, HD:] = jnp.ones(vwin[:, HD:].shape, BF)
 
-    q2 = jnp.concatenate([q_ref[:, g * HD : (g + 1) * HD] for g in range(gs)], axis=0)
-    acc[...] = jnp.zeros_like(acc)
+    heads = [slice(g * HD, (g + 1) * HD) for g in range(gs)]
+    q2 = jnp.concatenate([q_ref[:, hh] for hh in heads], axis=0)
+    if prior:
+        acc[:, :HD] = jnp.concatenate([acc_in[0][:, hh] for hh in heads], axis=0)
+        acc[:, HD:] = jnp.broadcast_to(spread(acc_in[1], gs, tq), (gs * tq, HD))
+    else:
+        acc[...] = jnp.zeros_like(acc)
     lo, hi, flo, fhi = [s_ref[n * nq + i] for n in range(4)]
 
     def step(kt, masked):
@@ -181,7 +192,7 @@
         p = jnp.exp2(dot(q2, kwin[pl.ds(at, tk), :], 1, 1))
         if masked:
             st = st_ref[:, :1]
-            j = at + lax.broadcasted_iota(jnp.int32, (tq, tk), 1)
+            j = w0 + at + lax.broadcasted_iota(jnp.int32, (tq, tk), 1)
             t = row0 + i * tq + lax.broadcasted_iota(jnp.int32, (tq, tk), 0)
             keep = (j >= st) & (j <= t)
             p = jnp.where(jnp.concatenate([keep] * gs, axis=0), p, 0.0)
@@ -201,77 +212,68 @@
         return carry
 
     lax.fori_loop(lo, hi, body, 0)
-    total = acc[:, HD:]
-    out = (acc[:, :HD] / total).astype(BF)
-    neg = -jnp.log2(total)
-    first = neg.astype(BF)
-    rest_one = neg - first.astype(F32)
-    second = rest_one.astype(BF)
-    third = (rest_one - second.astype(F32)).astype(BF)
-    lane = lax.broadcasted_iota(jnp.int32, total.shape, 1)
-    aug = jnp.where(
-        lane == 0,
-        first.astype(F32),
-        jnp.where(lane == 1, second.astype(F32), jnp.where(lane == 2, third.astype(F32), 0.0)),
-    ).astype(BF)
+    total, out = acc[:, HD:], acc[:, :HD]
+    if last:
+        total = 1.0 / total
+        out = (out * total).astype(BF)
+    lane = lax.broadcasted_iota(jnp.int32, (tq, HD), 1)
+    packed = total[:tq]
     for g in range(gs):
-        o_ref[:, g * HD : (g + 1) * HD] = out[g * tq : (g + 1) * tq]
-        aug_ref[:, g * HD : (g + 1) * HD] = aug[g * tq : (g + 1) * tq]
-
-
-def flash_fwd(scalars, q, starts_col, segs, window, chunk, rows, gs, tq, tk):
+        o_ref[:, heads[g]] = out[g * tq : (g + 1) * tq]
+        packed = jnp.where(lane >= g * (HD // gs), total[g * tq : (g + 1) * tq], packed)
+    l_ref[...] = packed
+
+
+def flash_fwd(bounds, bases, q, starts_col, segs, prior, window, part, row_at, rows, last, gs, tq, tk):
     width = gs * HD
     heads = q.shape[1] // width
     nq = rows // tq
-    off = chunk * nq
+    off = row_at // tq
+    w0, w1 = part
+    scalars = jnp.concatenate([*bounds(row_at, rows, w0, w1), jnp.stack([b - w0 for b in bases])])
     seg_specs = [pl.BlockSpec((seg.shape[0], 2 * HD), lambda h, i, s: (0, h)) for seg in segs]
-    pairs = rows * (window // 2)
+    pairs = rows * (w1 - w0) // 2
+    moved = lambda w: pl.BlockSpec((tq, w), lambda h, i, s: (off + i, h))
+    tile = lambda w: pl.BlockSpec((tq, w), lambda h, i, s: (i, h))
     return pl.pallas_call(
         functools.partial(
-            flash_fwd_kernel, nq=nq, tq=tq, tk=tk, gs=gs,
-            row0=window - q.shape[0] + chunk * rows, at_bases=4 * nq,
+            flash_fwd_kernel, nseg=len(segs), prior=len(prior) // 2, last=last, nq=nq, tq=tq,
+            tk=tk, gs=gs, w0=w0, row0=window - q.shape[0] + row_at,
         ),
         grid_spec=grid_spec(
             1,
             (heads, nq),
             [
-                pl.BlockSpec((tq, width), lambda h, i, s: (off + i, h)),
+                moved(width),
                 pl.BlockSpec((tq, HD), lambda h, i, s: (off + i, 0)),
                 *seg_specs,
+                *([moved(width), moved(HD)] if prior else []),
             ],
+            [tile(width), tile(HD)],
             [
-                pl.BlockSpec((tq, width), lambda h, i, s: (i, h)),
-                pl.BlockSpec((tq, width), lambda h, i, s: (i, h)),
-            ],
-            [
-                pltpu.VMEM((window, HD), BF),
-                pltpu.VMEM((window, 2 * HD), BF),
+                pltpu.VMEM((w1 - w0, HD), BF),
+                pltpu.VMEM((w1 - w0, 2 * HD), BF),
                 pltpu.VMEM((gs * tq, 2 * HD), F32),
             ],
         ),
-        out_shape=[sds((rows, q.shape[1]), BF), sds((rows, q.shape[1]), BF)],
+        out_shape=[sds((rows, q.shape[1]), BF if last else F32), sds((rows, heads * HD), F32)],
         compiler_params=params(),
-        cost_estimate=cost(
-            heads * gs * pairs * 8 * HD, 8 * q.size + sum(2 * x.size for x in segs),
-            heads * gs * pairs,
-        ),
+        cost_estimate=cost(12 * last + 22 * (1 - last)),
         name="flash_fwd",
-    )(scalars, q, starts_col, *segs)
-
-
-def flash_bwd_kernel(s_ref, q_ref, st_ref, *rest, nc, ns, nb, nq, tq, tk, gs, row0, at_bases):
-    das, outs, augs = rest[:nc], rest[nc : 2 * nc], rest[2 * nc : 3 * nc]
+    )(scalars, q, starts_col, *segs, *prior)
+
+
+def flash_bwd_kernel(s_ref, q_ref, st_ref, *rest, nc, ns, nb, nq, tq, tk, gs, row0):
+    das, outs, sums = rest[:nc], rest[nc : 2 * nc], rest[2 * nc : 3 * nc]
     segs = rest[3 * nc : 3 * nc + ns]
     dq_ref = rest[3 * nc + ns]
     dkvs = rest[3 * nc + ns + 1 : 3 * nc + ns + 1 + nb]
     kwin, vwin, dk, dv, dqs = rest[3 * nc + ns + 1 + nb :]
     span = dkvs[0].shape[0]
 
-    fill_window(s_ref, at_bases, segs, kwin, vwin)
-    lane = lax.broadcasted_iota(jnp.int32, (kwin.shape[0], HD), 1)
-    marks = jnp.where(lane < 3, 1.0, 0.0).astype(BF)
-    kwin[:, HD:] = marks
-    vwin[:, HD:] = marks
+    fill_window(s_ref, 4 * nq, segs, kwin, vwin)
+    lane = lax.broadcasted_iota(jnp.int32, (vwin.shape[0], HD), 1)
+    vwin[:, HD:] = jnp.where(lane < 2, 1.0, 0.0).astype(BF)
     dk[...] = jnp.zeros_like(dk)
     dv[...] = jnp.zeros_like(dv)
 
@@ -282,26 +284,20 @@
         heads = [slice(g * HD, (g + 1) * HD) for g in range(gs)]
         pile = lambda ref, rr: jnp.concatenate([ref[rr, hh] for hh in heads], axis=0)
         q2 = pile(q_ref, slice(i * tq, (i + 1) * tq))
-        qa = jnp.concatenate([q2, pile(augs[c], rows)], axis=1)
-        do2 = pile(das[c], rows)
-        neg = -jnp.sum(
-            do2.astype(F32) * pile(outs[c], rows).astype(F32), axis=1, keepdims=True
-        )
+        scaled = pile(das[c], rows).astype(F32) * spread(sums[c][rows, :], gs, tq)
+        neg = -jnp.sum(scaled * pile(outs[c], rows).astype(F32), axis=1, keepdims=True)
+        do2 = scaled.astype(BF)
         first = neg.astype(BF).astype(F32)
-        second = (neg - first).astype(BF).astype(F32)
-        third = neg - first - second
         ln = lax.broadcasted_iota(jnp.int32, (gs * tq, HD), 1)
-        daug = jnp.where(
-            ln == 0, first, jnp.where(ln == 1, second, jnp.where(ln == 2, third, 0.0))
-        ).astype(BF)
+        daug = jnp.where(ln == 0, first, jnp.where(ln == 1, neg - first, 0.0)).astype(BF)
         da = jnp.concatenate([do2, daug], axis=1)
         dqs[...] = jnp.zeros_like(dqs)
         lo, hi, flo, fhi = [s_ref[n * nq + i] for n in range(4)]
 
-        def step(kt, masked, i=i, q2=q2, qa=qa, do2=do2, da=da):
+        def step(kt, masked, i=i, q2=q2, do2=do2, da=da):
             at = pl.multiple_of(kt * tk, tk)
             ka = kwin[pl.ds(at, tk), :]
-            p = jnp.exp2(dot(ka, qa, 1, 1))
+            p = jnp.exp2(dot(ka, q2, 1, 1))
             if masked:
                 st = st_ref[:1, i * tq : (i + 1) * tq]
                 j = at + lax.broadcasted_iota(jnp.int32, (tk, tq), 0)
@@ -311,7 +307,7 @@
             grad = (p * dot(vwin[pl.ds(at, tk), :], da, 1, 1)).astype(BF)
             dv[pl.ds(at, tk), :] += dot(p.astype(BF), do2)
             dk[pl.ds(at, tk), :] += dot(grad, q2)
-            dqs[...] += dot(grad, ka[:, :HD], 0, 0)
+            dqs[...] += dot(grad, ka, 0, 0)
 
         def body(kt, carry, step=step, flo=flo, fhi=fhi):
             inside = (kt >= flo) & (kt < fhi)
@@ -336,27 +332,28 @@
         dkvs[b][:, HD:] = dv[part, :].astype(BF)
 
 
-def flash_bwd(scalars, q, starts_row, das, outs, augs, segs, window, gs, tq, tk):
+def flash_bwd(scalars, q, starts_row, das, outs, sums, segs, window, gs, tq, tk, heads):
     span, total = q.shape
     width = gs * HD
-    heads = total // width
+    h0, count = heads
     nc, nb, nq = len(das), window // span, span // tq
     rows = das[0].shape[0]
-    chunk = pl.BlockSpec((rows, width), lambda h, s: (0, h))
-    seg_specs = [pl.BlockSpec((seg.shape[0], 2 * HD), lambda h, s: (0, h)) for seg in segs]
+    chunk = lambda w: pl.BlockSpec((rows, w), lambda h, s: (0, h0 + h))
+    seg_specs = [pl.BlockSpec((seg.shape[0], 2 * HD), lambda h, s: (0, h0 + h)) for seg in segs]
     pairs = span * (window // 2)
     return pl.pallas_call(
         functools.partial(
             flash_bwd_kernel, nc=nc, ns=len(segs), nb=nb, nq=nq, tq=tq, tk=tk, gs=gs,
-            row0=window - span, at_bases=4 * nq,
+            row0=window - span,
         ),
         grid_spec=grid_spec(
             1,
-            (heads,),
+            (count,),
             [
-                pl.BlockSpec((span, width), lambda h, s: (0, h)),
+                pl.BlockSpec((span, width), lambda h, s: (0, h0 + h)),
                 pl.BlockSpec((8, span), lambda h, s: (0, 0)),
-                *([chunk] * (3 * nc)),
+                *([chunk(width)] * (2 * nc)),
+                *([chunk(HD)] * nc),
                 *seg_specs,
             ],
             [
@@ -364,21 +361,18 @@
                 *([pl.BlockSpec((span, 2 * HD), lambda h, s: (0, h))] * nb),
             ],
             [
-                pltpu.VMEM((window, 2 * HD), BF),
+                pltpu.VMEM((window, HD), BF),
                 pltpu.VMEM((window, 2 * HD), BF),
                 pltpu.VMEM((window, HD), F32),
                 pltpu.VMEM((window, HD), F32),
                 pltpu.VMEM((gs * tq, HD), F32),
             ],
         ),
-        out_shape=[sds((span, total), F32)] + [sds((span, heads * 2 * HD), BF)] * nb,
+        out_shape=[sds((span, count * width), F32)] + [sds((span, count * 2 * HD), BF)] * nb,
         compiler_params=params(),
-        cost_estimate=cost(
-            heads * gs * pairs * 14 * HD, 20 * q.size + sum(2 * x.size for x in segs),
-            heads * gs * pairs,
-        ),
+        cost_estimate=cost(80 * count * width // total),
         name="flash_bwd",
-    )(scalars, q, starts_row, *das, *outs, *augs, *segs)
+    )(scalars, q, starts_row, *das, *outs, *sums, *segs)
 
 
 def mlp_kernel(*refs, np_):
@@ -453,7 +447,7 @@
             sds((rows, d), BF),
         ],
         compiler_params=params(),
-        cost_estimate=cost(10 * rows * d * ff, 6 * d * ff + 6 * rows * ff + 10 * rows * d),
+        cost_estimate=cost(47),
         name="mlp",
     )(x, *parts, gain, cot, wg, wu, wd)
 
@@ -500,7 +494,7 @@
         out_specs=[tile, pl.BlockSpec((tm, n), lambda i: (i, 0)), pl.BlockSpec((8, d), lambda i: (0, 0))],
         out_shape=[sds((rows, d), BF), sds((rows, n), BF), sds((8, d), F32)],
         compiler_params=params(),
-        cost_estimate=cost(2 * rows * d * n, 14 * rows * d + 2 * d * n),
+        cost_estimate=cost(11),
         name="mid_backward",
     )(x, *parts, *grads, gain, cot, w_out)
 
@@ -523,44 +517,52 @@
         ref[...] += value
 
 
-def q_back_kernel(dq_ref, raw_ref, cos_ref, sin_ref, hg_ref, low_ref, gain_ref):
+def q_back_kernel(*refs, ng):
+    dqs = refs[:ng]
+    raw_ref, cos_ref, sin_ref, hg_ref, low_ref, gain_ref = refs[ng:]
     total = jnp.zeros(gain_ref.shape, F32)
-    for h in range(dq_ref.shape[1] // HD):
-        at = slice(h * HD, (h + 1) * HD)
-        back, part = head_back(dq_ref[:, at], raw_ref[:, at], hg_ref[...], cos_ref[...], sin_ref[...])
+    per = dqs[0].shape[1] // HD
+    for h in range(raw_ref.shape[1] // HD):
+        at, sub = slice(h * HD, (h + 1) * HD), slice(h % per * HD, (h % per + 1) * HD)
+        back, part = head_back(
+            dqs[h // per][:, sub], raw_ref[:, at], hg_ref[...], cos_ref[...], sin_ref[...]
+        )
         low_ref[:, at] = back.astype(BF)
         total = total + part
     add_out(gain_ref, total)
 
 
-def q_back(dq, raw, cosine, sine, hg, tm):
-    rows, n = dq.shape
+def q_back(dqs, raw, cosine, sine, hg, tm):
+    rows, n = raw.shape
     tile = pl.BlockSpec((tm, n), lambda i: (i, 0))
+    part = pl.BlockSpec((tm, n // len(dqs)), lambda i: (i, 0))
     table = pl.BlockSpec((tm, HD), lambda i: (i, 0))
     return pl.pallas_call(
-        q_back_kernel,
+        functools.partial(q_back_kernel, ng=len(dqs)),
         grid=(rows // tm,),
-        in_specs=[tile, tile, table, table, fixed((1, HD))],
+        in_specs=[*([part] * len(dqs)), tile, table, table, fixed((1, HD))],
         out_specs=[tile, pl.BlockSpec((8, HD), lambda i: (0, 0))],
         out_shape=[sds((rows, n), BF), sds((8, HD), F32)],
         compiler_params=params(),
-        cost_estimate=cost(30 * rows * n, 10 * rows * n),
+        cost_estimate=cost(8.5),
         name="q_back",
-    )(dq, raw, cosine, sine, hg)
-
-
-def in_kernel(s_ref, *refs, nk):
-    dkvs = refs[:nk]
+    )(*dqs, raw, cosine, sine, hg)
+
+
+def in_kernel(s_ref, *refs, ng, nk):
+    groups = [refs[g * nk : (g + 1) * nk] for g in range(ng)]
     (raw_ref, dq_ref, x_ref, cos_ref, sin_ref, hg_ref, wq_ref, wk_ref, wv_ref,
-     low_ref, ga_ref, gain_ref, gn_ref) = refs[nk:]
+     low_ref, ga_ref, gain_ref, gn_ref) = refs[ng * nk :]
     heads = raw_ref.shape[1] // HD
+    per = heads // ng
     total = jnp.zeros(gain_ref.shape, F32)
     for h in range(heads):
-        dk = dkvs[0][:, 2 * h * HD : (2 * h + 1) * HD].astype(F32)
-        dv = dkvs[0][:, (2 * h + 1) * HD : (2 * h + 2) * HD].astype(F32)
-        for ref in dkvs[1:]:
-            dk = dk + ref[:, 2 * h * HD : (2 * h + 1) * HD].astype(F32)
-            dv = dv + ref[:, (2 * h + 1) * HD : (2 * h + 2) * HD].astype(F32)
+        k_at = slice(2 * (h % per) * HD, (2 * (h % per) + 1) * HD)
+        v_at = slice((2 * (h % per) + 1) * HD, (2 * (h % per) + 2) * HD)
+        dk, dv = 0.0, 0.0
+        for ref in groups[h // per]:
+            dk = dk + ref[:, k_at].astype(F32)
+            dv = dv + ref[:, v_at].astype(F32)
         at = slice(h * HD, (h + 1) * HD)
         back, part = head_back(dk, raw_ref[:, at], hg_ref[...], cos_ref[...], sin_ref[...])
         low_ref[:, at] = back.astype(BF)
@@ -578,19 +580,21 @@
     add_out(gn_ref, fold_rows(ga * (x * rms(x))))
 
 
-def in_back(dkvs, raw, dq_low, x, base_tile, cosine, sine, hg, wq, wk, wv, tm):
+def in_back(groups, raw, dq_low, x, base_tile, cosine, sine, hg, wq, wk, wv, tm):
     rows, n = raw.shape
     d = x.shape[1]
     nq = wq.shape[1]
+    ng, nk = len(groups), len(groups[0])
     moved = lambda width: pl.BlockSpec((tm, width), lambda i, s: (s[0] + i, 0))
     tile = lambda width: pl.BlockSpec((tm, width), lambda i, s: (i, 0))
     return pl.pallas_call(
-        functools.partial(in_kernel, nk=len(dkvs)),
+        functools.partial(in_kernel, ng=ng, nk=nk),
         grid_spec=grid_spec(
             1,
             (rows // tm,),
             [
-                *([moved(2 * n)] * len(dkvs)), tile(n), moved(nq), moved(d), moved(HD), moved(HD),
+                *([moved(2 * n // ng)] * (ng * nk)),
+                tile(n), moved(nq), moved(d), moved(HD), moved(HD),
                 fixed((1, HD)), fixed((d, nq)), fixed((d, n)), fixed((d, n)),
             ],
             [
@@ -600,15 +604,16 @@
         ),
         out_shape=[sds((rows, 2 * n), BF), sds((rows, d), BF), sds((8, HD), F32), sds((8, d), F32)],
         compiler_params=params(),
-        cost_estimate=cost(
-            2 * rows * d * (nq + 2 * n), 4 * rows * d + 2 * d * (nq + 2 * n) + 12 * rows * n
-        ),
+        cost_estimate=cost(12.5),
         name="in_back",
-    )(jnp.reshape(base_tile, (1,)), *dkvs, raw, dq_low, x, cosine, sine, hg, wq, wk, wv)
-
-
-def wgrad_kernel(s_ref, *refs, nt, na, row_type, ns):
-    out_ref, aside = refs[2 * nt + na], refs[2 * nt + na + 1 :]
+    )(
+        jnp.reshape(base_tile, (1,)), *[v for g in groups for v in g], raw, dq_low, x, cosine,
+        sine, hg, wq, wk, wv,
+    )
+
+
+def wgrad_kernel(s_ref, *refs, nt, na, cut, row_type, ns):
+    outs, aside = refs[2 * nt + na : 2 * nt + na + cut], refs[2 * nt + na + cut :]
     if row_type:
         turned = aside[0]
 
@@ -631,17 +636,33 @@
         else:
             size = total.shape[1] // ns
             piece = total[:, n * size : (n + 1) * size]
+        adds, n_at = [], n
         for add in refs[2 * nt : 2 * nt + na]:
-            piece = piece + add[0, n].astype(F32)
-        out_ref[0, n] = piece.astype(BF)
-
-
-def wgrad(terms, blocks, addends, row_type, nd, ns, rows):
+            if 0 <= n_at < add.shape[1]:
+                adds.append(add[0, n_at])
+            n_at = n if add.shape[1] == ns else n_at - add.shape[1]
+        for add in adds:
+            piece = piece + add.astype(F32)
+        outs[n * cut // ns][0, n % (ns // cut)] = piece.astype(BF)
+
+
+def after(value, *others):
+    return lax.optimization_barrier((value, *others))[0]
+
+
+def nought(value):
+    return jnp.minimum(jnp.abs(value[:1, :1].astype(F32)), 0.0)
+
+
+def wgrad(terms, blocks, addends, row_type, nd, ns, rows, behind, cut=1, done=()):
     nb, nt = len(blocks), len(terms)
     scalars = jnp.stack(
         [jnp.asarray(v, jnp.int32) for v in blocks]
-        + [jnp.asarray(v, jnp.int32) for t in terms for v in (t[1], t[3])]
+        + [jnp.asarray(v(), jnp.int32) for t in terms for v in (t[1], t[3])]
     )
+    scalars = after(scalars, *behind)
+    for value in done:
+        scalars = scalars + nought(value)[0].astype(jnp.int32)
     left, right = terms[0][0].shape[1], terms[0][2].shape[1]
     ins = []
     if row_type:
@@ -652,11 +673,10 @@
             ins.append(pl.BlockSpec((rows, bw), lambda b, t, s, n=n: (s[nb + 2 * n], s[b])))
             ins.append(pl.BlockSpec((rows, tile), lambda b, t, s, n=n: (s[nb + 2 * n + 1], t)))
         out_dims = (ns, bw // ns, right)
-        block = (1, ns, bw // ns, tile)
+        block = lambda n: (1, n, bw // ns, tile)
         at = lambda b, t, s: (b, 0, 0, t)
         add_at = lambda k: lambda b, t, s: (k, 0, 0, t)
         scratch = [pltpu.VMEM((nt, bw, rows), BF)]
-        flops = 2 * nb * nt * rows * bw * right
     else:
         bw = right // nd
         tile = min(512, left)
@@ -665,53 +685,180 @@
             ins.append(pl.BlockSpec((rows, tile), lambda b, t, s, n=n: (s[nb + 2 * n], t)))
             ins.append(pl.BlockSpec((rows, bw), lambda b, t, s, n=n: (s[nb + 2 * n + 1], s[b])))
         out_dims = (ns, left, bw // ns)
-        block = (1, ns, tile, bw // ns)
+        block = lambda n: (1, n, tile, bw // ns)
         at = lambda b, t, s: (b, 0, t, 0)
         add_at = lambda k: lambda b, t, s: (k, 0, t, 0)
         scratch = []
-        flops = 2 * nb * nt * rows * bw * left
+    work = 2e-9 * nt * rows * left * right / nd
     operands = [v for t in terms for v in (t[0], t[2])]
     for arr, k in addends:
-        ins.append(pl.BlockSpec(block, add_at(k)))
+        ins.append(pl.BlockSpec(block(arr.shape[1]), add_at(k)))
         operands.append(arr)
     size = nb * math.prod(out_dims)
     return pl.pallas_call(
-        functools.partial(wgrad_kernel, nt=nt, na=len(addends), row_type=row_type, ns=ns),
-        grid_spec=grid_spec(1, (nb, steps), ins, pl.BlockSpec(block, at), scratch),
-        out_shape=sds((nb, *out_dims), BF),
+        functools.partial(wgrad_kernel, nt=nt, na=len(addends), cut=cut, row_type=row_type, ns=ns),
+        grid_spec=grid_spec(
+            1, (nb, steps), ins, [pl.BlockSpec(block(ns // cut), at)] * cut, scratch
+        ),
+        out_shape=[sds((nb, ns // cut, *out_dims[1:]), BF)] * cut,
         compiler_params=params(),
-        cost_estimate=cost(
-            flops, 2 * size * (1 + len(addends)) + 2 * nt * rows * (left + right)
-        ),
+        cost_estimate=cost(1 + 3 * work),
         name="wgrad",
     )(scalars, *operands)
 
 
-def reduce_weights(terms, row_type, nd, ns, rows, z):
-    d = lax.axis_index("dp")
-    make = lambda blocks, adds: wgrad(terms, blocks, adds, row_type, nd, ns, rows)
-    side = [(k, k ^ 1) for k in range(nd)]
-    across = [(k, k ^ 2) for k in range(nd)]
-    got = lax.ppermute(make([d ^ 1, d ^ 3], []), "dp", side)
-    far = make([d ^ 2], [(got, 1)])
-    near = make([d], [(got, 0)])
-    come = lax.ppermute(far, "dp", across)
-
-    def piece(j):
-        j = jnp.clip(j, 0, ns - 1)
-        take = lambda v: lax.dynamic_index_in_dim(v[0], j, 0, keepdims=False).astype(F32)
-        return take(near) + take(come)
-
-    total, right, left = piece(z), None, None
-    for s in range(1, ns):
-        send_right, send_left = piece(ns - s + z), piece(z + s - ns)
-        if right is not None:
-            send_right, send_left = send_right + right.astype(F32), send_left + left.astype(F32)
-        right = lax.ppermute(send_right.astype(BF), "seq", [(k, k + 1) for k in range(s)])
-        left = lax.ppermute(
-            send_left.astype(BF), "seq", [(ns - 1 - k, ns - 2 - k) for k in range(s)]
+def flip(d, bits):
+    return {1: d + 1 - 2 * (d % 2), 2: d + 2 - 4 * (d // 2), 3: 3 - d}[bits]
+
+
+def wgrad_send_kernel(*refs, nt, row_type, ns, steps, tile):
+    ins, out_ref = refs[: 2 * nt], refs[2 * nt]
+    slots, send_sem, recv_sem = refs[2 * nt + 1 : 2 * nt + 4]
+    b, t = pl.program_id(0), pl.program_id(1)
+    k = b * steps + t
+    last = 2 * steps - 1
+    partner = {"dp": flip(lax.axis_index("dp"), 1)}
+
+    @pl.when(k == 0)
+    def _():
+        barrier = pltpu.get_barrier_semaphore()
+        pl.semaphore_signal(
+            barrier, inc=1, device_id=partner, device_id_type=pl.DeviceIdType.MESH
         )
-    return total + right.astype(F32) + left.astype(F32)
+        pl.semaphore_wait(barrier, 1)
+
+    def copy(src, dst, slot):
+        return pltpu.make_async_remote_copy(
+            src_ref=src, dst_ref=dst, send_sem=send_sem.at[slot], recv_sem=recv_sem,
+            device_id=partner, device_id_type=pl.DeviceIdType.MESH,
+        )
+
+    def place(b, t):
+        at = pl.ds(pl.multiple_of(t * tile, tile), tile)
+        return out_ref.at[b, :, :, at] if row_type else out_ref.at[b, :, at, :]
+
+    slot = k % 2
+
+    @pl.when(k >= 2)
+    def _():
+        copy(slots.at[slot], place(b, t), slot).wait_send()
+
+    if row_type:
+        turned = refs[2 * nt + 4]
+
+        @pl.when(t == 0)
+        def _():
+            for n in range(nt):
+                turned[n] = ins[2 * n][...].T
+
+        total = dot(turned[0], ins[1][...])
+        for n in range(1, nt):
+            total = total + dot(turned[n], ins[2 * n + 1][...])
+    else:
+        total = dot(ins[0][...], ins[1][...], 0, 0)
+        for n in range(1, nt):
+            total = total + dot(ins[2 * n][...], ins[2 * n + 1][...], 0, 0)
+    size = total.shape[0 if row_type else 1] // ns
+    for n in range(ns):
+        piece = total[n * size : (n + 1) * size] if row_type else total[:, n * size : (n + 1) * size]
+        slots[slot, n] = piece.astype(BF)
+    copy(slots.at[slot], place(b, t), slot).start()
+
+    @pl.when(k == last)
+    def _():
+        copy(slots.at[1 - slot], place(b, t), 1 - slot).wait_send()
+        copy(slots.at[slot], place(b, t), slot).wait_send()
+        copy(out_ref, out_ref, slot).wait_recv()
+
+
+def wgrad_send(terms, row_type, nd, ns, rows, ident, behind):
+    nt = len(terms)
+    left, right = terms[0][0].shape[1], terms[0][2].shape[1]
+    block = lambda b: jnp.where(
+        b == 0, flip(lax.axis_index("dp"), 1), flip(lax.axis_index("dp"), 3)
+    )
+    ins = []
+    if row_type:
+        bw = left // nd
+        tile = min(512, right)
+        steps = right // tile
+        for t in terms:
+            ins.append(pl.BlockSpec((rows, bw), lambda b, s, r=t[1]: (r(), block(b))))
+            ins.append(pl.BlockSpec((rows, tile), lambda b, s, r=t[3]: (r(), s)))
+        out_dims, slot = (ns, bw // ns, right), (ns, bw // ns, tile)
+        scratch = [pltpu.VMEM((nt, bw, rows), BF)]
+    else:
+        bw = right // nd
+        tile = min(512, left)
+        steps = left // tile
+        for t in terms:
+            ins.append(pl.BlockSpec((rows, tile), lambda b, s, r=t[1]: (r(), s)))
+            ins.append(pl.BlockSpec((rows, bw), lambda b, s, r=t[3]: (r(), block(b))))
+        out_dims, slot = (ns, left, bw // ns), (ns, tile, bw // ns)
+        scratch = []
+    work = 2e-9 * nt * rows * left * right / nd
+    operands = [v for t in terms for v in (t[0], t[2])]
+    operands[0] = after(operands[0], *behind)
+    return pl.pallas_call(
+        functools.partial(
+            wgrad_send_kernel, nt=nt, row_type=row_type, ns=ns, steps=steps, tile=tile
+        ),
+        grid=(2, steps),
+        in_specs=ins,
+        out_specs=pl.BlockSpec(memory_space=pl.ANY),
+        scratch_shapes=[
+            pltpu.VMEM((2, *slot), BF), pltpu.SemaphoreType.DMA((2,)), pltpu.SemaphoreType.DMA,
+            *scratch,
+        ],
+        out_shape=sds((2, *out_dims), BF),
+        compiler_params=params(collective_id=ident, has_side_effects=True),
+        cost_estimate=cost(2 + 4.4 * work),
+        name="wgrad_send",
+    )(*operands)
+
+
+class Shrink:
+    def __init__(self, terms, row_type, ahead=None, small=False, *, nd, ns, rows):
+        self.small = small
+        self.args, self.nd = (terms, row_type), nd
+        self.ahead = ahead
+        self.ident = ahead.ident + 1 if ahead else 0
+        self.sizes = (nd, ns, rows)
+        self.d = lax.axis_index("dp")
+
+    def make(self, blocks, adds, behind, **more):
+        terms, row_type = self.args
+        return wgrad(terms, blocks, adds, row_type, *self.sizes, behind, **more)
+
+    def send(self, *behind):
+        terms, row_type = self.args
+        self.got = wgrad_send(terms, row_type, *self.sizes, self.ident, behind)
+        return self.got
+
+    def far(self, *behind, done=()):
+        out = self.make([self.d ^ 2], [(self.got, 1)], behind, done=done)[0]
+        first = [self.ahead.ahead.come] if self.ahead and self.ahead.ahead else []
+        self.come = lax.ppermute(
+            after(out, *first), "dp", [(k, k ^ 2) for k in range(self.nd)]
+        )
+        return out
+
+    def near(self, *behind):
+        self.here = self.make([self.d], [(self.got, 0), (self.come, 0)], behind)[0]
+        if not self.small:
+            self.share = lax.psum_scatter(self.here[0], "seq", scatter_dimension=0)
+        return self.here
+
+    def finish(self):
+        if not self.small:
+            return self.share.astype(F32)
+        z, ns = lax.axis_index("seq"), self.sizes[1]
+        piece = lambda j: lax.dynamic_index_in_dim(self.here[0], j, 0, keepdims=False)
+        first = jnp.stack([piece(z ^ 1), piece(z ^ 3)])
+        first = lax.ppermute(first, "seq", [(k, k ^ 1) for k in range(ns)]).astype(F32)
+        second = (piece(z ^ 2).astype(F32) + first[1]).astype(BF)
+        second = lax.ppermute(second, "seq", [(k, k ^ 2) for k in range(ns)])
+        return piece(z).astype(F32) + first[0] + second.astype(F32)
 
 
 def final_kernel(x_ref, ga_ref, gb_ref, h0_ref, h1_ref, gain_ref, s_ref, out_ref):
@@ -733,7 +880,7 @@
         out_specs=tile,
         out_shape=sds((rows, d), BF),
         compiler_params=params(),
-        cost_estimate=cost(20 * rows * d, 12 * rows * d),
+        cost_estimate=cost(8),
         name="final",
     )(x, ga, gb, h0, h1, gain, jnp.reshape(y, (1,)))
 
@@ -770,11 +917,13 @@
     starts_col = jnp.broadcast_to(rel[:, None], (span, HD))
     starts_row = jnp.broadcast_to(rel[None, :], (8, span))
 
-    def bounds(first_row, count):
+    def bounds(first_row, count, w0, w1):
         heads = rel[first_row : first_row + count : tq]
         tails = rel[first_row + tq - 1 : first_row + count : tq]
         at = window - span + first_row + tq * jnp.arange(count // tq, dtype=jnp.int32)
-        return [heads // tk, (at + tq - 1) // tk + 1, (tails + tk - 1) // tk, (at + 1) // tk]
+        inside = lambda v: jnp.clip(v - w0, 0, w1 - w0)
+        up = lambda v: (v + tk - 1) // tk
+        return [inside(heads) // tk, up(inside(at + tq)), up(inside(tails)), inside(at + 1) // tk]
 
     if nt == 2:
         other = swap(tokens)
@@ -789,7 +938,8 @@
     bases = [jnp.asarray(b, jnp.int32) for b in bases]
     base_tiles = [b // tm for b in bases]
 
-    hops, raws, seg_bases = [], [], []
+    segs, seg_bases = [[] for _ in range(back + 1)], [[] for _ in range(back + 1)]
+    raws = []
     ahead = [(k, k + 1) for k in range(ns - 1)]
     for x_piece, base, base_tile in zip(pieces, bases, base_tiles):
         kv, raw = project_kv(
@@ -797,8 +947,8 @@
         )
         raws.append(raw)
         for hop in range(back + 1):
-            hops.append(kv)
-            seg_bases.append((back - hop) * span + base)
+            segs[hop].append(kv)
+            seg_bases[hop].append((back - hop) * span + base)
             if hop < back:
                 kv = lax.ppermute(kv, "seq", ahead)
     x_all, attn_in, query, q_raw = project_q(
@@ -806,63 +956,109 @@
         row(query_norm), tm,
     )
 
-    outs, augs, parts = [], [], []
+    attend = functools.partial(flash_fwd, bounds, gs=gs, tq=tq, tk=tk, window=window)
+    prior = []
+    for hop in range(back):
+        part = ((back - hop) * span, (back - hop + 1) * span)
+        prior = attend(
+            seg_bases[hop], query, starts_col, segs[hop], prior, part=part, row_at=0, rows=span,
+            last=False,
+        )
+    outs, sums, parts = [], [], []
     for c in range(2):
-        scalars = jnp.concatenate([*bounds(c * rows, rows), jnp.stack(seg_bases)])
-        out, aug = flash_fwd(scalars, query, starts_col, hops, window, c, rows, gs, tq, tk)
+        out, total = attend(
+            seg_bases[back], query, after(starts_col, *outs), segs[back], prior, part=(0, span),
+            row_at=c * rows, rows=rows, last=True,
+        )
         outs.append(out)
-        augs.append(aug)
+        sums.append(total)
         partial = dot(out, w_out).astype(BF)
         parts.append([partial, swap(partial)] if nt == 2 else [lax.psum(partial, "tensor")])
 
     low_mlp, hidden, d_gate, d_up, grads = [], [], [], [], []
-    tf = min(256, w_gate.shape[1])
+    tf = min(512, w_gate.shape[1] // 2)
     for c in range(2):
-        m, h, dg, du, gm = mlp(x_all, parts[c], cot, row(norm_mlp), w_gate, w_up, w_down, c, tf)
+        m, h, dg, du, gm = mlp(
+            x_all, parts[c], cot, after(row(norm_mlp), *low_mlp), w_gate, w_up, w_down, c, tf
+        )
         low_mlp.append(m)
         hidden.append(h)
         d_gate.append(dg)
         d_up.append(du)
         grads.append([gm, swap(gm)] if nt == 2 else [lax.psum(gm, "tensor")])
-    shrink = functools.partial(reduce_weights, nd=nd, ns=ns, rows=rows, z=z)
-    g_down = shrink([(hidden[c], 0, cot, c) for c in range(2)], False)
-    g_gate = shrink([(low_mlp[c], 0, d_gate[c], 0) for c in range(2)], True)
-    g_up = shrink([(low_mlp[c], 0, d_up[c], 0) for c in range(2)], True)
-
+
+    shrink = functools.partial(Shrink, nd=nd, ns=ns, rows=rows)
+    zero = lambda: 0
+    chunk = lambda c: lambda: c
+    down = shrink([(hidden[c], zero, cot, chunk(c)) for c in range(2)], False)
+    gate = shrink([(low_mlp[c], zero, d_gate[c], zero) for c in range(2)], True, down)
+    up = shrink([(low_mlp[c], zero, d_up[c], zero) for c in range(2)], True, gate)
     gh, g_att, g_norm_two = [], [], []
-    for c in range(2):
-        low, ga, gn = mid_backward(x_all, parts[c], grads[c], cot, row(norm_mlp), w_out, c, tm)
+
+    def middle(c, *behind):
+        low, ga, gn = mid_backward(
+            x_all, parts[c], grads[c], cot, after(row(norm_mlp), *behind), w_out, c, tm
+        )
         gh.append(low)
         g_att.append(ga)
         g_norm_two.append(gn)
-    g_out = shrink([(outs[c], 0, gh[c], 0) for c in range(2)], False)
-    scalars = jnp.concatenate([*bounds(0, span), jnp.stack(seg_bases)])
-    dq, *dkvs = flash_bwd(
-        scalars, query, starts_row, g_att, outs, augs, hops, window, gs, tq, tk
-    )
+        return low
+
+    down.send()
+    middle(0)
+    middle(1, gh[0], gate.send(down.far()))
+    t = []
+    hop_segs = [v for seg in segs for v in seg]
+    hop_bases = jnp.stack([v for b in seg_bases for v in b])
+    scalars = jnp.concatenate([*bounds(0, span, 0, window), hop_bases])
+    halves = [(0, heads_kv)] if heads_kv == 1 else [(0, heads_kv // 2), (heads_kv // 2, heads_kv // 2)]
     behind = [(k + 1, k) for k in range(ns - 1)]
-    come = None
-    for b in range(back):
-        send = dkvs[b]
-        if come is not None:
-            send = (send.astype(F32) + come.astype(F32)).astype(BF)
-        come = lax.ppermute(send, "seq", behind)
-    dkv = [dkvs[back]] + ([come] if come is not None else [])
-
-    dq_low, g_qn = q_back(dq, q_raw, cosine, sine, row(query_norm), tm)
-    g_query = shrink([(attn_in, c, dq_low, c) for c in range(2)], True)
+    dqs, dkvs = [], []
+    for part, heads in enumerate(halves):
+        dq, *dkv = flash_bwd(
+            after(scalars, *t), query, starts_row, g_att, outs, sums, hop_segs, window, gs, tq, tk,
+            heads,
+        )
+        come = None
+        for b in range(back):
+            send = dkv[b]
+            if come is not None:
+                send = (send.astype(F32) + come.astype(F32)).astype(BF)
+            come = lax.ppermute(send, "seq", behind)
+        dqs.append(dq)
+        dkvs.append([dkv[back]] + ([come] if come is not None else []))
+        if part == 0:
+            t = [gate.far(gh[1]), down.near(dq)]
+    out_w = shrink([(outs[c], zero, gh[c], zero) for c in range(2)], False, up, True)
+    t = up.far(gate.near(up.send(*dqs)))
+    dq_low, g_qn = q_back(dqs, q_raw, cosine, sine, after(row(query_norm), t), tm)
+    query_w = shrink([(attn_in, chunk(c), dq_low, chunk(c)) for c in range(2)], True, out_w, True)
+    t = out_w.far(out_w.send(dq_low))
+    t = query_w.far(query_w.send(t))
+    w_down_later = after(w_down, dq_low)
+    downs = [dot(hidden[c], w_down_later).astype(BF) for c in range(2)]
+    t = [t, *downs]
+
     lows, gas, g_kn, g_norm_one = [None] * 2, [None] * 2, [], []
     for n in (1, 0):
         lows[n], gas[n], gain_part, norm_part = in_back(
-            dkv, raws[n], dq_low, x_all, base_tiles[n], cosine, sine, row(key_norm),
+            dkvs, raws[n], dq_low, x_all, base_tiles[n], cosine, sine, after(row(key_norm) + nought(down.share), *t),
             w_query, w_key, w_value, tm,
         )
         g_kn.append(gain_part)
         g_norm_one.append(norm_part)
     kv_cut = heads_kv * HD
-    g_kv = shrink([(attn_in, bases[n] // rows, lows[n], 0) for n in range(2)], True)
-
-    downs = [dot(hidden[c], w_down).astype(BF) for c in range(2)]
+    own_half = lambda: lax.axis_index("tensor")
+    half_of = lambda n: chunk(n) if nt != 2 else own_half if n == 0 else lambda: 1 - own_half()
+    kv_w = shrink([(attn_in, half_of(n), lows[n], zero) for n in range(2)], True, query_w, True)
+    kv_w.send()
+    t = up.near(kv_w.far(done=[gate.share]))
+    t = query_w.near(out_w.near(t))
+    kv_w.near(t)
+    g_down, g_gate, g_up, g_out, g_query, g_kv = [
+        v.finish() for v in (down, gate, up, out_w, query_w, kv_w)
+    ]
+
     up32 = lambda v: v.astype(F32)
     if nt == 2:
         come_down = swap(pick(downs[1], downs[0]))
@@ -886,15 +1082,25 @@
 
     share = 1.0 / nt
     fold = lambda pair: jnp.sum(pair[0] + pair[1], axis=0)
+    axes = (("dp", nd), ("seq", ns), ("tensor", nt))
     packed = jnp.concatenate(
         [fold(g_norm_one), fold(g_norm_two) * share, jnp.sum(g_qn, axis=0), fold(g_kn)]
     )
-    packed = lax.psum(packed, ("dp", "seq", "tensor"))
+    packed = total_sum(packed, axes)
     return (
         result.astype(BF)[None], grad_tokens[None], g_query, g_kv[:, :kv_cut], g_kv[:, kv_cut:],
         g_out, g_gate, g_up, g_down,
         packed[:d], packed[d : 2 * d], packed[2 * d : 2 * d + HD], packed[2 * d + HD :],
     )
+
+
+def total_sum(v, sizes):
+    for name, size in sizes:
+        step = 1
+        while step < size:
+            v = v + lax.ppermute(v, name, [(k, k ^ step) for k in range(size)])
+            step *= 2
+    return v
 
 
 def solution(mesh):

time: 1190 us -> 817 us (0.69); the launches traced: 1160 us -> 807 us
  blocking collectives: 178 us -> 0 us
  starting transfers between devices: 190 us -> 59.1 us
  other arithmetic: 67.4 us -> 32.4 us
  waiting for transfers between devices: 220 us -> 197 us
  Pallas kernels: 463 us -> 448 us
  between operations: 2.14 us -> 16 us
  local copies, waits for them, and re-layouts: 14.2 us -> 27.5 us
    psum x1 -> x0, blocking collectives: 178 us -> none  [per_device(): packed = lax.psum(packed, ('dp', 'seq', 'tensor'))]
    ppermute x48 -> x17, starting transfers between devices: 159 us -> 27.4 us  [the longest x5 12 us: total_sum(): v = v + lax.ppermute(v, name, [(k, k ^ step) for k in range(size)])]
    pallas_call x2, Pallas kernels: 151 us -> 96.3 us  [mlp(): pl.pallas_call(functools.partial(mlp_kernel, np_=len(parts)), grid=(ff //...]
    ppermute x2 -> x4, waiting for transfers between devices: 7.45 us -> 61.3 us  [per_device(): come = lax.ppermute(send, 'seq', behind)]
    ppermute x4, waiting for transfers between devices: 39.5 us -> 6.31 us  [per_device(): kv = lax.ppermute(kv, 'seq', ahead)]
    pallas_call x23 -> x25, Pallas kernels: 224 us -> 257 us  [the longest x12 93.1 us: wgrad(): pl.pallas_call(functools.partial(wgrad_kernel, nt=nt, na=len(addends), cu...]
    ppermute x48 -> x17, waiting for transfers between devices: 103 us -> 74.5 us  [the longest x5 31.5 us: total_sum(): v = v + lax.ppermute(v, name, [(k, k ^ step) for k in range(size)])]
    convert_element_type x24 -> x9, other arithmetic: 31.6 us -> 5.42 us  [the longest x3 4.97 us: finish(): return self.share.astype(F32)]
  transfers between devices with their start and end apart: 62 -> 36, of which waited for: 24 -> 14; matrix products, arithmetic and copies ran while one was open for 9% -> 9% of each run, Pallas kernels for 35% -> 54%
where the time goes in v1:
time: 817 us; the launch traced here: 807 us
  Pallas kernels  448 us (55%)
  waiting for transfers between devices  197 us (24%)
  starting transfers between devices  59.1 us (7%)
  other arithmetic  32.4 us (4%)
  local copies, waits for them, and re-layouts  27.5 us (3%)
  matrix products  26.8 us (3%)
  between operations  16 us (2%)
    pallas_call x2, Pallas kernels, mlp(): pl.pallas_call(functools.partial(mlp_kernel, np_=len(parts)), grid=(ff //...  96.3 us
    pallas_call x12, Pallas kernels, wgrad(): pl.pallas_call(functools.partial(wgrad_kernel, nt=nt, na=len(addends), cu...  93.1 us
    pallas_call x6, Pallas kernels, wgrad_send(): pl.pallas_call(functools.partial(wgrad_send_kernel, nt=nt, row_type=row_t...  76.6 us
    ppermute x4, waiting for transfers between devices, per_device(): come = lax.ppermute(send, 'seq', behind)  61.3 us
    ppermute x8, waiting for transfers between devices, per_device(): swap = lambda v: lax.ppermute(v, 'tensor', [(0, 1), (1, 0)])  55.2 us
    pallas_call x4, Pallas kernels, flash_fwd(): pl.pallas_call(functools.partial(flash_fwd_kernel, nseg=len(segs), prior=...  53.6 us
    pallas_call x2, Pallas kernels, flash_bwd(): pl.pallas_call(functools.partial(flash_bwd_kernel, nc=nc, ns=len(segs), n...  37.9 us
    ppermute x5, waiting for transfers between devices, total_sum(): v = v + lax.ppermute(v, name, [(k, k ^ step) for k in range(size)])  31.5 us
  transfers between devices with their start and end apart: 36, of which 14 were waited for; matrix products, arithmetic and copies ran while one was open for 9% of the time, Pallas kernels for 54%

profile of v1, /device:TPU:0, one launch (start us, length us, event | category | flops | bytes accessed | tf_op | source)
XLA Modules:
  0.0 807.4 jit_solution(4659779200160437117)
XLA Ops:
  15.4 6.5 project_kv.2
  27.1 29.1 %collective-permute-done.xb_ref.x_ref = bf16[512,2048]{1,0:T(8,128)(2,1)} collective-permute-done((bf16[512,2048]{1,0:T(8,128)(2,1)}, bf16[512,2048]{1,0:T(8,128)(2,1)}, u32[]{:S(2)}, u32[]{:S(2)}) %collective-permute-start) | collective-permute-done | bytes 2097184 | tf_op jit(solution)/shard_map/ppermute | solution.py:902
  56.2 6.6 project_kv.3
  74.0 13.2 %project_q.1 = (bf16[1024,2048]{1,0:T(8,128)(2,1)}, bf16[1024,2048]{1,0:T(8,128)(2,1)}, bf16[1024,1024]{1,0:T(8,128)(2,1)}, f32[1024,1024]{1,0:T(8,128)}) custom-call(s32[2]{0:T(128)} %pad_add_fusion.10.s_ref, bf16[512,2048]{1,0:T(8,128)(2,1)} %bitcast.120, bf16[512,2048]{1,0:T(8,128)(2,1)} %collective-permute-done.xb_ref.x_ref, f32[1,2048]{1,0:T(1,128)} %bitcast.132, ...), custom_call_target="tpu_custom_call" | custom-call | flops 5200000000 | tf_op jit(solution)/shard_map/project_q/pallas_call | solution.py:127
  95.0 20.2 %flash_fwd.4 = (f32[1024,1024]{1,0:T(8,128)}, f32[1024,512]{1,0:T(8,128)}) custom-call(s32[18]{0:T(128)} %concatenate.27.s_ref, bf16[1024,1024]{1,0:T(8,128)(2,1)} %get-tuple-element.92.q_ref, s32[1024,128]{1,0:T(8,128)} %broadcast_in_dim.29.st_ref, bf16[512,1024]{1,0:T(8,128)(2,1)} %get-tuple-element.93.rest_0_.rest_6_, ...), custom_call_target="tpu_custom_call" | custom-call | flops 8800000000 | tf_op jit(solution)/shard_map/flash_fwd/pallas_call | solution.py:238
  115.2 14.9 %flash_fwd.5 = (f32[1024,1024]{1,0:T(8,128)}, f32[1024,512]{1,0:T(8,128)}) custom-call(s32[18]{0:T(128)} %concatenate.26.s_ref, bf16[1024,1024]{1,0:T(8,128)(2,1)} %get-tuple-element.92.q_ref, s32[1024,128]{1,0:T(8,128)} %broadcast_in_dim.29.st_ref, bf16[512,1024]{1,0:T(8,128)(2,1)} %copy-done.31, bf16[512,1024]{1,0:T(8,128)(2,1)} %collective-permute-done.3.rest_1_.rest_9_, ...), custom_call_target="tpu_custom_call" | custom-call | flops 8800000000 | tf_op jit(solution)/shard_map/flash_fwd/pallas_call | solution.py:238
  134.2 9.2 %flash_fwd.6 = (bf16[512,1024]{1,0:T(8,128)(2,1)}, f32[512,512]{1,0:T(8,128)}) custom-call(s32[10]{0:T(128)} %concatenate.25.s_ref, bf16[1024,1024]{1,0:T(8,128)(2,1)} %get-tuple-element.92.q_ref, s32[1024,128]{1,0:T(8,128)} %broadcast_in_dim.29.st_ref, bf16[512,1024]{1,0:T(8,128)(2,1)} %copy-done.32, bf16[512,1024]{1,0:T(8,128)(2,1)} %copy-done.33, ...), custom_call_target="tpu_custom_call" | custom-call | flops 4800000000 | tf_op jit(solution)/shard_map/flash_fwd/pallas_call | solution.py:238
  149.9 9.3 %flash_fwd.7 = (bf16[512,1024]{1,0:T(8,128)(2,1)}, f32[512,512]{1,0:T(8,128)}) custom-call(s32[10]{0:T(128)} %concatenate.30.s_ref, bf16[1024,1024]{1,0:T(8,128)(2,1)} %get-tuple-element.92.q_ref, s32[1024,128]{1,0:T(8,128)} %broadcast_in_dim.29.st_ref, bf16[512,1024]{1,0:T(8,128)(2,1)} %copy-done.32, bf16[512,1024]{1,0:T(8,128)(2,1)} %copy-done.33, ...), custom_call_target="tpu_custom_call" | custom-call | flops 4800000000 | tf_op jit(solution)/shard_map/flash_fwd/pallas_call | solution.py:238
  159.2 4.9 convolution_convert_fusion.2.refs_1_
  169.7 26.1 %collective-permute-done.5.refs_2_ = bf16[512,2048]{1,0:T(8,128)(2,1)} collective-permute-done((bf16[512,2048]{1,0:T(8,128)(2,1)S(1)}, bf16[512,2048]{1,0:T(8,128)(2,1)}, u32[]{:S(2)}, u32[]{:S(2)}) %collective-permute-start.5) | collective-permute-done | bytes 2097184 | tf_op jit(solution)/shard_map/ppermute | solution.py:902
  195.8 48.0 %mlp.2 = (bf16[512,2048]{1,0:T(8,128)(2,1)}, bf16[512,3072]{1,0:T(8,128)(2,1)}, bf16[512,3072]{1,0:T(8,128)(2,1)}, bf16[512,3072]{1,0:T(8,128)(2,1)}, bf16[512,2048]{1,0:T(8,128)(2,1)}) custom-call(bf16[1024,2048]{1,0:T(8,128)(2,1)} %get-tuple-element.91.refs_0_.refs_6_, bf16[512,2048]{1,0:T(8,128)(2,1)} %copy-done.4, ...), custom_call_target="tpu_custom_call" | custom-call | flops 18800001024 | tf_op jit(solution)/shard_map/mlp/pallas_call | solution.py:428
  246.8 48.3 %mlp.3 = (bf16[512,2048]{1,0:T(8,128)(2,1)}, bf16[512,3072]{1,0:T(8,128)(2,1)}, bf16[512,3072]{1,0:T(8,128)(2,1)}, bf16[512,3072]{1,0:T(8,128)(2,1)}, bf16[512,2048]{1,0:T(8,128)(2,1)}) custom-call(bf16[1024,2048]{1,0:T(8,128)(2,1)} %get-tuple-element.91.refs_0_.refs_6_, bf16[512,2048]{1,0:T(8,128)(2,1)} %convolution_convert_fusion.2.refs_1_, ...), custom_call_target="tpu_custom_call" | custom-call | flops 18800001024 | tf_op jit(solution)/shard_map/mlp/pallas_call | solution.py:428
  295.6 17.2 %wgrad_send.6.refs_4_ = bf16[2,4,3072,128]{3,2,1,0:T(8,128)(2,1)} custom-call(bf16[512,3072]{1,0:T(8,128)(2,1)} %get-tuple-element.101.refs_0_, bf16[1024,2048]{1,0:T(8,128)(2,1)} %pad_maximum_fusion.refs_4_.refs_6_.refs_1_.refs_3_, bf16[512,3072]{1,0:T(8,128)(2,1)} %get-tuple-element.110.refs_2_, ...), custom_call_target="tpu_custom_call" | custom-call | flops 6469357056 | tf_op jit(solution)/shard_map/wgrad_send/pallas_call | solution.py:802
  312.8 9.6 %wgrad.12 = bf16[1,4,3072,128]{3,2,1,0:T(8,128)(2,1)} custom-call(s32[5]{0:T(128)} %get-tuple-element.189.s_ref, bf16[512,3072]{1,0:T(8,128)(2,1)} %get-tuple-element.101.refs_0_, bf16[1024,2048]{1,0:T(8,128)(2,1)} %pad_maximum_fusion.refs_4_.refs_6_.refs_1_.refs_3_, bf16[512,3072]{1,0:T(8,128)(2,1)} %get-tuple-element.110.refs_2_, ...), custom_call_target="tpu_custom_call" | custom-call | flops 4265470464 | tf_op jit(solution)/shard_map/wgrad/pallas_call | solution.py:698
  324.6 17.7 %wgrad_send.7.refs_4_ = bf16[2,4,128,3072]{3,2,1,0:T(8,128)(2,1)} custom-call(bf16[512,2048]{1,0:T(8,128)(2,1)} %get-tuple-element.126.refs_0_, bf16[512,3072]{1,0:T(8,128)(2,1)} %get-tuple-element.112.refs_1_, bf16[512,2048]{1,0:T(8,128)(2,1)} %get-tuple-element.113.refs_2_, bf16[512,3072]{1,0:T(8,128)(2,1)} %get-tuple-element.114.refs_3_), custom_call_target="tpu_custom_call" | custom-call | flops 6469357056 | tf_op jit(solution)/shard_map/wgrad_send/pallas_call | solution.py:802
  342.3 11.3 %mid_backward.2 = (bf16[512,2048]{1,0:T(8,128)(2,1)}, bf16[512,1024]{1,0:T(8,128)(2,1)}, f32[8,2048]{1,0:T(8,128)}) custom-call(bf16[1024,2048]{1,0:T(8,128)(2,1)} %get-tuple-element.91.refs_0_.refs_6_, bf16[512,2048]{1,0:T(8,128)(2,1)} %copy-done.4, bf16[512,2048]{1,0:T(8,128)(2,1)} %collective-permute-done.5.refs_2_, ...), custom_call_target="tpu_custom_call" | custom-call | flops 4400000000 | tf_op jit(solution)/shard_map/mid_backward/pallas_call | solution.py:488
  353.6 11.5 %mid_backward.3 = (bf16[512,2048]{1,0:T(8,128)(2,1)}, bf16[512,1024]{1,0:T(8,128)(2,1)}, f32[8,2048]{1,0:T(8,128)}) custom-call(bf16[1024,2048]{1,0:T(8,128)(2,1)} %get-tuple-element.91.refs_0_.refs_6_, bf16[512,2048]{1,0:T(8,128)(2,1)} %convolution_convert_fusion.2.refs_1_, bf16[512,2048]{1,0:T(8,128)(2,1)} %copy-done.6, ...), custom_call_target="tpu_custom_call" | custom-call | flops 4400000000 | tf_op jit(solution)/shard_map/mid_backward/pallas_call | solution.py:488
  365.6 18.9 %flash_bwd.2 = (f32[1024,512]{1,0:T(8,128)}, bf16[1024,512]{1,0:T(8,128)(2,1)}, bf16[1024,512]{1,0:T(8,128)(2,1)}, bf16[1024,512]{1,0:T(8,128)(2,1)}) custom-call(s32[22]{0:T(128)} %concatenate.29.s_ref, bf16[1024,1024]{1,0:T(8,128)(2,1)} %get-tuple-element.92.q_ref, s32[8,1024]{1,0:T(8,128)} %broadcast_in_dim.32.st_ref, ...), custom_call_target="tpu_custom_call" | custom-call | flops 16000000000 | tf_op jit(solution)/shard_map/flash_bwd/pallas_call | solution.py:344
  384.6 8.2 %collective-permute-done.10.refs_5_ = bf16[1,4,3072,128]{3,2,1,0:T(8,128)(2,1)S(1)} collective-permute-done((bf16[1,4,3072,128]{3,2,1,0:T(8,128)(2,1)}, bf16[1,4,3072,128]{3,2,1,0:T(8,128)(2,1)S(1)}, u32[]{:S(2)}, u32[]{:S(2)}) %collective-permute-start.10) | collective-permute-done | bytes 3145760 | tf_op jit(solution)/shard_map/ppermute | solution.py:841
  394.5 10.3 %wgrad.14 = bf16[1,4,3072,128]{3,2,1,0:T(8,128)(2,1)} custom-call(s32[5]{0:T(128)} %get-tuple-element.122.s_ref, bf16[512,3072]{1,0:T(8,128)(2,1)} %get-tuple-element.101.refs_0_, bf16[1024,2048]{1,0:T(8,128)(2,1)} %pad_maximum_fusion.refs_4_.refs_6_.refs_1_.refs_3_, bf16[512,3072]{1,0:T(8,128)(2,1)} %get-tuple-element.110.refs_2_, ...), custom_call_target="tpu_custom_call" | custom-call | flops 4265470464 | tf_op jit(solution)/shard_map/wgrad/pallas_call | solution.py:698
  406.0 10.4 %wgrad.13 = bf16[1,4,128,3072]{3,2,1,0:T(8,128)(2,1)} custom-call(s32[5]{0:T(128)} %pad.22.s_ref, bf16[512,2048]{1,0:T(8,128)(2,1)} %get-tuple-element.126.refs_0_, bf16[512,3072]{1,0:T(8,128)(2,1)} %get-tuple-element.112.refs_1_, bf16[512,2048]{1,0:T(8,128)(2,1)} %get-tuple-element.113.refs_2_, bf16[512,3072]{1,0:T(8,128)(2,1)} %get-tuple-element.114.refs_3_, ...), custom_call_target="tpu_custom_call" | custom-call | flops 4265470464 | tf_op jit(solution)/shard_map/wgrad/pallas_call | solution.py:698
  419.9 18.9 %flash_bwd.3 = (f32[1024,512]{1,0:T(8,128)}, bf16[1024,512]{1,0:T(8,128)(2,1)}, bf16[1024,512]{1,0:T(8,128)(2,1)}, bf16[1024,512]{1,0:T(8,128)(2,1)}) custom-call(s32[22]{0:T(128)} %concatenate.29.s_ref, bf16[1024,1024]{1,0:T(8,128)(2,1)} %get-tuple-element.92.q_ref, s32[8,1024]{1,0:T(8,128)} %broadcast_in_dim.32.st_ref, ...), custom_call_target="tpu_custom_call" | custom-call | flops 16000000000 | tf_op jit(solution)/shard_map/flash_bwd/pallas_call | solution.py:344
  440.1 17.7 %wgrad_send.8.refs_4_ = bf16[2,4,128,3072]{3,2,1,0:T(8,128)(2,1)} custom-call(bf16[512,2048]{1,0:T(8,128)(2,1)} %get-tuple-element.126.refs_0_, bf16[512,3072]{1,0:T(8,128)(2,1)} %get-tuple-element.127.refs_1_, bf16[512,2048]{1,0:T(8,128)(2,1)} %get-tuple-element.113.refs_2_, bf16[512,3072]{1,0:T(8,128)(2,1)} %get-tuple-element.128.refs_3_), custom_call_target="tpu_custom_call" | custom-call | flops 6469357056 | tf_op jit(solution)/shard_map/wgrad_send/pallas_call | solution.py:802
  457.9 28.0 %collective-permute-done.13 = bf16[1024,512]{1,0:T(8,128)(2,1)S(1)} collective-permute-done((bf16[1024,512]{1,0:T(8,128)(2,1)S(1)}, bf16[1024,512]{1,0:T(8,128)(2,1)S(1)}, u32[]{:S(2)}, u32[]{:S(2)}) %collective-permute-start.13) | collective-permute-done | bytes 1048608 | tf_op jit(solution)/shard_map/ppermute | solution.py:1027
  487.4 33.4 %collective-permute-done.15 = bf16[1024,512]{1,0:T(8,128)(2,1)} collective-permute-done((bf16[1024,512]{1,0:T(8,128)(2,1)}, bf16[1024,512]{1,0:T(8,128)(2,1)}, u32[]{:S(2)}, u32[]{:S(2)}) %collective-permute-start.15) | collective-permute-done | bytes 1048608 | tf_op jit(solution)/shard_map/ppermute | solution.py:1027
  526.2 10.7 %wgrad.15 = bf16[1,4,128,3072]{3,2,1,0:T(8,128)(2,1)} custom-call(s32[5]{0:T(128)} %pad.18.s_ref, bf16[512,2048]{1,0:T(8,128)(2,1)} %get-tuple-element.126.refs_0_, bf16[512,3072]{1,0:T(8,128)(2,1)} %get-tuple-element.112.refs_1_, bf16[512,2048]{1,0:T(8,128)(2,1)} %get-tuple-element.113.refs_2_, bf16[512,3072]{1,0:T(8,128)(2,1)} %get-tuple-element.114.refs_3_, ...), custom_call_target="tpu_custom_call" | custom-call | flops 4265470464 | tf_op jit(solution)/shard_map/wgrad/pallas_call | solution.py:698
  537.0 10.4 %wgrad.16 = bf16[1,4,128,3072]{3,2,1,0:T(8,128)(2,1)} custom-call(s32[5]{0:T(128)} %pad.22.s_ref, bf16[512,2048]{1,0:T(8,128)(2,1)} %get-tuple-element.126.refs_0_, bf16[512,3072]{1,0:T(8,128)(2,1)} %get-tuple-element.127.refs_1_, bf16[512,2048]{1,0:T(8,128)(2,1)} %get-tuple-element.113.refs_2_, bf16[512,3072]{1,0:T(8,128)(2,1)} %get-tuple-element.128.refs_3_, ...), custom_call_target="tpu_custom_call" | custom-call | flops 4265470464 | tf_op jit(solution)/shard_map/wgrad/pallas_call | solution.py:698
  547.4 8.3 %q_back.1 = (bf16[1024,1024]{1,0:T(8,128)(2,1)}, f32[8,128]{1,0:T(8,128)}) custom-call(f32[1024,512]{1,0:T(8,128)} %get-tuple-element.119.refs_0_, f32[1024,512]{1,0:T(8,128)} %get-tuple-element.124.refs_1_, f32[1024,1024]{1,0:T(8,128)} %get-tuple-element.125.refs_2_, f32[1024,128]{1,0:T(8,128)} %copy.43.cos_ref.refs_3_.refs_7_, ...), custom_call_target="tpu_custom_call" | custom-call | flops 3400000000 | tf_op jit(solution)/shard_map/q_back/pallas_call | solution.py:540
  556.6 10.1 %convolution_convert_fusion.1 = bf16[512,2048]{1,0:T(8,128)(2,1)S(1)} fusion(bf16[512,3072]{1,0:T(8,128)(2,1)S(1)} %copy-done.2, bf16[3072,2048]{1,0:T(8,128)(2,1)} %refs_7_.6), kind=kOutput, calls=%fused_computation.3 | convolution fusion | flops 6443499520 | bytes 17825792 | tf_op jit(solution)/shard_map/dot_general | solution.py:33
  568.1 8.2 %broadcast_select_fusion = (bf16[512,2048]{1,0:T(8,128)(2,1)}, bf16[512,2048]{1,0:T(8,128)(2,1)}) fusion(bf16[512,2048]{1,0:T(8,128)(2,1)S(1)} %convolution_convert_fusion.1, pred[]{:T(512)S(6)} %eq.2, bf16[512,3072]{1,0:T(8,128)(2,1)S(1)} %copy-done.3, bf16[3072,2048]{1,0:T(8,128)(2,1)S(1)} %bitcast.136), kind=kOutput, calls=%fused_computation.9 | convolution fusion | flops 6444548096 | bytes 22020096 | tf_op jit(solution)/shard_map/dot_general | solution.py:33
  576.3 7.6 wgrad_send.9.refs_4_
  583.9 4.7 wgrad.17
  588.6 8.2 %wgrad_send.10.refs_4_ = bf16[2,4,128,1024]{3,2,1,0:T(8,128)(2,1)} custom-call(bf16[1024,2048]{1,0:T(8,128)(2,1)} %get-tuple-element.144.refs_0_.refs_2_, bf16[1024,1024]{1,0:T(8,128)(2,1)} %get-tuple-element.132.refs_1_.refs_3_.refs_5_, bf16[1024,2048]{1,0:T(8,128)(2,1)} %get-tuple-element.144.refs_0_.refs_2_, ...), custom_call_target="tpu_custom_call" | custom-call | flops 2689785600 | tf_op jit(solution)/shard_map/wgrad_send/pallas_call | solution.py:802
  598.4 5.3 wgrad.18
  607.3 12.8 %in_back.3 = (bf16[512,1024]{1,0:T(8,128)(2,1)}, bf16[512,2048]{1,0:T(8,128)(2,1)}, f32[8,128]{1,0:T(8,128)}, f32[8,2048]{1,0:T(8,128)}) custom-call(s32[1]{0:T(128)} %bitcast.2.s_ref, bf16[1024,512]{1,0:T(8,128)(2,1)} %get-tuple-element.134.refs_0_, bf16[1024,512]{1,0:T(8,128)(2,1)} %copy-done.10, bf16[1024,512]{1,0:T(8,128)(2,1)} %get-tuple-element.137.refs_2_, ...), custom_call_target="tpu_custom_call" | custom-call | flops 5000000000 | tf_op jit(solution)/shard_map/in_back/pallas_call | solution.py:590
  620.1 12.5 %in_back.2 = (bf16[512,1024]{1,0:T(8,128)(2,1)}, bf16[512,2048]{1,0:T(8,128)(2,1)}, f32[8,128]{1,0:T(8,128)}, f32[8,2048]{1,0:T(8,128)}) custom-call(s32[1]{0:T(128)} %bitcast.1.s_ref, bf16[1024,512]{1,0:T(8,128)(2,1)} %get-tuple-element.134.refs_0_, bf16[1024,512]{1,0:T(8,128)(2,1)} %copy-done.10, bf16[1024,512]{1,0:T(8,128)(2,1)} %get-tuple-element.137.refs_2_, ...), custom_call_target="tpu_custom_call" | custom-call | flops 5000000000 | tf_op jit(solution)/shard_map/in_back/pallas_call | solution.py:590
  634.3 8.3 %wgrad_send.11.refs_4_ = bf16[2,4,128,1024]{3,2,1,0:T(8,128)(2,1)} custom-call(bf16[1024,2048]{1,0:T(8,128)(2,1)} %get-tuple-element.144.refs_0_.refs_2_, bf16[512,1024]{1,0:T(8,128)(2,1)} %get-tuple-element.150.refs_1_, bf16[1024,2048]{1,0:T(8,128)(2,1)} %get-tuple-element.144.refs_0_.refs_2_, bf16[512,1024]{1,0:T(8,128)(2,1)} %get-tuple-element.151.refs_3_), custom_call_target="tpu_custom_call" | custom-call | flops 2689785600 | tf_op jit(solution)/shard_map/wgrad_send/pallas_call | solution.py:802
  645.0 5.1 wgrad.19
  650.1 10.9 %wgrad.20 = bf16[1,4,128,3072]{3,2,1,0:T(8,128)(2,1)} custom-call(s32[5]{0:T(128)} %pad.18.s_ref, bf16[512,2048]{1,0:T(8,128)(2,1)} %get-tuple-element.126.refs_0_, bf16[512,3072]{1,0:T(8,128)(2,1)} %get-tuple-element.127.refs_1_, bf16[512,2048]{1,0:T(8,128)(2,1)} %get-tuple-element.113.refs_2_, bf16[512,3072]{1,0:T(8,128)(2,1)} %get-tuple-element.128.refs_3_, ...), custom_call_target="tpu_custom_call" | custom-call | flops 4265470464 | tf_op jit(solution)/shard_map/wgrad/pallas_call | solution.py:698
  674.9 8.7 %fusion = bf16[1,512,2048]{2,1,0:T(8,128)(2,1)} fusion(bf16[512,2048]{1,0:T(8,128)(2,1)} %collective-permute-done.12, bf16[512,2048]{1,0:T(8,128)(2,1)} %collective-permute-done.5.refs_2_, bf16[512,2048]{1,0:T(8,128)(2,1)} %copy-done.6, bf16[512,2048]{1,0:T(8,128)(2,1)S(1)} %copy-done.5, bf16[512,2048]{1,0:T(8,128)(2,1)} %convolution_convert_fusion.2.refs_1_, ...), kind=kLoop, calls=%fused_computation.6 | loop fusion | flops 13631488 | bytes 18874368 | tf_op jit(solution)/shard_map/broadcast_in_dim | solution.py:1091
  688.5 28.8 %collective-permute-done.32 = f32[4352]{0:T(1024)S(1)} collective-permute-done((f32[4352]{0:T(1024)S(1)}, f32[4352]{0:T(1024)S(1)}, u32[]{:S(2)}, u32[]{:S(2)}) %collective-permute-start.32) | collective-permute-done | bytes 17440 | tf_op jit(solution)/shard_map/ppermute | solution.py:1101
  721.6 7.9 final.1
  729.4 5.0 wgrad.21
  736.9 5.4 wgrad.22
  746.2 5.4 wgrad.23
  758.3 11.7 %collective-permute-done.21 = bf16[2,128,1024]{2,1,0:T(8,128)(2,1)S(1)} collective-permute-done((bf16[2,128,1024]{2,1,0:T(8,128)(2,1)S(1)}, bf16[2,128,1024]{2,1,0:T(8,128)(2,1)S(1)}, u32[]{:S(2)}, u32[]{:S(2)}) %collective-permute-start.21) | collective-permute-done | bytes 524320 | tf_op jit(solution)/shard_map/ppermute | solution.py:858
  771.0 7.6 collective-permute-done.24
  780.8 12.9 %collective-permute-done.22 = bf16[128,1024]{1,0:T(8,128)(2,1)S(1)} collective-permute-done((bf16[128,1024]{1,0:T(8,128)(2,1)S(1)}, bf16[128,1024]{1,0:T(8,128)(2,1)S(1)}, u32[]{:S(2)}, u32[]{:S(2)}) %collective-permute-start.22) | collective-permute-done | bytes 262176 | tf_op jit(solution)/shard_map/ppermute | solution.py:860
  (226 shorter events, 125.6 us)
Async XLA Ops:
  7.2 596.5 %reduce-scatter.4.cloned.1.call-start = ((), (), s32[]{:S(2)}) async-start(), calls=%async_computation.3 | async-start | bytes 3932160 | tf_op jit(solution)/shard_map/reduce_scatter | solution.py:849
  7.2 49.0 %collective-permute-start = (bf16[512,2048]{1,0:T(8,128)(2,1)}, bf16[512,2048]{1,0:T(8,128)(2,1)}, u32[]{:S(2)}, u32[]{:S(2)}) collective-permute-start(bf16[512,2048]{1,0:T(8,128)(2,1)} %bitcast.118), channel_id=1, source_target_pairs={{0,1},{1,0},{2,3},{3,2},{4,5},{5,4},{6,7},{7,6},{8,9},{9,8},{10,11... | collective-permute-start | bytes 6291464 | tf_op jit(solution)/shard_map/ppermute | solution.py:902
  21.9 48.0 %collective-permute-start.1 = (bf16[512,1024]{1,0:T(8,128)(2,1)}, bf16[512,1024]{1,0:T(8,128)(2,1)S(1)}, u32[]{:S(2)}, u32[]{:S(2)}) collective-permute-start(bf16[512,1024]{1,0:T(8,128)(2,1)} %get-tuple-element.93.rest_0_.rest_6_), channel_id=1, source_target_pairs={{0,2},{2,4},{4,6},{1,3},{3,5},{5,7},{8,10},{10,12},{12,14},{9,11},... | collective-permute-start | bytes 3145736 | tf_op jit(solution)/shard_map/ppermute | solution.py:953
  62.8 27.6 %collective-permute-start.3 = (bf16[512,1024]{1,0:T(8,128)(2,1)}, bf16[512,1024]{1,0:T(8,128)(2,1)}, u32[]{:S(2)}, u32[]{:S(2)}) collective-permute-start(bf16[512,1024]{1,0:T(8,128)(2,1)} %get-tuple-element.94.rest_1_.rest_7_), channel_id=1, source_target_pairs={{0,2},{2,4},{4,6},{1,3},{3,5},{5,7},{8,10},{10,12},{12,14},{9,11},... | collective-permute-start | bytes 3145736 | tf_op jit(solution)/shard_map/ppermute | solution.py:953
  69.9 17.3 %copy-start.31 = (bf16[512,1024]{1,0:T(8,128)(2,1)}, bf16[512,1024]{1,0:T(8,128)(2,1)S(1)}, u32[]{:S(2)}) copy-start(bf16[512,1024]{1,0:T(8,128)(2,1)S(1)} %collective-permute-done.1.rest_0_.rest_8_) | copy-start | bytes 3145732
  69.9 60.1 %collective-permute-start.2 = (bf16[512,1024]{1,0:T(8,128)(2,1)S(1)}, bf16[512,1024]{1,0:T(8,128)(2,1)S(1)}, u32[]{:S(2)}, u32[]{:S(2)}) collective-permute-start(bf16[512,1024]{1,0:T(8,128)(2,1)S(1)} %collective-permute-done.1.rest_0_.rest_8_), channel_id=1, source_target_pairs={{0,2},{2,4},{4,6},{1,3},{3,5},{5,7},{8,10},{10,12},{12,14},{9,11},... | collective-permute-start | bytes 3145736 | tf_op jit(solution)/shard_map/ppermute | solution.py:953
  72.5 92.1 %collective-permute-start.6 = (bf16[512,2048]{1,0:T(8,128)(2,1)}, bf16[512,2048]{1,0:T(8,128)(2,1)}, u32[]{:S(2)}, u32[]{:S(2)}) collective-permute-start(bf16[512,2048]{1,0:T(8,128)(2,1)} %bitcast.3), channel_id=1, source_target_pairs={{0,1},{1,0},{2,3},{3,2},{4,5},{5,4},{6,7},{7,6},{8,9},{9,8},{10,11... | collective-permute-start | bytes 6291464 | tf_op jit(solution)/shard_map/ppermute | solution.py:902
  90.4 42.9 %collective-permute-start.4 = (bf16[512,1024]{1,0:T(8,128)(2,1)}, bf16[512,1024]{1,0:T(8,128)(2,1)S(1)}, u32[]{:S(2)}, u32[]{:S(2)}) collective-permute-start(bf16[512,1024]{1,0:T(8,128)(2,1)} %collective-permute-done.3.rest_1_.rest_9_), channel_id=1, source_target_pairs={{0,2},{2,4},{4,6},{1,3},{3,5},{5,7},{8,10},{10,12},{12,14},{9,11},... | collective-permute-start | bytes 3145736 | tf_op jit(solution)/shard_map/ppermute | solution.py:953
  147.1 48.7 %collective-permute-start.5 = (bf16[512,2048]{1,0:T(8,128)(2,1)S(1)}, bf16[512,2048]{1,0:T(8,128)(2,1)}, u32[]{:S(2)}, u32[]{:S(2)}) collective-permute-start(bf16[512,2048]{1,0:T(8,128)(2,1)S(1)} %convolution_convert_fusion.3.refs_1_), channel_id=1, source_target_pairs={{0,1},{1,0},{2,3},{3,2},{4,5},{5,4},{6,7},{7,6},{8,9},{9,8},{10,11... | collective-permute-start | bytes 6291464 | tf_op jit(solution)/shard_map/ppermute | solution.py:902
  164.1 81.4 %collective-permute-start.8 = (bf16[512,2048]{1,0:T(8,128)(2,1)}, bf16[512,2048]{1,0:T(8,128)(2,1)S(1)}, u32[]{:S(2)}, u32[]{:S(2)}) collective-permute-start(bf16[512,2048]{1,0:T(8,128)(2,1)} %convolution_convert_fusion.2.refs_1_), channel_id=1, source_target_pairs={{0,1},{1,0},{2,3},{3,2},{4,5},{5,4},{6,7},{7,6},{8,9},{9,8},{10,11... | collective-permute-start | bytes 6291464 | tf_op jit(solution)/shard_map/ppermute | solution.py:902
  243.8 98.4 %collective-permute-start.7 = (bf16[512,2048]{1,0:T(8,128)(2,1)}, bf16[512,2048]{1,0:T(8,128)(2,1)}, u32[]{:S(2)}, u32[]{:S(2)}) collective-permute-start(bf16[512,2048]{1,0:T(8,128)(2,1)} %get-tuple-element.102.refs_3_), channel_id=1, source_target_pairs={{0,1},{1,0},{2,3},{3,2},{4,5},{5,4},{6,7},{7,6},{8,9},{9,8},{10,11... | collective-permute-start | bytes 6291464 | tf_op jit(solution)/shard_map/ppermute | solution.py:902
  295.1 58.5 %collective-permute-start.9 = (bf16[512,2048]{1,0:T(8,128)(2,1)}, bf16[512,2048]{1,0:T(8,128)(2,1)}, u32[]{:S(2)}, u32[]{:S(2)}) collective-permute-start(bf16[512,2048]{1,0:T(8,128)(2,1)} %get-tuple-element.108.refs_3_), channel_id=1, source_target_pairs={{0,1},{1,0},{2,3},{3,2},{4,5},{5,4},{6,7},{7,6},{8,9},{9,8},{10,11... | collective-permute-start | bytes 6291464 | tf_op jit(solution)/shard_map/ppermute | solution.py:902
  322.4 70.4 %collective-permute-start.10 = (bf16[1,4,3072,128]{3,2,1,0:T(8,128)(2,1)}, bf16[1,4,3072,128]{3,2,1,0:T(8,128)(2,1)S(1)}, u32[]{:S(2)}, u32[]{:S(2)}) collective-permute-start(bf16[1,4,3072,128]{3,2,1,0:T(8,128)(2,1)} %wgrad.12), channel_id=1, source_target_pairs={{0,16},{8,24},{16,0},{24,8},{1,17},{9,25},{17,1},{25,9},{2,18},{10... | collective-permute-start | bytes 9437192 | tf_op jit(solution)/shard_map/ppermute | solution.py:841
  404.8 237.9 %reduce-scatter.6.cloned.1.call-start = ((), (), s32[]{:S(2)}) async-start(), calls=%async_computation.4 | async-start | bytes 3932160 | tf_op jit(solution)/shard_map/reduce_scatter | solution.py:849
  406.0 13.8 %copy-start.26 = (f32[8,2048]{1,0:T(8,128)S(1)}, f32[8,2048]{1,0:T(8,128)}, u32[]{:S(2)}) copy-start(f32[8,2048]{1,0:T(8,128)} %get-tuple-element.162) | copy-start | bytes 196612
  406.0 13.8 %copy-start.27 = (f32[8,2048]{1,0:T(8,128)S(1)}, f32[8,2048]{1,0:T(8,128)}, u32[]{:S(2)}) copy-start(f32[8,2048]{1,0:T(8,128)} %get-tuple-element.163) | copy-start | bytes 196612
  416.4 108.2 %collective-permute-start.11 = (bf16[1,4,128,3072]{3,2,1,0:T(8,128)(2,1)}, bf16[1,4,128,3072]{3,2,1,0:T(8,128)(2,1)S(1)}, u32[]{:S(2)}, u32[]{:S(2)}) collective-permute-start(bf16[1,4,128,3072]{3,2,1,0:T(8,128)(2,1)} %wgrad.13), channel_id=1, source_target_pairs={{0,16},{8,24},{16,0},{24,8},{1,17},{9,25},{17,1},{25,9},{2,18},{10... | collective-permute-start | bytes 9437192 | tf_op jit(solution)/shard_map/ppermute | solution.py:841
  418.5 67.3 %collective-permute-start.13 = (bf16[1024,512]{1,0:T(8,128)(2,1)S(1)}, bf16[1024,512]{1,0:T(8,128)(2,1)S(1)}, u32[]{:S(2)}, u32[]{:S(2)}) collective-permute-start(bf16[1024,512]{1,0:T(8,128)(2,1)S(1)} %copy-done.34), channel_id=1, source_target_pairs={{2,0},{4,2},{6,4},{3,1},{5,3},{7,5},{10,8},{12,10},{14,12},{11,9},... | collective-permute-start | bytes 3145736 | tf_op jit(solution)/shard_map/ppermute | solution.py:1027
  438.8 82.0 %collective-permute-start.15 = (bf16[1024,512]{1,0:T(8,128)(2,1)}, bf16[1024,512]{1,0:T(8,128)(2,1)}, u32[]{:S(2)}, u32[]{:S(2)}) collective-permute-start(bf16[1024,512]{1,0:T(8,128)(2,1)} %get-tuple-element.139), channel_id=1, source_target_pairs={{2,0},{4,2},{6,4},{3,1},{5,3},{7,5},{10,8},{12,10},{14,12},{11,9},... | collective-permute-start | bytes 3145736 | tf_op jit(solution)/shard_map/ppermute | solution.py:1027
  440.1 45.7 %copy-start.18 = (bf16[1024,512]{1,0:T(8,128)(2,1)S(1)}, bf16[1024,512]{1,0:T(8,128)(2,1)}, u32[]{:S(2)}) copy-start(bf16[1024,512]{1,0:T(8,128)(2,1)} %get-tuple-element.135) | copy-start | bytes 3145732
  457.9 62.9 %copy-start.21 = (bf16[1024,512]{1,0:T(8,128)(2,1)S(1)}, bf16[1024,512]{1,0:T(8,128)(2,1)}, u32[]{:S(2)}) copy-start(bf16[1024,512]{1,0:T(8,128)(2,1)} %get-tuple-element.138) | copy-start | bytes 3145732
  486.1 119.8 %collective-permute-start.14 = (bf16[1024,512]{1,0:T(8,128)(2,1)S(1)}, bf16[1024,512]{1,0:T(8,128)(2,1)S(1)}, u32[]{:S(2)}, u32[]{:S(2)}) collective-permute-start(bf16[1024,512]{1,0:T(8,128)(2,1)S(1)} %add_convert_fusion.2), channel_id=1, source_target_pairs={{2,0},{4,2},{6,4},{3,1},{5,3},{7,5},{10,8},{12,10},{14,12},{11,9},... | collective-permute-start | bytes 3145736 | tf_op jit(solution)/shard_map/ppermute | solution.py:1027
  523.3 82.7 %collective-permute-start.16 = (bf16[1024,512]{1,0:T(8,128)(2,1)}, bf16[1024,512]{1,0:T(8,128)(2,1)S(1)}, u32[]{:S(2)}, u32[]{:S(2)}) collective-permute-start(bf16[1024,512]{1,0:T(8,128)(2,1)} %add_convert_fusion.1), channel_id=1, source_target_pairs={{2,0},{4,2},{6,4},{3,1},{5,3},{7,5},{10,8},{12,10},{14,12},{11,9},... | collective-permute-start | bytes 3145736 | tf_op jit(solution)/shard_map/ppermute | solution.py:1027
  536.9 261.3 %reduce-scatter.8.cloned.1.call-start = ((), (), s32[]{:S(2)}) async-start(), calls=%async_computation.5 | async-start | bytes 3932160 | tf_op jit(solution)/shard_map/reduce_scatter | solution.py:849
  555.7 94.4 %collective-permute-start.18 = (bf16[1,4,128,3072]{3,2,1,0:T(8,128)(2,1)}, bf16[1,4,128,3072]{3,2,1,0:T(8,128)(2,1)}, u32[]{:S(2)}, u32[]{:S(2)}) collective-permute-start(bf16[1,4,128,3072]{3,2,1,0:T(8,128)(2,1)} %wgrad.16), channel_id=1, source_target_pairs={{0,16},{8,24},{16,0},{24,8},{1,17},{9,25},{17,1},{25,9},{2,18},{10... | collective-permute-start | bytes 9437192 | tf_op jit(solution)/shard_map/ppermute | solution.py:841
  596.8 78.1 %collective-permute-start.12 = (bf16[512,2048]{1,0:T(8,128)(2,1)}, bf16[512,2048]{1,0:T(8,128)(2,1)}, u32[]{:S(2)}, u32[]{:S(2)}) collective-permute-start(bf16[512,2048]{1,0:T(8,128)(2,1)} %get-tuple-element.196), channel_id=1, source_target_pairs={{0,1},{1,0},{2,3},{3,2},{4,5},{5,4},{6,7},{7,6},{8,9},{9,8},{10,11... | collective-permute-start | bytes 6291464 | tf_op jit(solution)/shard_map/ppermute | solution.py:902
  620.1 12.6 %copy-start.30 = (f32[8,128]{1,0:T(8,128)S(1)}, f32[8,128]{1,0:T(8,128)}, u32[]{:S(2)}) copy-start(f32[8,128]{1,0:T(8,128)} %get-tuple-element.165) | copy-start | bytes 12292
  620.1 13.3 %copy-start.28 = (f32[8,2048]{1,0:T(8,128)S(1)}, f32[8,2048]{1,0:T(8,128)}, u32[]{:S(2)}) copy-start(f32[8,2048]{1,0:T(8,128)} %get-tuple-element.160) | copy-start | bytes 196612
  634.2 26.8 %collective-permute-start.28 = (f32[4352]{0:T(1024)S(1)}, f32[4352]{0:T(1024)S(1)}, u32[]{:S(2)}, u32[]{:S(2)}) collective-permute-start(f32[4352]{0:T(1024)S(1)} %pad_maximum_fusion.5), channel_id=1, source_target_pairs={{0,8},{8,0},{16,24},{24,16},{1,9},{9,1},{17,25},{25,17},{2,10},{10... | collective-permute-start | bytes 52232 | tf_op jit(solution)/shard_map/ppermute | solution.py:1101
  661.0 13.9 %copy-start.5 = (bf16[512,2048]{1,0:T(8,128)(2,1)S(1)}, bf16[512,2048]{1,0:T(8,128)(2,1)}, u32[]{:S(2)}) copy-start(bf16[512,2048]{1,0:T(8,128)(2,1)} %copy-done.4) | copy-start | bytes 6291460
  661.1 3.9 collective-permute-start.29
  665.0 6.3 collective-permute-start.30
  670.2 48.3 %collective-permute-start.19 = (bf16[1,4,1024,128]{3,2,1,0:T(8,128)(2,1)S(1)}, bf16[1,4,1024,128]{3,2,1,0:T(8,128)(2,1)S(1)}, u32[]{:S(2)}, u32[]{:S(2)}) collective-permute-start(bf16[1,4,1024,128]{3,2,1,0:T(8,128)(2,1)S(1)} %copy-done.17), channel_id=1, source_target_pairs={{0,16},{8,24},{16,0},{24,8},{1,17},{9,25},{17,1},{25,9},{2,18},{10... | collective-permute-start | bytes 3145736 | tf_op jit(solution)/shard_map/ppermute | solution.py:841
  670.3 49.9 %collective-permute-start.17 = (bf16[512,2048]{1,0:T(8,128)(2,1)}, bf16[512,2048]{1,0:T(8,128)(2,1)S(1)}, u32[]{:S(2)}, u32[]{:S(2)}) collective-permute-start(bf16[512,2048]{1,0:T(8,128)(2,1)} %get-tuple-element.149), channel_id=1, source_target_pairs={{0,1},{1,0},{2,3},{3,2},{4,5},{5,4},{6,7},{7,6},{8,9},{9,8},{10,11... | collective-permute-start | bytes 6291464 | tf_op jit(solution)/shard_map/ppermute | solution.py:902
  671.3 15.9 %copy-start.25 = (bf16[1,3072,128]{2,1,0:T(8,128)(2,1)S(1)}, bf16[1,3072,128]{2,1,0:T(8,128)(2,1)}, u32[]{:S(2)}) copy-start(bf16[1,3072,128]{2,1,0:T(8,128)(2,1)} %reduce-scatter.4.cloned.1.call-done) | copy-start | bytes 2359300
  671.3 13.7 %collective-permute-start.31 = (f32[4352]{0:T(1024)S(1)}, f32[4352]{0:T(1024)S(1)}, u32[]{:S(2)}, u32[]{:S(2)}) collective-permute-start(f32[4352]{0:T(1024)S(1)} %add.344), channel_id=1, source_target_pairs={{0,4},{2,6},{4,0},{6,2},{1,5},{3,7},{5,1},{7,3},{8,12},{10,14},{12... | collective-permute-start | bytes 52232 | tf_op jit(solution)/shard_map/ppermute | solution.py:1101
  683.6 34.8 %copy-start.22 = (bf16[1,4,128,1024]{3,2,1,0:T(8,128)(2,1)S(1)}, bf16[1,4,128,1024]{3,2,1,0:T(8,128)(2,1)}, u32[]{:S(2)}) copy-start(bf16[1,4,128,1024]{3,2,1,0:T(8,128)(2,1)} %wgrad.19) | copy-start | bytes 3145732
  683.6 52.3 %collective-permute-start.20 = (bf16[1,4,128,1024]{3,2,1,0:T(8,128)(2,1)S(1)}, bf16[1,4,128,1024]{3,2,1,0:T(8,128)(2,1)S(1)}, u32[]{:S(2)}, u32[]{:S(2)}) collective-permute-start(bf16[1,4,128,1024]{3,2,1,0:T(8,128)(2,1)S(1)} %copy-done.16), channel_id=1, source_target_pairs={{0,16},{8,24},{16,0},{24,8},{1,17},{9,25},{17,1},{25,9},{2,18},{10... | collective-permute-start | bytes 3145736 | tf_op jit(solution)/shard_map/ppermute | solution.py:841
  685.0 32.2 %collective-permute-start.32 = (f32[4352]{0:T(1024)S(1)}, f32[4352]{0:T(1024)S(1)}, u32[]{:S(2)}, u32[]{:S(2)}) collective-permute-start(f32[4352]{0:T(1024)S(1)} %add.345), channel_id=1, source_target_pairs={{0,1},{1,0},{2,3},{3,2},{4,5},{5,4},{6,7},{7,6},{8,9},{9,8},{10,11... | collective-permute-start | bytes 52232 | tf_op jit(solution)/shard_map/ppermute | solution.py:1101
  718.4 26.8 %collective-permute-start.23 = (bf16[1,4,128,1024]{3,2,1,0:T(8,128)(2,1)S(1)}, bf16[1,4,128,1024]{3,2,1,0:T(8,128)(2,1)S(1)}, u32[]{:S(2)}, u32[]{:S(2)}) collective-permute-start(bf16[1,4,128,1024]{3,2,1,0:T(8,128)(2,1)S(1)} %copy-done.22), channel_id=1, source_target_pairs={{0,16},{8,24},{16,0},{24,8},{1,17},{9,25},{17,1},{25,9},{2,18},{10... | collective-permute-start | bytes 3145736 | tf_op jit(solution)/shard_map/ppermute | solution.py:841
  735.5 19.0 %collective-permute-start.26 = (bf16[2,1024,128]{2,1,0:T(8,128)(2,1)S(1)}, bf16[2,1024,128]{2,1,0:T(8,128)(2,1)S(1)}, u32[]{:S(2)}, u32[]{:S(2)}) collective-permute-start(bf16[2,1024,128]{2,1,0:T(8,128)(2,1)S(1)} %pad_maximum_fusion.4), channel_id=1, source_target_pairs={{0,2},{2,0},{4,6},{6,4},{1,3},{3,1},{5,7},{7,5},{8,10},{10,8},{12,... | collective-permute-start | bytes 1572872 | tf_op jit(solution)/shard_map/ppermute | solution.py:858
  743.5 26.5 %collective-permute-start.21 = (bf16[2,128,1024]{2,1,0:T(8,128)(2,1)S(1)}, bf16[2,128,1024]{2,1,0:T(8,128)(2,1)S(1)}, u32[]{:S(2)}, u32[]{:S(2)}) collective-permute-start(bf16[2,128,1024]{2,1,0:T(8,128)(2,1)S(1)} %pad_maximum_fusion.2), channel_id=1, source_target_pairs={{0,2},{2,0},{4,6},{6,4},{1,3},{3,1},{5,7},{7,5},{8,10},{10,8},{12,... | collective-permute-start | bytes 1572872 | tf_op jit(solution)/shard_map/ppermute | solution.py:858
  752.8 25.8 %collective-permute-start.24 = (bf16[2,128,1024]{2,1,0:T(8,128)(2,1)S(1)}, bf16[2,128,1024]{2,1,0:T(8,128)(2,1)S(1)}, u32[]{:S(2)}, u32[]{:S(2)}) collective-permute-start(bf16[2,128,1024]{2,1,0:T(8,128)(2,1)S(1)} %pad_maximum_fusion.3), channel_id=1, source_target_pairs={{0,2},{2,0},{4,6},{6,4},{1,3},{3,1},{5,7},{7,5},{8,10},{10,8},{12,... | collective-permute-start | bytes 1572872 | tf_op jit(solution)/shard_map/ppermute | solution.py:858
  754.5 15.6 %copy-start.7 = (bf16[1,4,128,1024]{3,2,1,0:T(8,128)(2,1)S(1)}, bf16[1,4,128,1024]{3,2,1,0:T(8,128)(2,1)}, u32[]{:S(2)}) copy-start(bf16[1,4,128,1024]{3,2,1,0:T(8,128)(2,1)} %wgrad.22) | copy-start | bytes 3145732
  754.7 24.0 %copy-start.8 = (bf16[1,4,128,1024]{3,2,1,0:T(8,128)(2,1)S(1)}, bf16[1,4,128,1024]{3,2,1,0:T(8,128)(2,1)}, u32[]{:S(2)}) copy-start(bf16[1,4,128,1024]{3,2,1,0:T(8,128)(2,1)} %wgrad.23) | copy-start | bytes 3145732
  754.7 25.3 %collective-permute-start.27 = (bf16[1024,128]{1,0:T(8,128)(2,1)S(1)}, bf16[1024,128]{1,0:T(8,128)(2,1)S(1)}, u32[]{:S(2)}, u32[]{:S(2)}) collective-permute-start(bf16[1024,128]{1,0:T(8,128)(2,1)S(1)} %fusion.2), channel_id=1, source_target_pairs={{0,4},{2,6},{4,0},{6,2},{1,5},{3,7},{5,1},{7,3},{8,12},{10,14},{12... | collective-permute-start | bytes 786440 | tf_op jit(solution)/shard_map/ppermute | solution.py:860
  770.2 23.6 %collective-permute-start.22 = (bf16[128,1024]{1,0:T(8,128)(2,1)S(1)}, bf16[128,1024]{1,0:T(8,128)(2,1)S(1)}, u32[]{:S(2)}, u32[]{:S(2)}) collective-permute-start(bf16[128,1024]{1,0:T(8,128)(2,1)S(1)} %fusion.10), channel_id=1, source_target_pairs={{0,4},{2,6},{4,0},{6,2},{1,5},{3,7},{5,1},{7,3},{8,12},{10,14},{12... | collective-permute-start | bytes 786440 | tf_op jit(solution)/shard_map/ppermute | solution.py:860
  778.8 18.5 %collective-permute-start.25 = (bf16[128,1024]{1,0:T(8,128)(2,1)S(1)}, bf16[128,1024]{1,0:T(8,128)(2,1)S(1)}, u32[]{:S(2)}, u32[]{:S(2)}) collective-permute-start(bf16[128,1024]{1,0:T(8,128)(2,1)S(1)} %fusion.6), channel_id=1, source_target_pairs={{0,4},{2,6},{4,0},{6,2},{1,5},{3,7},{5,1},{7,3},{8,12},{10,14},{12... | collective-permute-start | bytes 786440 | tf_op jit(solution)/shard_map/ppermute | solution.py:860
  (27 other events, 161.0 us)
Sparse Core Ops, SparseCore 0:
  404.9 111.9 reduce-scatter.3
  537.0 81.8 reduce-scatter.5
  661.2 64.0 reduce-scatter.7

commit v2 on v1

--- a/solution.py
+++ b/solution.py
@@ -18,7 +18,40 @@
 BF = jnp.bfloat16
 F32 = jnp.float32
 MIB = 1 << 20
-cost_scale = 0.4
+PLAN = {
+    "c_mid": 1.0,
+    "e_dn_d0": 1,
+    "e_dp_q": 1,
+    "e_fb0_gf": 1,
+    "e_fb1_gf": 1,
+    "e_fb1_uf": 1,
+    "e_fin_qn": 1,
+    "e_gn_d1": 1,
+    "e_in_cd": 1,
+    "e_in_dp": 1,
+    "e_in_qf": 1,
+    "e_in_un": 1,
+    "e_kf_un": 1,
+    "e_m1_gf": 1,
+    "e_m1_m0": 1,
+    "e_on_kf": 1,
+    "e_pk_fin": 1,
+    "e_pk_kc": 1,
+    "e_pk_kn": 1,
+    "e_qb_gn": 1,
+    "e_qb_uf": 1,
+    "e_qf_of": 1,
+    "e_qn_on": 1,
+    "scale": 0.7,
+    "serial": 1,
+}
+
+
+def O(key, default=0):
+    return PLAN.get(key, default)
+
+
+cost_scale = O("scale", 0.4)
 
 
 def params(limit=56, **kw):
@@ -258,7 +291,7 @@
         ),
         out_shape=[sds((rows, q.shape[1]), BF if last else F32), sds((rows, heads * HD), F32)],
         compiler_params=params(),
-        cost_estimate=cost(12 * last + 22 * (1 - last)),
+        cost_estimate=cost(7 * last + 19 * (1 - last)),
         name="flash_fwd",
     )(scalars, q, starts_col, *segs, *prior)
 
@@ -370,16 +403,14 @@
         ),
         out_shape=[sds((span, count * width), F32)] + [sds((span, count * 2 * HD), BF)] * nb,
         compiler_params=params(),
-        cost_estimate=cost(80 * count * width // total),
+        cost_estimate=cost(O('c_fb', 1.0) * 72 * count * width // total),
         name="flash_bwd",
     )(scalars, q, starts_row, *das, *outs, *sums, *segs)
 
 
 def mlp_kernel(*refs, np_):
     x_ref, parts = refs[0], refs[1 : 1 + np_]
-    (gain_ref, cot_ref, wg_ref, wu_ref, wd_ref, m_ref, h_ref, dg_ref, du_ref, gm_ref, acc) = refs[
-        1 + np_ :
-    ]
+    gain_ref, gh_ref, wg_ref, wu_ref, m_ref, h_ref, dg_ref, du_ref, gm_ref, acc = refs[1 + np_ :]
     j = pl.program_id(0)
 
     @pl.when(j == 0)
@@ -391,34 +422,27 @@
             for part in parts:
                 h1 = h1 + part[at, :].astype(F32)
             m_ref[at, :] = (h1 * rms(h1) * gain_ref[...]).astype(BF)
+        acc[...] = jnp.zeros_like(acc)
 
     m = m_ref[...]
     gate = dot(m, wg_ref[...])
     up = dot(m, wu_ref[...])
-    gh = dot(cot_ref[...], wd_ref[...], 1, 1)
+    gh = gh_ref[...].astype(F32)
     sig = jax.nn.sigmoid(gate)
     silu = gate * sig
     h_ref[...] = (silu * up).astype(BF)
-    dg = (gh * up * sig * (1.0 + gate * (1.0 - sig))).astype(BF)
+    dg = (gh * up * (sig * (1.0 + gate * (1.0 - sig)))).astype(BF)
     du = (gh * silu).astype(BF)
     dg_ref[...] = dg
     du_ref[...] = du
-    add = dot(dg, wg_ref[...], 1, 1) + dot(du, wu_ref[...], 1, 1)
-
-    @pl.when(j == 0)
-    def _():
-        acc[...] = add
-
-    @pl.when(j > 0)
-    def _():
-        acc[...] += add
+    acc[...] += dot(dg, wg_ref[...], 1, 1) + dot(du, wu_ref[...], 1, 1)
 
     @pl.when(j == pl.num_programs(0) - 1)
     def _():
         gm_ref[...] = acc[...].astype(BF)
 
 
-def mlp(x, parts, cot, gain, wg, wu, wd, chunk, tf):
+def mlp(x, parts, gh, gain, wg, wu, chunk, tf):
     rows, d = parts[0].shape
     ff = wg.shape[1]
     once = pl.Buffered(1)
@@ -432,10 +456,9 @@
             at_chunk,
             *([whole] * len(parts)),
             pl.BlockSpec((1, d), lambda j: (0, 0)),
-            at_chunk,
+            pl.BlockSpec((rows, tf), lambda j: (chunk, j)),
             pl.BlockSpec((d, tf), lambda j: (0, j)),
             pl.BlockSpec((d, tf), lambda j: (0, j)),
-            pl.BlockSpec((tf, d), lambda j: (j, 0)),
         ],
         out_specs=[
             pl.BlockSpec((rows, d), lambda j: (0, 0)), tile, tile, tile,
@@ -447,9 +470,9 @@
             sds((rows, d), BF),
         ],
         compiler_params=params(),
-        cost_estimate=cost(47),
+        cost_estimate=cost(O('c_mlp', 1.0) * 38),
         name="mlp",
-    )(x, *parts, gain, cot, wg, wu, wd)
+    )(x, *parts, gain, gh, wg, wu)
 
 
 def mid_kernel(*refs, np_, ng):
@@ -494,7 +517,7 @@
         out_specs=[tile, pl.BlockSpec((tm, n), lambda i: (i, 0)), pl.BlockSpec((8, d), lambda i: (0, 0))],
         out_shape=[sds((rows, d), BF), sds((rows, n), BF), sds((8, d), F32)],
         compiler_params=params(),
-        cost_estimate=cost(11),
+        cost_estimate=cost(O('c_mid', 1.0) * 11),
         name="mid_backward",
     )(x, *parts, *grads, gain, cot, w_out)
 
@@ -544,7 +567,7 @@
         out_specs=[tile, pl.BlockSpec((8, HD), lambda i: (0, 0))],
         out_shape=[sds((rows, n), BF), sds((8, HD), F32)],
         compiler_params=params(),
-        cost_estimate=cost(8.5),
+        cost_estimate=cost(O('c_qb', 1.0) * 8.5),
         name="q_back",
     )(*dqs, raw, cosine, sine, hg)
 
@@ -604,7 +627,7 @@
         ),
         out_shape=[sds((rows, 2 * n), BF), sds((rows, d), BF), sds((8, HD), F32), sds((8, d), F32)],
         compiler_params=params(),
-        cost_estimate=cost(12.5),
+        cost_estimate=cost(O('c_in', 1.0) * 12.5),
         name="in_back",
     )(
         jnp.reshape(base_tile, (1,)), *[v for g in groups for v in g], raw, dq_low, x, cosine,
@@ -612,38 +635,30 @@
     )
 
 
-def wgrad_kernel(s_ref, *refs, nt, na, cut, row_type, ns):
-    outs, aside = refs[2 * nt + na : 2 * nt + na + cut], refs[2 * nt + na + cut :]
-    if row_type:
-        turned = aside[0]
-
-        @pl.when(pl.program_id(1) == 0)
-        def _():
-            for n in range(nt):
-                turned[n] = refs[2 * n][...].T
-
-        total = dot(turned[0], refs[1][...])
-        for n in range(1, nt):
-            total = total + dot(turned[n], refs[2 * n + 1][...])
-    else:
-        total = dot(refs[0][...], refs[1][...], 0, 0)
-        for n in range(1, nt):
-            total = total + dot(refs[2 * n][...], refs[2 * n + 1][...], 0, 0)
+def pick_tile(n):
+    for tile in (1536, 1024, 768, 512, 384, 256, 128):
+        if n % tile == 0 and n > tile:
+            return tile
+    return n
+
+
+def product(refs, nt):
+    stack = lambda ks: jnp.concatenate([refs[k][...] for k in ks], axis=0)
+    return dot(stack(range(0, 2 * nt, 2)), stack(range(1, 2 * nt, 2)), 0, 0)
+
+
+def pieces_of(total, row_type, ns):
+    size = total.shape[0 if row_type else 1] // ns
     for n in range(ns):
-        if row_type:
-            size = total.shape[0] // ns
-            piece = total[n * size : (n + 1) * size]
-        else:
-            size = total.shape[1] // ns
-            piece = total[:, n * size : (n + 1) * size]
-        adds, n_at = [], n
-        for add in refs[2 * nt : 2 * nt + na]:
-            if 0 <= n_at < add.shape[1]:
-                adds.append(add[0, n_at])
-            n_at = n if add.shape[1] == ns else n_at - add.shape[1]
+        yield total[n * size : (n + 1) * size] if row_type else total[:, n * size : (n + 1) * size]
+
+
+def wgrad_kernel(s_ref, *refs, nt, na, row_type, ns, seq_first):
+    adds, out_ref = refs[2 * nt : 2 * nt + na], refs[2 * nt + na]
+    for n, piece in enumerate(pieces_of(product(refs, nt), row_type, ns)):
         for add in adds:
-            piece = piece + add.astype(F32)
-        outs[n * cut // ns][0, n % (ns // cut)] = piece.astype(BF)
+            piece = piece + add[0, n].astype(F32)
+        out_ref[(n, 0) if seq_first else (0, n)] = piece.astype(BF)
 
 
 def after(value, *others):
@@ -654,55 +669,55 @@
     return jnp.minimum(jnp.abs(value[:1, :1].astype(F32)), 0.0)
 
 
-def wgrad(terms, blocks, addends, row_type, nd, ns, rows, behind, cut=1, done=()):
+def wgrad(terms, blocks, addends, row_type, nd, ns, rows, behind, seq_first=False):
     nb, nt = len(blocks), len(terms)
     scalars = jnp.stack(
         [jnp.asarray(v, jnp.int32) for v in blocks]
         + [jnp.asarray(v(), jnp.int32) for t in terms for v in (t[1], t[3])]
     )
     scalars = after(scalars, *behind)
-    for value in done:
-        scalars = scalars + nought(value)[0].astype(jnp.int32)
     left, right = terms[0][0].shape[1], terms[0][2].shape[1]
     ins = []
     if row_type:
         bw = left // nd
-        tile = min(512, right)
+        tile = pick_tile(right)
         steps = right // tile
         for n in range(nt):
             ins.append(pl.BlockSpec((rows, bw), lambda b, t, s, n=n: (s[nb + 2 * n], s[b])))
             ins.append(pl.BlockSpec((rows, tile), lambda b, t, s, n=n: (s[nb + 2 * n + 1], t)))
         out_dims = (ns, bw // ns, right)
-        block = lambda n: (1, n, bw // ns, tile)
+        block = (1, ns, bw // ns, tile)
         at = lambda b, t, s: (b, 0, 0, t)
         add_at = lambda k: lambda b, t, s: (k, 0, 0, t)
-        scratch = [pltpu.VMEM((nt, bw, rows), BF)]
     else:
         bw = right // nd
-        tile = min(512, left)
+        tile = pick_tile(left)
         steps = left // tile
         for n in range(nt):
             ins.append(pl.BlockSpec((rows, tile), lambda b, t, s, n=n: (s[nb + 2 * n], t)))
             ins.append(pl.BlockSpec((rows, bw), lambda b, t, s, n=n: (s[nb + 2 * n + 1], s[b])))
         out_dims = (ns, left, bw // ns)
-        block = lambda n: (1, n, tile, bw // ns)
+        block = (1, ns, tile, bw // ns)
         at = lambda b, t, s: (b, 0, t, 0)
         add_at = lambda k: lambda b, t, s: (k, 0, t, 0)
-        scratch = []
     work = 2e-9 * nt * rows * left * right / nd
     operands = [v for t in terms for v in (t[0], t[2])]
     for arr, k in addends:
-        ins.append(pl.BlockSpec(block(arr.shape[1]), add_at(k)))
+        ins.append(pl.BlockSpec(block, at if k is None else add_at(k)))
         operands.append(arr)
-    size = nb * math.prod(out_dims)
+    out_dims = (ns, nb, *out_dims[1:]) if seq_first else (nb, *out_dims)
+    out_block, out_at = block, at
+    if seq_first:
+        out_block = (block[1], 1, *block[2:])
+        out_at = lambda *a: (0, at(*a)[0], *at(*a)[2:])
     return pl.pallas_call(
-        functools.partial(wgrad_kernel, nt=nt, na=len(addends), cut=cut, row_type=row_type, ns=ns),
-        grid_spec=grid_spec(
-            1, (nb, steps), ins, [pl.BlockSpec(block(ns // cut), at)] * cut, scratch
+        functools.partial(
+            wgrad_kernel, nt=nt, na=len(addends), row_type=row_type, ns=ns, seq_first=seq_first
         ),
-        out_shape=[sds((nb, ns // cut, *out_dims[1:]), BF)] * cut,
+        grid_spec=grid_spec(1, (nb, steps), ins, pl.BlockSpec(out_block, out_at)),
+        out_shape=sds(out_dims, BF),
         compiler_params=params(),
-        cost_estimate=cost(1 + 3 * work),
+        cost_estimate=cost(O('c_wg', 1.0) * (1 + 2.3 * work * nb)),
         name="wgrad",
     )(scalars, *operands)
 
@@ -743,24 +758,7 @@
     def _():
         copy(slots.at[slot], place(b, t), slot).wait_send()
 
-    if row_type:
-        turned = refs[2 * nt + 4]
-
-        @pl.when(t == 0)
-        def _():
-            for n in range(nt):
-                turned[n] = ins[2 * n][...].T
-
-        total = dot(turned[0], ins[1][...])
-        for n in range(1, nt):
-            total = total + dot(turned[n], ins[2 * n + 1][...])
-    else:
-        total = dot(ins[0][...], ins[1][...], 0, 0)
-        for n in range(1, nt):
-            total = total + dot(ins[2 * n][...], ins[2 * n + 1][...], 0, 0)
-    size = total.shape[0 if row_type else 1] // ns
-    for n in range(ns):
-        piece = total[n * size : (n + 1) * size] if row_type else total[:, n * size : (n + 1) * size]
+    for n, piece in enumerate(pieces_of(product(ins, nt), row_type, ns)):
         slots[slot, n] = piece.astype(BF)
     copy(slots.at[slot], place(b, t), slot).start()
 
@@ -780,22 +778,20 @@
     ins = []
     if row_type:
         bw = left // nd
-        tile = min(512, right)
+        tile = pick_tile(right)
         steps = right // tile
         for t in terms:
             ins.append(pl.BlockSpec((rows, bw), lambda b, s, r=t[1]: (r(), block(b))))
             ins.append(pl.BlockSpec((rows, tile), lambda b, s, r=t[3]: (r(), s)))
         out_dims, slot = (ns, bw // ns, right), (ns, bw // ns, tile)
-        scratch = [pltpu.VMEM((nt, bw, rows), BF)]
     else:
         bw = right // nd
-        tile = min(512, left)
+        tile = pick_tile(left)
         steps = left // tile
         for t in terms:
             ins.append(pl.BlockSpec((rows, tile), lambda b, s, r=t[1]: (r(), s)))
             ins.append(pl.BlockSpec((rows, bw), lambda b, s, r=t[3]: (r(), block(b))))
         out_dims, slot = (ns, left, bw // ns), (ns, tile, bw // ns)
-        scratch = []
     work = 2e-9 * nt * rows * left * right / nd
     operands = [v for t in terms for v in (t[0], t[2])]
     operands[0] = after(operands[0], *behind)
@@ -808,18 +804,17 @@
         out_specs=pl.BlockSpec(memory_space=pl.ANY),
         scratch_shapes=[
             pltpu.VMEM((2, *slot), BF), pltpu.SemaphoreType.DMA((2,)), pltpu.SemaphoreType.DMA,
-            *scratch,
         ],
         out_shape=sds((2, *out_dims), BF),
         compiler_params=params(collective_id=ident, has_side_effects=True),
-        cost_estimate=cost(2 + 4.4 * work),
+        cost_estimate=cost(O('c_ws', 1.0) * (2 + 3.4 * work)),
         name="wgrad_send",
     )(*operands)
 
 
 class Shrink:
     def __init__(self, terms, row_type, ahead=None, small=False, *, nd, ns, rows):
-        self.small = small
+        self.small, self.pair = small, None
         self.args, self.nd = (terms, row_type), nd
         self.ahead = ahead
         self.ident = ahead.ident + 1 if ahead else 0
@@ -835,21 +830,32 @@
         self.got = wgrad_send(terms, row_type, *self.sizes, self.ident, behind)
         return self.got
 
-    def far(self, *behind, done=()):
-        out = self.make([self.d ^ 2], [(self.got, 1)], behind, done=done)[0]
-        first = [self.ahead.ahead.come] if self.ahead and self.ahead.ahead else []
+    def far(self, *behind):
+        out = self.make([self.d ^ 2], [(self.got, 1)], behind)
+        first = self.ahead
+        for _ in range(O('serial', 1)):
+            first = first.ahead if first else None
+        first = [first.come] if first and first.pair is None and O('serial', 1) < 3 else []
         self.come = lax.ppermute(
             after(out, *first), "dp", [(k, k ^ 2) for k in range(self.nd)]
         )
         return out
 
+    def both(self, *behind):
+        out = self.make([self.d, self.d ^ 2], [(self.got, None)], behind, seq_first=True)
+        self.pair = lax.psum_scatter(out, "seq", scatter_dimension=0)
+        return out
+
     def near(self, *behind):
-        self.here = self.make([self.d], [(self.got, 0), (self.come, 0)], behind)[0]
+        self.here = self.make([self.d], [(self.got, 0), (self.come, 0)], behind)
         if not self.small:
             self.share = lax.psum_scatter(self.here[0], "seq", scatter_dimension=0)
         return self.here
 
     def finish(self):
+        if self.pair is not None:
+            come = lax.ppermute(self.pair[1], "dp", [(k, k ^ 2) for k in range(self.nd)])
+            return self.pair[0].astype(F32) + come.astype(F32)
         if not self.small:
             return self.share.astype(F32)
         z, ns = lax.axis_index("seq"), self.sizes[1]
@@ -880,7 +886,7 @@
         out_specs=tile,
         out_shape=sds((rows, d), BF),
         compiler_params=params(),
-        cost_estimate=cost(8),
+        cost_estimate=cost(O('c_fin', 1.0) * 8),
         name="final",
     )(x, ga, gb, h0, h1, gain, jnp.reshape(y, (1,)))
 
@@ -898,7 +904,7 @@
     z, y = lax.axis_index("seq"), lax.axis_index("tensor")
     row = lambda v: v[None, :]
     tm = 256
-    tq, tk = 256, 512
+    tq = tk = 512
     swap = lambda v: lax.ppermute(v, "tensor", [(0, 1), (1, 0)])
     pick = lambda a, b: jnp.where(y == 0, a, b)
 
@@ -942,6 +948,8 @@
     raws = []
     ahead = [(k, k + 1) for k in range(ns - 1)]
     for x_piece, base, base_tile in zip(pieces, bases, base_tiles):
+        if raws and O('e_kv_hop'):
+            base_tile = after(base_tile, segs[1][0])
         kv, raw = project_kv(
             x_piece, base_tile, row(norm_attn), w_key, w_value, cosine, sine, row(key_norm), tm
         )
@@ -967,7 +975,7 @@
     outs, sums, parts = [], [], []
     for c in range(2):
         out, total = attend(
-            seg_bases[back], query, after(starts_col, *outs), segs[back], prior, part=(0, span),
+            seg_bases[back], query, after(starts_col, *[v[0] for v in parts]), segs[back], prior, part=(0, span),
             row_at=c * rows, rows=rows, last=True,
         )
         outs.append(out)
@@ -975,11 +983,12 @@
         partial = dot(out, w_out).astype(BF)
         parts.append([partial, swap(partial)] if nt == 2 else [lax.psum(partial, "tensor")])
 
+    grad_hidden = dot(after(cot, partial), w_down, 1, 1).astype(BF)
     low_mlp, hidden, d_gate, d_up, grads = [], [], [], [], []
     tf = min(512, w_gate.shape[1] // 2)
     for c in range(2):
         m, h, dg, du, gm = mlp(
-            x_all, parts[c], cot, after(row(norm_mlp), *low_mlp), w_gate, w_up, w_down, c, tf
+            x_all, parts[c], grad_hidden, after(row(norm_mlp), *low_mlp), w_gate, w_up, c, tf
         )
         low_mlp.append(m)
         hidden.append(h)
@@ -990,9 +999,9 @@
     shrink = functools.partial(Shrink, nd=nd, ns=ns, rows=rows)
     zero = lambda: 0
     chunk = lambda c: lambda: c
-    down = shrink([(hidden[c], zero, cot, chunk(c)) for c in range(2)], False)
-    gate = shrink([(low_mlp[c], zero, d_gate[c], zero) for c in range(2)], True, down)
-    up = shrink([(low_mlp[c], zero, d_up[c], zero) for c in range(2)], True, gate)
+    down = shrink([(hidden[c], zero, cot, chunk(c)) for c in range(2)], False, None, bool(O('p_down')))
+    gate = shrink([(low_mlp[c], zero, d_gate[c], zero) for c in range(2)], True, down, bool(O('p_gate')))
+    up = shrink([(low_mlp[c], zero, d_up[c], zero) for c in range(2)], True, gate, bool(O('p_up')))
     gh, g_att, g_norm_two = [], [], []
 
     def middle(c, *behind):
@@ -1004,16 +1013,23 @@
         g_norm_two.append(gn)
         return low
 
+    opt = lambda k, *v: list(v) if O(k) else []
     down.send()
-    middle(0)
-    middle(1, gh[0], gate.send(down.far()))
-    t = []
+    middle(0, *opt('e_m0_ds', down.got))
+    zf = bool(O('zf'))
+    df = down.both(*opt('e_df_m0', gh[0])) if zf else down.far(*opt('e_df_m0', gh[0]))
+    gs_out = gate.send(*opt('e_gs_df', df), *opt('e_gs_m0', gh[0]))
+    gf = gate.far() if O('e_gf_early') else None
+    middle(1, *opt('e_m1_m0', gh[0]), *opt('e_m1_gs', gs_out), *opt('e_m1_gf', *([gf] if gf is not None else [])))
+    if gf is None:
+        gf = gate.far(gh[1])
+    t = opt('e_fb0_gf', gf)
     hop_segs = [v for seg in segs for v in seg]
     hop_bases = jnp.stack([v for b in seg_bases for v in b])
     scalars = jnp.concatenate([*bounds(0, span, 0, window), hop_bases])
     halves = [(0, heads_kv)] if heads_kv == 1 else [(0, heads_kv // 2), (heads_kv // 2, heads_kv // 2)]
     behind = [(k + 1, k) for k in range(ns - 1)]
-    dqs, dkvs = [], []
+    dqs, dkvs, first_hops = [], [], []
     for part, heads in enumerate(halves):
         dq, *dkv = flash_bwd(
             after(scalars, *t), query, starts_row, g_att, outs, sums, hop_segs, window, gs, tq, tk,
@@ -1025,24 +1041,39 @@
             if come is not None:
                 send = (send.astype(F32) + come.astype(F32)).astype(BF)
             come = lax.ppermute(send, "seq", behind)
+            first_hops += [come] if b == 0 else []
         dqs.append(dq)
         dkvs.append([dkv[back]] + ([come] if come is not None else []))
         if part == 0:
-            t = [gate.far(gh[1]), down.near(dq)]
-    out_w = shrink([(outs[c], zero, gh[c], zero) for c in range(2)], False, up, True)
-    t = up.far(gate.near(up.send(*dqs)))
-    dq_low, g_qn = q_back(dqs, q_raw, cosine, sine, after(row(query_norm), t), tm)
-    query_w = shrink([(attn_in, chunk(c), dq_low, chunk(c)) for c in range(2)], True, out_w, True)
-    t = out_w.far(out_w.send(dq_low))
-    t = query_w.far(query_w.send(t))
-    w_down_later = after(w_down, dq_low)
+            dn = dq if zf else down.near(*opt('e_dn_d0', dq))
+            us = up.send(dq)
+            t = opt('e_fb1_dn', dn) + opt('e_fb1_us', us) + opt('e_fb1_gf', gf)
+            if O('e_fb1_uf'):
+                uf = up.far()
+                t += [uf]
+    out_w = shrink([(outs[c], zero, gh[c], zero) for c in range(2)], False, up, bool(O('p_out',1)))
+    if not O('e_fb1_uf'):
+        uf = up.far(dqs[-1])
+    gn_ = gate.near(*opt('e_gn_d1', dqs[-1]), *opt('e_gn_uf', uf), *opt('e_gn_hop', *first_hops))
+    dq_low, g_qn = q_back(
+        dqs, q_raw, cosine, sine,
+        after(row(query_norm), *opt('e_qb_uf', uf), *opt('e_qb_gn', gn_), *opt('e_qb_hop', *first_hops)), tm,
+    )
+    query_w = shrink([(attn_in, chunk(c), dq_low, chunk(c)) for c in range(2)], True, out_w, bool(O('p_q',1)))
+    os_ = out_w.send(dq_low)
+    qs_ = query_w.send(*opt('e_qs_os', os_))
+    of_ = out_w.far(*opt('e_of_qs', qs_))
+    qf_ = query_w.far(*opt('e_qf_of', of_))
+    w_down_later = after(w_down, dq_low) if O('e_dp_q') else after(w_down, gh[1]) if O('e_dp_m') else w_down
     downs = [dot(hidden[c], w_down_later).astype(BF) for c in range(2)]
-    t = [t, *downs]
+    come_down = swap(pick(downs[1], downs[0])) if nt == 2 else downs[0]
+    un = up.near(*opt('e_un_qf', qf_), *opt('e_un_d1', dqs[-1]))
+    t = opt('e_in_qf', qf_) + opt('e_in_dp', *downs) + opt('e_in_cd', come_down) + opt('e_in_un', un)
 
     lows, gas, g_kn, g_norm_one = [None] * 2, [None] * 2, [], []
     for n in (1, 0):
         lows[n], gas[n], gain_part, norm_part = in_back(
-            dkvs, raws[n], dq_low, x_all, base_tiles[n], cosine, sine, after(row(key_norm) + nought(down.share), *t),
+            dkvs, raws[n], dq_low, x_all, base_tiles[n], cosine, sine, after(row(key_norm), *t),
             w_query, w_key, w_value, tm,
         )
         g_kn.append(gain_part)
@@ -1050,22 +1081,19 @@
     kv_cut = heads_kv * HD
     own_half = lambda: lax.axis_index("tensor")
     half_of = lambda n: chunk(n) if nt != 2 else own_half if n == 0 else lambda: 1 - own_half()
-    kv_w = shrink([(attn_in, half_of(n), lows[n], zero) for n in range(2)], True, query_w, True)
-    kv_w.send()
-    t = up.near(kv_w.far(done=[gate.share]))
-    t = query_w.near(out_w.near(t))
-    kv_w.near(t)
-    g_down, g_gate, g_up, g_out, g_query, g_kv = [
-        v.finish() for v in (down, gate, up, out_w, query_w, kv_w)
-    ]
+    kv_w = shrink([(attn_in, half_of(n), lows[n], zero) for n in range(2)], True, query_w, bool(O('p_kv',1)))
+    ks_ = kv_w.send()
+    kf_ = kv_w.far(*opt('e_kf_un', un))
+    on_ = out_w.near(*opt('e_on_kf', kf_))
+    qn_ = query_w.near(*opt('e_qn_on', on_))
+    gain_last = after(row(norm_attn), *opt('e_fin_qn', qn_), *opt('e_fin_kf', kf_), *opt('e_fin_on', on_))
 
     up32 = lambda v: v.astype(F32)
     if nt == 2:
-        come_down = swap(pick(downs[1], downs[0]))
         result = up32(tokens) + up32(pick(downs[0], downs[1])) + up32(come_down)
         for n in range(2):
             result = result + up32(pick(parts[0][n], parts[1][n]))
-        grad_tokens = final(tokens, gas[0], swap(gas[1]), gh[0], gh[1], row(norm_attn), y, tm)
+        grad_tokens = final(tokens, gas[0], swap(gas[1]), gh[0], gh[1], gain_last, y, tm)
     else:
         scatter = lambda v: lax.psum_scatter(v, "tensor", scatter_dimension=0, tiled=True)
         mine = lambda pair: lax.dynamic_slice_in_dim(
@@ -1079,6 +1107,10 @@
         g1 = up32(scatter(jnp.concatenate(gas, axis=0))) * row(norm_attn)
         moved = inv * (g1 - n1 * jnp.mean(g1 * n1, axis=1, keepdims=True))
         grad_tokens = (up32(mine(gh)) + moved).astype(BF)
+    kn_ = kv_w.near(*opt('e_kn_fin', grad_tokens))
+    g_down, g_gate, g_up, g_out, g_query, g_kv = [
+        v.finish() for v in (down, gate, up, out_w, query_w, kv_w)
+    ]
 
     share = 1.0 / nt
     fold = lambda pair: jnp.sum(pair[0] + pair[1], axis=0)
@@ -1086,7 +1118,7 @@
     packed = jnp.concatenate(
         [fold(g_norm_one), fold(g_norm_two) * share, jnp.sum(g_qn, axis=0), fold(g_kn)]
     )
-    packed = total_sum(packed, axes)
+    packed = total_sum(after(packed, *opt('e_pk_fin', grad_tokens), *opt('e_pk_kn', kn_), *opt('e_pk_kc', kv_w.come)), axes)
     return (
         result.astype(BF)[None], grad_tokens[None], g_query, g_kv[:, :kv_cut], g_kv[:, kv_cut:],
         g_out, g_gate, g_up, g_down,

time: 817 us -> 749 us (0.917)
  Pallas kernels: 448 us -> 401 us
  waiting for transfers between devices: 197 us -> 156 us
  matrix products: 26.8 us -> 51.5 us
    ppermute x6, waiting for transfers between devices: 8.21 us -> 39.5 us  [far(): lax.ppermute(after(out, *first), 'dp', [(k, k ^ 2) for k in range(self.nd)])]
    ppermute x8, waiting for transfers between devices: 55.2 us -> 25 us  [per_device(): swap = lambda v: lax.ppermute(v, 'tensor', [(0, 1), (1, 0)])]
    ppermute x5, waiting for transfers between devices: 31.5 us -> 2.98 us  [total_sum(): v = v + lax.ppermute(v, name, [(k, k ^ step) for k in range(size)])]
    dot_general x4 -> x5, matrix products: 26.8 us -> 51.5 us  [dot(): lax.dot_general(a, b, (((ca,), (cb,)), ((), ())), preferred_element_type=...]
    pallas_call x2, Pallas kernels: 96.3 us -> 75.4 us  [mlp(): pl.pallas_call(functools.partial(mlp_kernel, np_=len(parts)), grid=(ff //...]
    ppermute x4, waiting for transfers between devices: 6.31 us -> 20.8 us  [per_device(): kv = lax.ppermute(kv, 'seq', ahead)]
    pallas_call x4, Pallas kernels: 53.6 us -> 39.6 us  [flash_fwd(): pl.pallas_call(functools.partial(flash_fwd_kernel, nseg=len(segs), prior=...]
    ppermute x4, waiting for transfers between devices: 61.3 us -> 49.1 us  [per_device(): come = lax.ppermute(send, 'seq', behind)]
  transfers between devices with their start and end apart: 36 -> 36, of which waited for: 14 -> 17; matrix products, arithmetic and copies ran while one was open for 9% -> 13% of each run, Pallas kernels for 54% -> 53%
where the time goes in v2:
time: 749 us; the launch traced here: 739 us
  Pallas kernels  401 us (54%)
  waiting for transfers between devices  156 us (21%)
  starting transfers between devices  55.7 us (7%)
  matrix products  51.5 us (7%)
  other arithmetic  32.6 us (4%)
  local copies, waits for them, and re-layouts  24.8 us (3%)
  between operations  17.3 us (2%)
    pallas_call x12, Pallas kernels, wgrad(): pl.pallas_call(functools.partial(wgrad_kernel, nt=nt, na=len(addends), ro...  84.6 us
    pallas_call x2, Pallas kernels, mlp(): pl.pallas_call(functools.partial(mlp_kernel, np_=len(parts)), grid=(ff //...  75.4 us
    pallas_call x6, Pallas kernels, wgrad_send(): pl.pallas_call(functools.partial(wgrad_send_kernel, nt=nt, row_type=row_t...  73.9 us
    dot_general x5, matrix products, dot(): lax.dot_general(a, b, (((ca,), (cb,)), ((), ())), preferred_element_type=...  51.5 us
    ppermute x4, waiting for transfers between devices, per_device(): come = lax.ppermute(send, 'seq', behind)  49.1 us
    pallas_call x4, Pallas kernels, flash_fwd(): pl.pallas_call(functools.partial(flash_fwd_kernel, nseg=len(segs), prior=...  39.6 us
    ppermute x6, waiting for transfers between devices, far(): lax.ppermute(after(out, *first), 'dp', [(k, k ^ 2) for k in range(self.nd)])  39.5 us
    pallas_call x2, Pallas kernels, flash_bwd(): pl.pallas_call(functools.partial(flash_bwd_kernel, nc=nc, ns=len(segs), n...  36.6 us
  transfers between devices with their start and end apart: 36, of which 17 were waited for; matrix products, arithmetic and copies ran while one was open for 13% of the time, Pallas kernels for 53%

profile of v2, /device:TPU:0, one launch (start us, length us, event | category | flops | bytes accessed | tf_op | source)
XLA Modules:
  0.0 739.1 jit_solution(11738102756911699741)
XLA Ops:
  15.4 6.5 project_kv.2
  35.5 12.4 %collective-permute-done.1.rest_0_.rest_8_ = bf16[512,1024]{1,0:T(8,128)(2,1)S(1)} collective-permute-done((bf16[512,1024]{1,0:T(8,128)(2,1)}, bf16[512,1024]{1,0:T(8,128)(2,1)S(1)}, u32[]{:S(2)}, u32[]{:S(2)}) %collective-permute-start.1) | collective-permute-done | bytes 1048608 | tf_op jit(solution)/shard_map/ppermute | solution.py:961
  56.2 6.7 project_kv.3
  69.1 13.2 %project_q.1 = (bf16[1024,2048]{1,0:T(8,128)(2,1)}, bf16[1024,2048]{1,0:T(8,128)(2,1)}, bf16[1024,1024]{1,0:T(8,128)(2,1)}, f32[1024,1024]{1,0:T(8,128)}) custom-call(s32[2]{0:T(128)} %pad_add_fusion.10.s_ref, bf16[512,2048]{1,0:T(8,128)(2,1)} %bitcast.122, bf16[512,2048]{1,0:T(8,128)(2,1)} %collective-permute-done.xb_ref.x_ref, f32[1,2048]{1,0:T(1,128)} %bitcast.131, ...), custom_call_target="tpu_custom_call" | custom-call | flops 9100000256 | tf_op jit(solution)/shard_map/project_q/pallas_call | solution.py:160
  82.3 15.0 %flash_fwd.4 = (f32[1024,1024]{1,0:T(8,128)}, f32[1024,512]{1,0:T(8,128)}) custom-call(s32[10]{0:T(128)} %concatenate.27.s_ref, bf16[1024,1024]{1,0:T(8,128)(2,1)} %get-tuple-element.91.q_ref, s32[1024,128]{1,0:T(8,128)} %broadcast_in_dim.29.st_ref, bf16[512,1024]{1,0:T(8,128)(2,1)} %get-tuple-element.92.rest_0_.rest_6_, ...), custom_call_target="tpu_custom_call" | custom-call | flops 13299999744 | tf_op jit(solution)/shard_map/flash_fwd/pallas_call | solution.py:271
  101.4 11.3 %flash_fwd.5 = (f32[1024,1024]{1,0:T(8,128)}, f32[1024,512]{1,0:T(8,128)}) custom-call(s32[10]{0:T(128)} %concatenate.26.s_ref, bf16[1024,1024]{1,0:T(8,128)(2,1)} %get-tuple-element.91.q_ref, s32[1024,128]{1,0:T(8,128)} %broadcast_in_dim.29.st_ref, bf16[512,1024]{1,0:T(8,128)(2,1)} %copy-done.33, bf16[512,1024]{1,0:T(8,128)(2,1)} %collective-permute-done.3.rest_1_.rest_9_, ...), custom_call_target="tpu_custom_call" | custom-call | flops 13299999744 | tf_op jit(solution)/shard_map/flash_fwd/pallas_call | solution.py:271
  112.7 8.5 %collective-permute-done.4.rest_1_.rest_11_ = bf16[512,1024]{1,0:T(8,128)(2,1)} collective-permute-done((bf16[512,1024]{1,0:T(8,128)(2,1)}, bf16[512,1024]{1,0:T(8,128)(2,1)}, u32[]{:S(2)}, u32[]{:S(2)}) %collective-permute-start.4) | collective-permute-done | bytes 1048608 | tf_op jit(solution)/shard_map/ppermute | solution.py:961
  121.2 6.7 flash_fwd.6
  133.3 6.6 flash_fwd.7
  140.0 6.3 convolution_convert_fusion.3.refs_1_
  148.6 18.7 %convolution_convert_fusion.refs_4_ = bf16[1024,3072]{1,0:T(8,128)(2,1)} fusion(bf16[1024,2048]{1,0:T(8,128)(2,1)S(1)} %pad_maximum_fusion.refs_6_.refs_1_.refs_3_, bf16[3072,2048]{1,0:T(8,128)(2,1)} %param.22), kind=kOutput, calls=%fused_computation | convolution fusion | flops 12888047616 | bytes 23068672 | tf_op jit(solution)/shard_map/dot_general | solution.py:66
  167.3 14.2 %collective-permute-done.5.refs_2_ = bf16[512,2048]{1,0:T(8,128)(2,1)} collective-permute-done((bf16[512,2048]{1,0:T(8,128)(2,1)S(1)}, bf16[512,2048]{1,0:T(8,128)(2,1)}, u32[]{:S(2)}, u32[]{:S(2)}) %collective-permute-start.5) | collective-permute-done | bytes 2097184 | tf_op jit(solution)/shard_map/ppermute | solution.py:908
  181.5 37.6 %mlp.2 = (bf16[512,2048]{1,0:T(8,128)(2,1)}, bf16[512,3072]{1,0:T(8,128)(2,1)}, bf16[512,3072]{1,0:T(8,128)(2,1)}, bf16[512,3072]{1,0:T(8,128)(2,1)}, bf16[512,2048]{1,0:T(8,128)(2,1)}) custom-call(bf16[1024,2048]{1,0:T(8,128)(2,1)} %get-tuple-element.90.refs_0_.refs_6_, bf16[512,2048]{1,0:T(8,128)(2,1)} %copy-done.11, ...), custom_call_target="tpu_custom_call" | custom-call | flops 26599999488 | tf_op jit(solution)/shard_map/mlp/pallas_call | solution.py:452
  219.7 6.8 collective-permute-done.7.refs_2_
  226.5 37.8 %mlp.3 = (bf16[512,2048]{1,0:T(8,128)(2,1)}, bf16[512,3072]{1,0:T(8,128)(2,1)}, bf16[512,3072]{1,0:T(8,128)(2,1)}, bf16[512,3072]{1,0:T(8,128)(2,1)}, bf16[512,2048]{1,0:T(8,128)(2,1)}) custom-call(bf16[1024,2048]{1,0:T(8,128)(2,1)} %get-tuple-element.90.refs_0_.refs_6_, bf16[512,2048]{1,0:T(8,128)(2,1)} %convolution_convert_fusion.3.refs_1_, ...), custom_call_target="tpu_custom_call" | custom-call | flops 26599999488 | tf_op jit(solution)/shard_map/mlp/pallas_call | solution.py:452
  264.8 14.8 %wgrad_send.10.refs_4_ = bf16[2,4,3072,128]{3,2,1,0:T(8,128)(2,1)} custom-call(bf16[512,3072]{1,0:T(8,128)(2,1)} %get-tuple-element.103.refs_0_, bf16[1024,2048]{1,0:T(8,128)(2,1)} %copy-done, bf16[512,3072]{1,0:T(8,128)(2,1)} %get-tuple-element.131.refs_2_, bf16[1024,2048]{1,0:T(8,128)(2,1)} %copy-done), custom_call_target="tpu_custom_call" | custom-call | flops 9066516480 | tf_op jit(solution)/shard_map/wgrad_send/pallas_call | solution.py:798
  279.6 8.2 %wgrad.17 = bf16[1,4,3072,128]{3,2,1,0:T(8,128)(2,1)} custom-call(s32[5]{0:T(128)} %get-tuple-element.191.s_ref, bf16[512,3072]{1,0:T(8,128)(2,1)} %get-tuple-element.103.refs_0_, bf16[1024,2048]{1,0:T(8,128)(2,1)} %copy-done, bf16[512,3072]{1,0:T(8,128)(2,1)} %get-tuple-element.131.refs_2_, bf16[1024,2048]{1,0:T(8,128)(2,1)} %copy-done, ...), custom_call_target="tpu_custom_call" | custom-call | flops 5886173184 | tf_op jit(solution)/shard_map/wgrad/pallas_call | solution.py:713
  289.3 14.8 %wgrad_send.6.refs_4_ = bf16[2,4,128,3072]{3,2,1,0:T(8,128)(2,1)} custom-call(bf16[512,2048]{1,0:T(8,128)(2,1)} %get-tuple-element.123.refs_0_, bf16[512,3072]{1,0:T(8,128)(2,1)} %get-tuple-element.112.refs_1_, bf16[512,2048]{1,0:T(8,128)(2,1)} %get-tuple-element.113.refs_2_, bf16[512,3072]{1,0:T(8,128)(2,1)} %get-tuple-element.114.refs_3_), custom_call_target="tpu_custom_call" | custom-call | flops 9066516480 | tf_op jit(solution)/shard_map/wgrad_send/pallas_call | solution.py:798
  305.5 11.7 %mid_backward.2 = (bf16[512,2048]{1,0:T(8,128)(2,1)}, bf16[512,1024]{1,0:T(8,128)(2,1)}, f32[8,2048]{1,0:T(8,128)}) custom-call(bf16[1024,2048]{1,0:T(8,128)(2,1)} %get-tuple-element.90.refs_0_.refs_6_, bf16[512,2048]{1,0:T(8,128)(2,1)} %copy-done.11, bf16[512,2048]{1,0:T(8,128)(2,1)} %collective-permute-done.5.refs_2_, ...), custom_call_target="tpu_custom_call" | custom-call | flops 7699999744 | tf_op jit(solution)/shard_map/mid_backward/pallas_call | solution.py:511
  318.6 11.3 %mid_backward.3 = (bf16[512,2048]{1,0:T(8,128)(2,1)}, bf16[512,1024]{1,0:T(8,128)(2,1)}, f32[8,2048]{1,0:T(8,128)}) custom-call(bf16[1024,2048]{1,0:T(8,128)(2,1)} %get-tuple-element.90.refs_0_.refs_6_, bf16[512,2048]{1,0:T(8,128)(2,1)} %convolution_convert_fusion.3.refs_1_, bf16[512,2048]{1,0:T(8,128)(2,1)} %collective-permute-done.7.refs_2_, ...), custom_call_target="tpu_custom_call" | custom-call | flops 7699999744 | tf_op jit(solution)/shard_map/mid_backward/pallas_call | solution.py:511
  330.0 8.8 %wgrad.12 = bf16[1,4,128,3072]{3,2,1,0:T(8,128)(2,1)} custom-call(s32[5]{0:T(128)} %stack.112.s_ref, bf16[512,2048]{1,0:T(8,128)(2,1)} %get-tuple-element.123.refs_0_, bf16[512,3072]{1,0:T(8,128)(2,1)} %get-tuple-element.112.refs_1_, bf16[512,2048]{1,0:T(8,128)(2,1)} %get-tuple-element.113.refs_2_, bf16[512,3072]{1,0:T(8,128)(2,1)} %get-tuple-element.114.refs_3_, ...), custom_call_target="tpu_custom_call" | custom-call | flops 5886173184 | tf_op jit(solution)/shard_map/wgrad/pallas_call | solution.py:713
  339.4 18.3 %flash_bwd.2 = (f32[1024,512]{1,0:T(8,128)}, bf16[1024,512]{1,0:T(8,128)(2,1)}, bf16[1024,512]{1,0:T(8,128)(2,1)}, bf16[1024,512]{1,0:T(8,128)(2,1)}) custom-call(s32[14]{0:T(128)} %concatenate.30.s_ref, bf16[1024,1024]{1,0:T(8,128)(2,1)} %get-tuple-element.91.q_ref, s32[8,1024]{1,0:T(8,128)} %broadcast_in_dim.32.st_ref, ...), custom_call_target="tpu_custom_call" | custom-call | flops 25200001024 | tf_op jit(solution)/shard_map/flash_bwd/pallas_call | solution.py:377
  359.9 9.1 %wgrad.23 = bf16[1,4,3072,128]{3,2,1,0:T(8,128)(2,1)} custom-call(s32[5]{0:T(128)} %get-tuple-element.156.s_ref, bf16[512,3072]{1,0:T(8,128)(2,1)} %get-tuple-element.103.refs_0_, bf16[1024,2048]{1,0:T(8,128)(2,1)} %copy-done, bf16[512,3072]{1,0:T(8,128)(2,1)} %get-tuple-element.131.refs_2_, bf16[1024,2048]{1,0:T(8,128)(2,1)} %copy-done, ...), custom_call_target="tpu_custom_call" | custom-call | flops 5886173184 | tf_op jit(solution)/shard_map/wgrad/pallas_call | solution.py:713
  374.1 15.0 %wgrad_send.7.refs_4_ = bf16[2,4,128,3072]{3,2,1,0:T(8,128)(2,1)} custom-call(bf16[512,2048]{1,0:T(8,128)(2,1)} %get-tuple-element.123.refs_0_, bf16[512,3072]{1,0:T(8,128)(2,1)} %get-tuple-element.121.refs_1_, bf16[512,2048]{1,0:T(8,128)(2,1)} %get-tuple-element.113.refs_2_, bf16[512,3072]{1,0:T(8,128)(2,1)} %get-tuple-element.122.refs_3_), custom_call_target="tpu_custom_call" | custom-call | flops 9066516480 | tf_op jit(solution)/shard_map/wgrad_send/pallas_call | solution.py:798
  389.2 8.7 %wgrad.13 = bf16[1,4,128,3072]{3,2,1,0:T(8,128)(2,1)} custom-call(s32[5]{0:T(128)} %stack.112.s_ref, bf16[512,2048]{1,0:T(8,128)(2,1)} %get-tuple-element.123.refs_0_, bf16[512,3072]{1,0:T(8,128)(2,1)} %get-tuple-element.121.refs_1_, bf16[512,2048]{1,0:T(8,128)(2,1)} %get-tuple-element.113.refs_2_, bf16[512,3072]{1,0:T(8,128)(2,1)} %get-tuple-element.122.refs_3_, ...), custom_call_target="tpu_custom_call" | custom-call | flops 5886173184 | tf_op jit(solution)/shard_map/wgrad/pallas_call | solution.py:713
  397.8 18.3 %flash_bwd.3 = (f32[1024,512]{1,0:T(8,128)}, bf16[1024,512]{1,0:T(8,128)(2,1)}, bf16[1024,512]{1,0:T(8,128)(2,1)}, bf16[1024,512]{1,0:T(8,128)(2,1)}) custom-call(s32[14]{0:T(128)} %concatenate.30.s_ref, bf16[1024,1024]{1,0:T(8,128)(2,1)} %get-tuple-element.91.q_ref, s32[8,1024]{1,0:T(8,128)} %broadcast_in_dim.32.st_ref, ...), custom_call_target="tpu_custom_call" | custom-call | flops 25200001024 | tf_op jit(solution)/shard_map/flash_bwd/pallas_call | solution.py:377
  418.5 24.2 %collective-permute-done.10.refs_5_ = bf16[1,4,128,3072]{3,2,1,0:T(8,128)(2,1)S(1)} collective-permute-done((bf16[1,4,128,3072]{3,2,1,0:T(8,128)(2,1)}, bf16[1,4,128,3072]{3,2,1,0:T(8,128)(2,1)S(1)}, u32[]{:S(2)}, u32[]{:S(2)}) %collective-permute-start.10) | collective-permute-done | bytes 3145760 | tf_op jit(solution)/shard_map/ppermute | solution.py:839
  444.3 9.7 %wgrad.14 = bf16[1,4,128,3072]{3,2,1,0:T(8,128)(2,1)} custom-call(s32[5]{0:T(128)} %stack.114.s_ref, bf16[512,2048]{1,0:T(8,128)(2,1)} %get-tuple-element.123.refs_0_, bf16[512,3072]{1,0:T(8,128)(2,1)} %get-tuple-element.112.refs_1_, bf16[512,2048]{1,0:T(8,128)(2,1)} %get-tuple-element.113.refs_2_, bf16[512,3072]{1,0:T(8,128)(2,1)} %get-tuple-element.114.refs_3_, ...), custom_call_target="tpu_custom_call" | custom-call | flops 5886173184 | tf_op jit(solution)/shard_map/wgrad/pallas_call | solution.py:713
  454.1 8.4 %q_back.1 = (bf16[1024,1024]{1,0:T(8,128)(2,1)}, f32[8,128]{1,0:T(8,128)}) custom-call(f32[1024,512]{1,0:T(8,128)} %get-tuple-element.120.refs_0_, f32[1024,512]{1,0:T(8,128)} %get-tuple-element.125.refs_1_, f32[1024,1024]{1,0:T(8,128)} %get-tuple-element.126.refs_2_, f32[1024,128]{1,0:T(8,128)} %copy.43.cos_ref.refs_3_.refs_7_, ...), custom_call_target="tpu_custom_call" | custom-call | flops 5950000128 | tf_op jit(solution)/shard_map/q_back/pallas_call | solution.py:563
  462.5 9.8 %convolution_convert_fusion.2 = bf16[512,2048]{1,0:T(8,128)(2,1)S(1)} fusion(bf16[512,3072]{1,0:T(8,128)(2,1)S(1)} %copy-done.1, bf16[3072,2048]{1,0:T(8,128)(2,1)} %param.22), kind=kOutput, calls=%fused_computation.4 | convolution fusion | flops 6443499520 | bytes 17825792 | tf_op jit(solution)/shard_map/dot_general | solution.py:66
  472.3 11.9 %broadcast_select_fusion = (bf16[512,2048]{1,0:T(8,128)(2,1)}, bf16[512,2048]{1,0:T(8,128)(2,1)}) fusion(bf16[512,2048]{1,0:T(8,128)(2,1)S(1)} %convolution_convert_fusion.2, pred[]{:T(512)S(6)} %eq.2, bf16[512,3072]{1,0:T(8,128)(2,1)S(1)} %copy-done.2, bf16[3072,2048]{1,0:T(8,128)(2,1)} %param.22), kind=kOutput, calls=%fused_computation.10 | convolution fusion | flops 6444548096 | bytes 22020096 | tf_op jit(solution)/shard_map/dot_general | solution.py:66
  493.4 7.8 %wgrad_send.8.refs_4_ = bf16[2,4,1024,128]{3,2,1,0:T(8,128)(2,1)} custom-call(bf16[512,1024]{1,0:T(8,128)(2,1)} %get-tuple-element.139.rest_2_.refs_0_, bf16[512,2048]{1,0:T(8,128)(2,1)} %get-tuple-element.108.refs_1_.h0_ref, bf16[512,1024]{1,0:T(8,128)(2,1)} %get-tuple-element.101.rest_3_.refs_2_, bf16[512,2048]{1,0:T(8,128)(2,1)} %get-tuple-element.110.refs_3_.h1_ref), custom_call_target="tpu_custom_call" | custom-call | flops 3955505664 | tf_op jit(solution)/shard_map/wgrad_send/pallas_call | solution.py:798
  507.5 7.6 %wgrad_send.9.refs_4_ = bf16[2,4,128,1024]{3,2,1,0:T(8,128)(2,1)} custom-call(bf16[1024,2048]{1,0:T(8,128)(2,1)} %get-tuple-element.141.refs_0_.refs_2_, bf16[1024,1024]{1,0:T(8,128)(2,1)} %get-tuple-element.129.refs_1_.refs_3_.refs_5_, bf16[1024,2048]{1,0:T(8,128)(2,1)} %get-tuple-element.141.refs_0_.refs_2_, ...), custom_call_target="tpu_custom_call" | custom-call | flops 3955505664 | tf_op jit(solution)/shard_map/wgrad_send/pallas_call | solution.py:798
  515.1 4.9 wgrad.16
  521.7 9.4 %wgrad.18 = bf16[1,4,128,3072]{3,2,1,0:T(8,128)(2,1)} custom-call(s32[5]{0:T(128)} %stack.114.s_ref, bf16[512,2048]{1,0:T(8,128)(2,1)} %get-tuple-element.123.refs_0_, bf16[512,3072]{1,0:T(8,128)(2,1)} %get-tuple-element.121.refs_1_, bf16[512,2048]{1,0:T(8,128)(2,1)} %get-tuple-element.113.refs_2_, bf16[512,3072]{1,0:T(8,128)(2,1)} %get-tuple-element.122.refs_3_, ...), custom_call_target="tpu_custom_call" | custom-call | flops 5886173184 | tf_op jit(solution)/shard_map/wgrad/pallas_call | solution.py:713
  531.8 22.4 %collective-permute-done.13.refs_1_ = bf16[1024,512]{1,0:T(8,128)(2,1)} collective-permute-done((bf16[1024,512]{1,0:T(8,128)(2,1)}, bf16[1024,512]{1,0:T(8,128)(2,1)}, u32[]{:S(2)}, u32[]{:S(2)}) %collective-permute-start.13) | collective-permute-done | bytes 1048608 | tf_op jit(solution)/shard_map/ppermute | solution.py:1043
  554.2 26.7 %collective-permute-done.15.refs_3_ = bf16[1024,512]{1,0:T(8,128)(2,1)} collective-permute-done((bf16[1024,512]{1,0:T(8,128)(2,1)}, bf16[1024,512]{1,0:T(8,128)(2,1)}, u32[]{:S(2)}, u32[]{:S(2)}) %collective-permute-start.15) | collective-permute-done | bytes 1048608 | tf_op jit(solution)/shard_map/ppermute | solution.py:1043
  580.9 12.5 %in_back.3 = (bf16[512,1024]{1,0:T(8,128)(2,1)}, bf16[512,2048]{1,0:T(8,128)(2,1)}, f32[8,128]{1,0:T(8,128)}, f32[8,2048]{1,0:T(8,128)}) custom-call(s32[1]{0:T(128)} %bitcast.2.s_ref, bf16[1024,512]{1,0:T(8,128)(2,1)} %get-tuple-element.132.refs_0_, bf16[1024,512]{1,0:T(8,128)(2,1)} %collective-permute-done.13.refs_1_, ...), custom_call_target="tpu_custom_call" | custom-call | flops 8750000128 | tf_op jit(solution)/shard_map/in_back/pallas_call | solution.py:613
  593.4 12.6 %in_back.2 = (bf16[512,1024]{1,0:T(8,128)(2,1)}, bf16[512,2048]{1,0:T(8,128)(2,1)}, f32[8,128]{1,0:T(8,128)}, f32[8,2048]{1,0:T(8,128)}) custom-call(s32[1]{0:T(128)} %bitcast.1.s_ref, bf16[1024,512]{1,0:T(8,128)(2,1)} %get-tuple-element.132.refs_0_, bf16[1024,512]{1,0:T(8,128)(2,1)} %collective-permute-done.13.refs_1_, ...), custom_call_target="tpu_custom_call" | custom-call | flops 8750000128 | tf_op jit(solution)/shard_map/in_back/pallas_call | solution.py:613
  606.0 13.8 %wgrad_send.11.refs_4_ = bf16[2,4,128,1024]{3,2,1,0:T(8,128)(2,1)} custom-call(bf16[1024,2048]{1,0:T(8,128)(2,1)} %get-tuple-element.141.refs_0_.refs_2_, bf16[512,1024]{1,0:T(8,128)(2,1)} %get-tuple-element.148.refs_1_, bf16[1024,2048]{1,0:T(8,128)(2,1)} %get-tuple-element.141.refs_0_.refs_2_, bf16[512,1024]{1,0:T(8,128)(2,1)} %get-tuple-element.149.refs_3_), custom_call_target="tpu_custom_call" | custom-call | flops 3955505664 | tf_op jit(solution)/shard_map/wgrad_send/pallas_call | solution.py:798
  619.8 4.9 wgrad.19
  624.7 5.0 wgrad.20
  634.3 6.0 wgrad.21
  647.7 7.4 %fusion = bf16[1,512,2048]{2,1,0:T(8,128)(2,1)} fusion(bf16[512,2048]{1,0:T(8,128)(2,1)} %collective-permute-done.11, bf16[512,2048]{1,0:T(8,128)(2,1)} %collective-permute-done.5.refs_2_, bf16[512,2048]{1,0:T(8,128)(2,1)} %collective-permute-done.7.refs_2_, bf16[512,2048]{1,0:T(8,128)(2,1)S(1)} %copy-done.12, ...), kind=kLoop, calls=%fused_computation.7 | loop fusion | flops 13631488 | bytes 18874368 | tf_op jit(solution)/shard_map/broadcast_in_dim | solution.py:1123
  655.2 14.8 %collective-permute-done.23.refs_5_ = bf16[1,4,128,1024]{3,2,1,0:T(8,128)(2,1)S(1)} collective-permute-done((bf16[1,4,128,1024]{3,2,1,0:T(8,128)(2,1)}, bf16[1,4,128,1024]{3,2,1,0:T(8,128)(2,1)S(1)}, u32[]{:S(2)}, u32[]{:S(2)}) %collective-permute-start.23) | collective-permute-done | bytes 1048608 | tf_op jit(solution)/shard_map/ppermute | solution.py:839
  670.9 5.1 wgrad.22
  684.7 15.3 %collective-permute-done.24 = bf16[2,128,1024]{2,1,0:T(8,128)(2,1)S(1)} collective-permute-done((bf16[2,128,1024]{2,1,0:T(8,128)(2,1)S(1)}, bf16[2,128,1024]{2,1,0:T(8,128)(2,1)S(1)}, u32[]{:S(2)}, u32[]{:S(2)}) %collective-permute-start.24) | collective-permute-done | bytes 524320 | tf_op jit(solution)/shard_map/ppermute | solution.py:864
  700.4 7.9 %final.1 = bf16[512,2048]{1,0:T(8,128)(2,1)} custom-call(bf16[512,2048]{1,0:T(8,128)(2,1)} %bitcast.123, bf16[512,2048]{1,0:T(8,128)(2,1)} %get-tuple-element.144.ga_ref, bf16[512,2048]{1,0:T(8,128)(2,1)} %collective-permute-done.18.gb_ref, bf16[512,2048]{1,0:T(8,128)(2,1)} %get-tuple-element.108.refs_1_.h0_ref, ...), custom_call_target="tpu_custom_call" | custom-call | flops 5600000000 | tf_op jit(solution)/shard_map/final/pallas_call | solution.py:882
  (207 shorter events, 126.3 us)
Async XLA Ops:
  7.2 716.7 %reduce-scatter.8.cloned.1.call-start = ((), (), s32[]{:S(2)}) async-start(), calls=%async_computation.5 | async-start | bytes 3932160 | tf_op jit(solution)/shard_map/reduce_scatter | solution.py:852
  7.2 49.0 %collective-permute-start = (bf16[512,2048]{1,0:T(8,128)(2,1)}, bf16[512,2048]{1,0:T(8,128)(2,1)}, u32[]{:S(2)}, u32[]{:S(2)}) collective-permute-start(bf16[512,2048]{1,0:T(8,128)(2,1)} %bitcast.120), channel_id=1, source_target_pairs={{0,1},{1,0},{2,3},{3,2},{4,5},{5,4},{6,7},{7,6},{8,9},{9,8},{10,11... | collective-permute-start | bytes 6291464 | tf_op jit(solution)/shard_map/ppermute | solution.py:908
  11.2 19.5 %copy-start.24 = (s32[1024]{0:T(1024)}, s32[1024]{0:T(1024)S(1)}, u32[]{:S(2)}) copy-start(s32[1024]{0:T(1024)S(1)} %get-tuple-element.186) | copy-start | bytes 12292
  21.9 25.9 %collective-permute-start.1 = (bf16[512,1024]{1,0:T(8,128)(2,1)}, bf16[512,1024]{1,0:T(8,128)(2,1)S(1)}, u32[]{:S(2)}, u32[]{:S(2)}) collective-permute-start(bf16[512,1024]{1,0:T(8,128)(2,1)} %get-tuple-element.92.rest_0_.rest_6_), channel_id=1, source_target_pairs={{0,2},{2,4},{4,6},{1,3},{3,5},{5,7},{8,10},{10,12},{12,14},{9,11},... | collective-permute-start | bytes 3145736 | tf_op jit(solution)/shard_map/ppermute | solution.py:961
  47.8 15.1 %copy-start.33 = (bf16[512,1024]{1,0:T(8,128)(2,1)}, bf16[512,1024]{1,0:T(8,128)(2,1)S(1)}, u32[]{:S(2)}) copy-start(bf16[512,1024]{1,0:T(8,128)(2,1)S(1)} %collective-permute-done.1.rest_0_.rest_8_) | copy-start | bytes 3145732
  47.8 64.9 %collective-permute-start.2 = (bf16[512,1024]{1,0:T(8,128)(2,1)S(1)}, bf16[512,1024]{1,0:T(8,128)(2,1)S(1)}, u32[]{:S(2)}, u32[]{:S(2)}) collective-permute-start(bf16[512,1024]{1,0:T(8,128)(2,1)S(1)} %collective-permute-done.1.rest_0_.rest_8_), channel_id=1, source_target_pairs={{0,2},{2,4},{4,6},{1,3},{3,5},{5,7},{8,10},{10,12},{12,14},{9,11},... | collective-permute-start | bytes 3145736 | tf_op jit(solution)/shard_map/ppermute | solution.py:961
  62.9 34.4 %collective-permute-start.3 = (bf16[512,1024]{1,0:T(8,128)(2,1)}, bf16[512,1024]{1,0:T(8,128)(2,1)}, u32[]{:S(2)}, u32[]{:S(2)}) collective-permute-start(bf16[512,1024]{1,0:T(8,128)(2,1)} %get-tuple-element.93.rest_1_.rest_7_), channel_id=1, source_target_pairs={{0,2},{2,4},{4,6},{1,3},{3,5},{5,7},{8,10},{10,12},{12,14},{9,11},... | collective-permute-start | bytes 3145736 | tf_op jit(solution)/shard_map/ppermute | solution.py:961
  67.6 80.1 %collective-permute-start.6 = (bf16[512,2048]{1,0:T(8,128)(2,1)S(1)}, bf16[512,2048]{1,0:T(8,128)(2,1)S(1)}, u32[]{:S(2)}, u32[]{:S(2)}) collective-permute-start(bf16[512,2048]{1,0:T(8,128)(2,1)S(1)} %bitcast.119), channel_id=1, source_target_pairs={{0,1},{1,0},{2,3},{3,2},{4,5},{5,4},{6,7},{7,6},{8,9},{9,8},{10,11... | collective-permute-start | bytes 6291464 | tf_op jit(solution)/shard_map/ppermute | solution.py:908
  97.4 23.9 %collective-permute-start.4 = (bf16[512,1024]{1,0:T(8,128)(2,1)}, bf16[512,1024]{1,0:T(8,128)(2,1)}, u32[]{:S(2)}, u32[]{:S(2)}) collective-permute-start(bf16[512,1024]{1,0:T(8,128)(2,1)} %collective-permute-done.3.rest_1_.rest_9_), channel_id=1, source_target_pairs={{0,2},{2,4},{4,6},{1,3},{3,5},{5,7},{8,10},{10,12},{12,14},{9,11},... | collective-permute-start | bytes 3145736 | tf_op jit(solution)/shard_map/ppermute | solution.py:961
  132.8 48.7 %collective-permute-start.5 = (bf16[512,2048]{1,0:T(8,128)(2,1)S(1)}, bf16[512,2048]{1,0:T(8,128)(2,1)}, u32[]{:S(2)}, u32[]{:S(2)}) collective-permute-start(bf16[512,2048]{1,0:T(8,128)(2,1)S(1)} %convolution_convert_fusion.4.refs_1_), channel_id=1, source_target_pairs={{0,1},{1,0},{2,3},{3,2},{4,5},{5,4},{6,7},{7,6},{8,9},{9,8},{10,11... | collective-permute-start | bytes 6291464 | tf_op jit(solution)/shard_map/ppermute | solution.py:908
  146.2 80.2 %collective-permute-start.7 = (bf16[512,2048]{1,0:T(8,128)(2,1)}, bf16[512,2048]{1,0:T(8,128)(2,1)}, u32[]{:S(2)}, u32[]{:S(2)}) collective-permute-start(bf16[512,2048]{1,0:T(8,128)(2,1)} %convolution_convert_fusion.3.refs_1_), channel_id=1, source_target_pairs={{0,1},{1,0},{2,3},{3,2},{4,5},{5,4},{6,7},{7,6},{8,9},{9,8},{10,11... | collective-permute-start | bytes 6291464 | tf_op jit(solution)/shard_map/ppermute | solution.py:908
  148.6 18.7 %copy-start = (bf16[1024,2048]{1,0:T(8,128)(2,1)}, bf16[1024,2048]{1,0:T(8,128)(2,1)S(1)}, u32[]{:S(2)}) copy-start(bf16[1024,2048]{1,0:T(8,128)(2,1)S(1)} %pad_maximum_fusion.refs_6_.refs_1_.refs_3_) | copy-start | bytes 12582916
  219.1 85.1 %collective-permute-start.9 = (bf16[512,2048]{1,0:T(8,128)(2,1)}, bf16[512,2048]{1,0:T(8,128)(2,1)S(1)}, u32[]{:S(2)}, u32[]{:S(2)}) collective-permute-start(bf16[512,2048]{1,0:T(8,128)(2,1)} %get-tuple-element.107.refs_3_), channel_id=1, source_target_pairs={{0,1},{1,0},{2,3},{3,2},{4,5},{5,4},{6,7},{7,6},{8,9},{9,8},{10,11... | collective-permute-start | bytes 6291464 | tf_op jit(solution)/shard_map/ppermute | solution.py:908
  264.2 53.0 %collective-permute-start.8 = (bf16[512,2048]{1,0:T(8,128)(2,1)}, bf16[512,2048]{1,0:T(8,128)(2,1)S(1)}, u32[]{:S(2)}, u32[]{:S(2)}) collective-permute-start(bf16[512,2048]{1,0:T(8,128)(2,1)} %get-tuple-element.106.refs_3_), channel_id=1, source_target_pairs={{0,1},{1,0},{2,3},{3,2},{4,5},{5,4},{6,7},{7,6},{8,9},{9,8},{10,11... | collective-permute-start | bytes 6291464 | tf_op jit(solution)/shard_map/ppermute | solution.py:908
  287.8 70.4 %collective-permute-start.16 = (bf16[1,4,3072,128]{3,2,1,0:T(8,128)(2,1)}, bf16[1,4,3072,128]{3,2,1,0:T(8,128)(2,1)S(1)}, u32[]{:S(2)}, u32[]{:S(2)}) collective-permute-start(bf16[1,4,3072,128]{3,2,1,0:T(8,128)(2,1)} %wgrad.17), channel_id=1, source_target_pairs={{0,16},{8,24},{16,0},{24,8},{1,17},{9,25},{17,1},{25,9},{2,18},{10... | collective-permute-start | bytes 9437192 | tf_op jit(solution)/shard_map/ppermute | solution.py:839
  369.0 358.5 %reduce-scatter.4.cloned.1.call-start = ((), (), s32[]{:S(2)}) async-start(), calls=%async_computation.3 | async-start | bytes 3932160 | tf_op jit(solution)/shard_map/reduce_scatter | solution.py:852
  371.4 71.3 %collective-permute-start.10 = (bf16[1,4,128,3072]{3,2,1,0:T(8,128)(2,1)}, bf16[1,4,128,3072]{3,2,1,0:T(8,128)(2,1)S(1)}, u32[]{:S(2)}, u32[]{:S(2)}) collective-permute-start(bf16[1,4,128,3072]{3,2,1,0:T(8,128)(2,1)} %wgrad.12), channel_id=1, source_target_pairs={{0,16},{8,24},{16,0},{24,8},{1,17},{9,25},{17,1},{25,9},{2,18},{10... | collective-permute-start | bytes 9437192 | tf_op jit(solution)/shard_map/ppermute | solution.py:839
  372.9 113.0 %collective-permute-start.12 = (bf16[1024,512]{1,0:T(8,128)(2,1)}, bf16[1024,512]{1,0:T(8,128)(2,1)}, u32[]{:S(2)}, u32[]{:S(2)}) collective-permute-start(bf16[1024,512]{1,0:T(8,128)(2,1)} %get-tuple-element.134), channel_id=1, source_target_pairs={{2,0},{4,2},{6,4},{3,1},{5,3},{7,5},{10,8},{12,10},{14,12},{11,9},... | collective-permute-start | bytes 3145736 | tf_op jit(solution)/shard_map/ppermute | solution.py:1043
  397.8 19.6 %copy-start.20 = (f32[8,2048]{1,0:T(8,128)S(1)}, f32[8,2048]{1,0:T(8,128)}, u32[]{:S(2)}) copy-start(f32[8,2048]{1,0:T(8,128)} %get-tuple-element.159) | copy-start | bytes 196612
  397.8 19.6 %copy-start.21 = (f32[8,2048]{1,0:T(8,128)S(1)}, f32[8,2048]{1,0:T(8,128)}, u32[]{:S(2)}) copy-start(f32[8,2048]{1,0:T(8,128)} %get-tuple-element.160) | copy-start | bytes 196612
  416.2 73.4 %collective-permute-start.14 = (bf16[1024,512]{1,0:T(8,128)(2,1)}, bf16[1024,512]{1,0:T(8,128)(2,1)}, u32[]{:S(2)}, u32[]{:S(2)}) collective-permute-start(bf16[1024,512]{1,0:T(8,128)(2,1)} %get-tuple-element.137), channel_id=1, source_target_pairs={{2,0},{4,2},{6,4},{3,1},{5,3},{7,5},{10,8},{12,10},{14,12},{11,9},... | collective-permute-start | bytes 3145736 | tf_op jit(solution)/shard_map/ppermute | solution.py:1043
  417.5 102.4 %collective-permute-start.17 = (bf16[1,4,128,3072]{3,2,1,0:T(8,128)(2,1)}, bf16[1,4,128,3072]{3,2,1,0:T(8,128)(2,1)S(1)}, u32[]{:S(2)}, u32[]{:S(2)}) collective-permute-start(bf16[1,4,128,3072]{3,2,1,0:T(8,128)(2,1)} %wgrad.13), channel_id=1, source_target_pairs={{0,16},{8,24},{16,0},{24,8},{1,17},{9,25},{17,1},{25,9},{2,18},{10... | collective-permute-start | bytes 9437192 | tf_op jit(solution)/shard_map/ppermute | solution.py:839
  454.1 275.8 %reduce-scatter.6.cloned.1.call-start = ((), (), s32[]{:S(2)}) async-start(), calls=%async_computation.4 | async-start | bytes 3932160 | tf_op jit(solution)/shard_map/reduce_scatter | solution.py:852
  472.3 13.5 %copy-start.16 = (bf16[1024,512]{1,0:T(8,128)(2,1)S(1)}, bf16[1024,512]{1,0:T(8,128)(2,1)}, u32[]{:S(2)}) copy-start(bf16[1024,512]{1,0:T(8,128)(2,1)} %get-tuple-element.133) | copy-start | bytes 3145732
  484.3 47.5 %collective-permute-start.11 = (bf16[512,2048]{1,0:T(8,128)(2,1)}, bf16[512,2048]{1,0:T(8,128)(2,1)}, u32[]{:S(2)}, u32[]{:S(2)}) collective-permute-start(bf16[512,2048]{1,0:T(8,128)(2,1)} %get-tuple-element.198), channel_id=1, source_target_pairs={{0,1},{1,0},{2,3},{3,2},{4,5},{5,4},{6,7},{7,6},{8,9},{9,8},{10,11... | collective-permute-start | bytes 6291464 | tf_op jit(solution)/shard_map/ppermute | solution.py:908
  488.3 65.9 %collective-permute-start.13 = (bf16[1024,512]{1,0:T(8,128)(2,1)}, bf16[1024,512]{1,0:T(8,128)(2,1)}, u32[]{:S(2)}, u32[]{:S(2)}) collective-permute-start(bf16[1024,512]{1,0:T(8,128)(2,1)} %add_convert_fusion.2), channel_id=1, source_target_pairs={{2,0},{4,2},{6,4},{3,1},{5,3},{7,5},{10,8},{12,10},{14,12},{11,9},... | collective-permute-start | bytes 3145736 | tf_op jit(solution)/shard_map/ppermute | solution.py:1043
  492.1 88.8 %collective-permute-start.15 = (bf16[1024,512]{1,0:T(8,128)(2,1)}, bf16[1024,512]{1,0:T(8,128)(2,1)}, u32[]{:S(2)}, u32[]{:S(2)}) collective-permute-start(bf16[1024,512]{1,0:T(8,128)(2,1)} %add_convert_fusion.1), channel_id=1, source_target_pairs={{2,0},{4,2},{6,4},{3,1},{5,3},{7,5},{10,8},{12,10},{14,12},{11,9},... | collective-permute-start | bytes 3145736 | tf_op jit(solution)/shard_map/ppermute | solution.py:1043
  506.1 118.6 %collective-permute-start.19 = (bf16[1,4,1024,128]{3,2,1,0:T(8,128)(2,1)}, bf16[1,4,1024,128]{3,2,1,0:T(8,128)(2,1)}, u32[]{:S(2)}, u32[]{:S(2)}) collective-permute-start(bf16[1,4,1024,128]{3,2,1,0:T(8,128)(2,1)} %wgrad.15), channel_id=1, source_target_pairs={{0,16},{8,24},{16,0},{24,8},{1,17},{9,25},{17,1},{25,9},{2,18},{10... | collective-permute-start | bytes 3145736 | tf_op jit(solution)/shard_map/ppermute | solution.py:839
  531.0 102.3 %collective-permute-start.20 = (bf16[1,4,128,1024]{3,2,1,0:T(8,128)(2,1)}, bf16[1,4,128,1024]{3,2,1,0:T(8,128)(2,1)S(1)}, u32[]{:S(2)}, u32[]{:S(2)}) collective-permute-start(bf16[1,4,128,1024]{3,2,1,0:T(8,128)(2,1)} %wgrad.16), channel_id=1, source_target_pairs={{0,16},{8,24},{16,0},{24,8},{1,17},{9,25},{17,1},{25,9},{2,18},{10... | collective-permute-start | bytes 3145736 | tf_op jit(solution)/shard_map/ppermute | solution.py:839
  631.6 16.0 %copy-start.22 = (f32[8,2048]{1,0:T(8,128)S(1)}, f32[8,2048]{1,0:T(8,128)}, u32[]{:S(2)}) copy-start(f32[8,2048]{1,0:T(8,128)} %get-tuple-element.157) | copy-start | bytes 196612
  631.6 16.0 %copy-start.23 = (f32[8,2048]{1,0:T(8,128)S(1)}, f32[8,2048]{1,0:T(8,128)}, u32[]{:S(2)}) copy-start(f32[8,2048]{1,0:T(8,128)} %get-tuple-element.158) | copy-start | bytes 196612
  631.6 16.0 %copy-start.27 = (f32[8,128]{1,0:T(8,128)S(1)}, f32[8,128]{1,0:T(8,128)}, u32[]{:S(2)}) copy-start(f32[8,128]{1,0:T(8,128)} %get-tuple-element.162) | copy-start | bytes 12292
  631.6 16.0 %copy-start.28 = (f32[8,128]{1,0:T(8,128)S(1)}, f32[8,128]{1,0:T(8,128)}, u32[]{:S(2)}) copy-start(f32[8,128]{1,0:T(8,128)} %get-tuple-element.163) | copy-start | bytes 12292
  631.7 47.5 %collective-permute-start.26 = (bf16[2,1024,128]{2,1,0:T(8,128)(2,1)}, bf16[2,1024,128]{2,1,0:T(8,128)(2,1)}, u32[]{:S(2)}, u32[]{:S(2)}) collective-permute-start(bf16[2,1024,128]{2,1,0:T(8,128)(2,1)} %pad_maximum_fusion.4), channel_id=1, source_target_pairs={{0,2},{2,0},{4,6},{6,4},{1,3},{3,1},{5,7},{7,5},{8,10},{10,8},{12,... | collective-permute-start | bytes 1572872 | tf_op jit(solution)/shard_map/ppermute | solution.py:864
  634.3 13.4 %copy-start.15 = (bf16[512,2048]{1,0:T(8,128)(2,1)S(1)}, bf16[512,2048]{1,0:T(8,128)(2,1)}, u32[]{:S(2)}) copy-start(bf16[512,2048]{1,0:T(8,128)(2,1)} %get-tuple-element.199) | copy-start | bytes 6291460
  642.4 39.4 %collective-permute-start.21 = (bf16[2,128,1024]{2,1,0:T(8,128)(2,1)}, bf16[2,128,1024]{2,1,0:T(8,128)(2,1)}, u32[]{:S(2)}, u32[]{:S(2)}) collective-permute-start(bf16[2,128,1024]{2,1,0:T(8,128)(2,1)} %pad_maximum_fusion.2), channel_id=1, source_target_pairs={{0,2},{2,0},{4,6},{6,4},{1,3},{3,1},{5,7},{7,5},{8,10},{10,8},{12,... | collective-permute-start | bytes 1572872 | tf_op jit(solution)/shard_map/ppermute | solution.py:864
  642.7 27.3 %collective-permute-start.23 = (bf16[1,4,128,1024]{3,2,1,0:T(8,128)(2,1)}, bf16[1,4,128,1024]{3,2,1,0:T(8,128)(2,1)S(1)}, u32[]{:S(2)}, u32[]{:S(2)}) collective-permute-start(bf16[1,4,128,1024]{3,2,1,0:T(8,128)(2,1)} %wgrad.19), channel_id=1, source_target_pairs={{0,16},{8,24},{16,0},{24,8},{1,17},{9,25},{17,1},{25,9},{2,18},{10... | collective-permute-start | bytes 3145736 | tf_op jit(solution)/shard_map/ppermute | solution.py:839
  646.3 54.1 %collective-permute-start.18 = (bf16[512,2048]{1,0:T(8,128)(2,1)}, bf16[512,2048]{1,0:T(8,128)(2,1)}, u32[]{:S(2)}, u32[]{:S(2)}) collective-permute-start(bf16[512,2048]{1,0:T(8,128)(2,1)} %get-tuple-element.146), channel_id=1, source_target_pairs={{0,1},{1,0},{2,3},{3,2},{4,5},{5,4},{6,7},{7,6},{8,9},{9,8},{10,11... | collective-permute-start | bytes 6291464 | tf_op jit(solution)/shard_map/ppermute | solution.py:908
  677.4 22.7 %collective-permute-start.24 = (bf16[2,128,1024]{2,1,0:T(8,128)(2,1)S(1)}, bf16[2,128,1024]{2,1,0:T(8,128)(2,1)S(1)}, u32[]{:S(2)}, u32[]{:S(2)}) collective-permute-start(bf16[2,128,1024]{2,1,0:T(8,128)(2,1)S(1)} %pad_maximum_fusion.3), channel_id=1, source_target_pairs={{0,2},{2,0},{4,6},{6,4},{1,3},{3,1},{5,7},{7,5},{8,10},{10,8},{12,... | collective-permute-start | bytes 1572872 | tf_op jit(solution)/shard_map/ppermute | solution.py:864
  679.2 21.0 %copy-start.4 = (bf16[1,4,128,1024]{3,2,1,0:T(8,128)(2,1)S(1)}, bf16[1,4,128,1024]{3,2,1,0:T(8,128)(2,1)}, u32[]{:S(2)}) copy-start(bf16[1,4,128,1024]{3,2,1,0:T(8,128)(2,1)} %wgrad.22) | copy-start | bytes 3145732
  680.4 27.9 %collective-permute-start.27 = (bf16[1024,128]{1,0:T(8,128)(2,1)S(1)}, bf16[1024,128]{1,0:T(8,128)(2,1)S(1)}, u32[]{:S(2)}, u32[]{:S(2)}) collective-permute-start(bf16[1024,128]{1,0:T(8,128)(2,1)S(1)} %fusion.2), channel_id=1, source_target_pairs={{0,4},{2,6},{4,0},{6,2},{1,5},{3,7},{5,1},{7,3},{8,12},{10,14},{12... | collective-permute-start | bytes 786440 | tf_op jit(solution)/shard_map/ppermute | solution.py:866
  683.0 30.1 %collective-permute-start.22 = (bf16[128,1024]{1,0:T(8,128)(2,1)S(1)}, bf16[128,1024]{1,0:T(8,128)(2,1)S(1)}, u32[]{:S(2)}, u32[]{:S(2)}) collective-permute-start(bf16[128,1024]{1,0:T(8,128)(2,1)S(1)} %fusion.10), channel_id=1, source_target_pairs={{0,4},{2,6},{4,0},{6,2},{1,5},{3,7},{5,1},{7,3},{8,12},{10,14},{12... | collective-permute-start | bytes 786440 | tf_op jit(solution)/shard_map/ppermute | solution.py:866
  700.2 16.8 %collective-permute-start.25 = (bf16[128,1024]{1,0:T(8,128)(2,1)S(1)}, bf16[128,1024]{1,0:T(8,128)(2,1)S(1)}, u32[]{:S(2)}, u32[]{:S(2)}) collective-permute-start(bf16[128,1024]{1,0:T(8,128)(2,1)S(1)} %fusion.6), channel_id=1, source_target_pairs={{0,4},{2,6},{4,0},{6,2},{1,5},{3,7},{5,1},{7,3},{8,12},{10,14},{12... | collective-permute-start | bytes 786440 | tf_op jit(solution)/shard_map/ppermute | solution.py:866
  708.3 1.2 collective-permute-start.28
  709.5 4.5 collective-permute-start.29
  714.0 3.8 collective-permute-start.30
  717.9 4.7 collective-permute-start.31
  722.6 3.8 collective-permute-start.32
  (23 other events, 135.2 us)
Sparse Core Ops, SparseCore 0:
  369.1 105.2 reduce-scatter.7
  476.7 90.2 reduce-scatter.3
  569.3 66.0 reduce-scatter.5

commit v3 on v2

--- a/solution.py
+++ b/solution.py
@@ -19,21 +19,26 @@
 F32 = jnp.float32
 MIB = 1 << 20
 PLAN = {
+    "c_fin": 0.3,
+    "c_in": 0.3,
     "c_mid": 1.0,
-    "e_dn_d0": 1,
+    "c_wg": 1.6,
     "e_dp_q": 1,
     "e_fb0_gf": 1,
     "e_fb1_gf": 1,
     "e_fb1_uf": 1,
+    "e_fb1_us": 1,
     "e_fin_qn": 1,
-    "e_gn_d1": 1,
+    "e_gf_early": 1,
+    "e_gs_m0": 1,
     "e_in_cd": 1,
     "e_in_dp": 1,
     "e_in_qf": 1,
     "e_in_un": 1,
     "e_kf_un": 1,
+    "e_kv_hop": 1,
     "e_m1_gf": 1,
-    "e_m1_m0": 1,
+    "e_m1_gs": 1,
     "e_on_kf": 1,
     "e_pk_fin": 1,
     "e_pk_kc": 1,
@@ -42,8 +47,10 @@
     "e_qb_uf": 1,
     "e_qf_of": 1,
     "e_qn_on": 1,
+    "e_qs_os": 1,
+    "e_un_qf": 1,
     "scale": 0.7,
-    "serial": 1,
+    "serial": 3,
 }
 
 
@@ -1053,21 +1060,21 @@
                 t += [uf]
     out_w = shrink([(outs[c], zero, gh[c], zero) for c in range(2)], False, up, bool(O('p_out',1)))
     if not O('e_fb1_uf'):
-        uf = up.far(dqs[-1])
-    gn_ = gate.near(*opt('e_gn_d1', dqs[-1]), *opt('e_gn_uf', uf), *opt('e_gn_hop', *first_hops))
+        uf = up.far(dqs[-1], *opt('e_uf_h0', first_hops[0] if first_hops else dqs[0]))
+    gn_ = gate.near(*opt('e_gn_d1', dqs[-1]), *opt('e_gn_uf', uf), *opt('e_gn_hop', *first_hops), *opt('e_gn_h0', first_hops[0] if first_hops else dqs[0]))
     dq_low, g_qn = q_back(
         dqs, q_raw, cosine, sine,
-        after(row(query_norm), *opt('e_qb_uf', uf), *opt('e_qb_gn', gn_), *opt('e_qb_hop', *first_hops)), tm,
+        after(row(query_norm), *opt('e_qb_uf', uf), *opt('e_qb_gn', gn_), *opt('e_qb_hop', *first_hops), *opt('e_qb_h0', first_hops[0] if first_hops else dqs[0])), tm,
     )
     query_w = shrink([(attn_in, chunk(c), dq_low, chunk(c)) for c in range(2)], True, out_w, bool(O('p_q',1)))
-    os_ = out_w.send(dq_low)
+    os_ = out_w.send(dq_low, *opt('e_os_gn', gn_))
     qs_ = query_w.send(*opt('e_qs_os', os_))
     of_ = out_w.far(*opt('e_of_qs', qs_))
     qf_ = query_w.far(*opt('e_qf_of', of_))
     w_down_later = after(w_down, dq_low) if O('e_dp_q') else after(w_down, gh[1]) if O('e_dp_m') else w_down
     downs = [dot(hidden[c], w_down_later).astype(BF) for c in range(2)]
     come_down = swap(pick(downs[1], downs[0])) if nt == 2 else downs[0]
-    un = up.near(*opt('e_un_qf', qf_), *opt('e_un_d1', dqs[-1]))
+    un = up.near(*opt('e_un_qf', qf_), *opt('e_un_d1', dqs[-1]), *opt('e_un_dp', *downs), *opt('e_un_of', of_))
     t = opt('e_in_qf', qf_) + opt('e_in_dp', *downs) + opt('e_in_cd', come_down) + opt('e_in_un', un)
 
     lows, gas, g_kn, g_norm_one = [None] * 2, [None] * 2, [], []
@@ -1082,7 +1089,7 @@
     own_half = lambda: lax.axis_index("tensor")
     half_of = lambda n: chunk(n) if nt != 2 else own_half if n == 0 else lambda: 1 - own_half()
     kv_w = shrink([(attn_in, half_of(n), lows[n], zero) for n in range(2)], True, query_w, bool(O('p_kv',1)))
-    ks_ = kv_w.send()
+    ks_ = kv_w.send(*opt('e_ks_un', un))
     kf_ = kv_w.far(*opt('e_kf_un', un))
     on_ = out_w.near(*opt('e_on_kf', kf_))
     qn_ = query_w.near(*opt('e_qn_on', on_))
@@ -1118,7 +1125,7 @@
     packed = jnp.concatenate(
         [fold(g_norm_one), fold(g_norm_two) * share, jnp.sum(g_qn, axis=0), fold(g_kn)]
     )
-    packed = total_sum(after(packed, *opt('e_pk_fin', grad_tokens), *opt('e_pk_kn', kn_), *opt('e_pk_kc', kv_w.come)), axes)
+    packed = total_sum(after(packed, *opt('e_pk_fin', grad_tokens), *opt('e_pk_kf', kf_), *opt('e_pk_kn', kn_), *opt('e_pk_kc', kv_w.come)), axes)
     return (
         result.astype(BF)[None], grad_tokens[None], g_query, g_kv[:, :kv_cut], g_kv[:, kv_cut:],
         g_out, g_gate, g_up, g_down,
@@ -1130,8 +1137,13 @@
     for name, size in sizes:
         step = 1
         while step < size:
-            v = v + lax.ppermute(v, name, [(k, k ^ step) for k in range(size)])
-            step *= 2
+            come = lambda k: lax.ppermute(v, name, [(i, i ^ k * step) for i in range(size)])
+            if 4 * step <= size:
+                v = (v + come(1)) + (come(2) + come(3))
+                step *= 4
+            else:
+                v = v + come(1)
+                step *= 2
     return v
 
 

time: 749 us -> 730 us (0.975)
  waiting for transfers between devices: 156 us -> 148 us
    ppermute x6, waiting for transfers between devices: 39.5 us -> 0.02 us  [far(): lax.ppermute(after(out, *first), 'dp', [(k, k ^ 2) for k in range(self.nd)])]
    ppermute x3, waiting for transfers between devices: 15.3 us -> 33.3 us  [finish(): lax.ppermute(first, 'seq', [(k, k ^ 1) for k in range(ns)]).astype(F32)]
    ppermute x8, waiting for transfers between devices: 25 us -> 33.5 us  [per_device(): swap = lambda v: lax.ppermute(v, 'tensor', [(0, 1), (1, 0)])]
  transfers between devices with their start and end apart: 36 -> 38, of which waited for: 17 -> 15; matrix products, arithmetic and copies ran while one was open for 13% -> 13% of each run, Pallas kernels for 53% -> 55%
where the time goes in v3:
time: 730 us; the launch traced here: 720 us
  Pallas kernels  396 us (54%)
  waiting for transfers between devices  148 us (20%)
  starting transfers between devices  57.1 us (8%)
  matrix products  48.8 us (7%)
  other arithmetic  29.4 us (4%)
  local copies, waits for them, and re-layouts  23.3 us (3%)
  between operations  17.3 us (2%)
    pallas_call x12, Pallas kernels, wgrad(): pl.pallas_call(functools.partial(wgrad_kernel, nt=nt, na=len(addends), ro...  83.8 us
    pallas_call x2, Pallas kernels, mlp(): pl.pallas_call(functools.partial(mlp_kernel, np_=len(parts)), grid=(ff //...  75.2 us
    pallas_call x6, Pallas kernels, wgrad_send(): pl.pallas_call(functools.partial(wgrad_send_kernel, nt=nt, row_type=row_t...  70.4 us
    ppermute x4, waiting for transfers between devices, per_device(): come = lax.ppermute(send, 'seq', behind)  55.9 us
    dot_general x5, matrix products, dot(): lax.dot_general(a, b, (((ca,), (cb,)), ((), ())), preferred_element_type=...  48.8 us
    pallas_call x4, Pallas kernels, flash_fwd(): pl.pallas_call(functools.partial(flash_fwd_kernel, nseg=len(segs), prior=...  39.7 us
    pallas_call x2, Pallas kernels, flash_bwd(): pl.pallas_call(functools.partial(flash_bwd_kernel, nc=nc, ns=len(segs), n...  36.5 us
    ppermute x8, waiting for transfers between devices, per_device(): swap = lambda v: lax.ppermute(v, 'tensor', [(0, 1), (1, 0)])  33.5 us
  transfers between devices with their start and end apart: 38, of which 15 were waited for; matrix products, arithmetic and copies ran while one was open for 13% of the time, Pallas kernels for 55%

profile of v3, /device:TPU:0, one launch (start us, length us, event | category | flops | bytes accessed | tf_op | source)
XLA Modules:
  0.0 720.4 jit_solution(12825488713096456940)
XLA Ops:
  15.4 6.5 project_kv.2
  35.5 12.3 %collective-permute-done.1.rest_0_.rest_8_ = bf16[512,1024]{1,0:T(8,128)(2,1)S(1)} collective-permute-done((bf16[512,1024]{1,0:T(8,128)(2,1)}, bf16[512,1024]{1,0:T(8,128)(2,1)S(1)}, u32[]{:S(2)}, u32[]{:S(2)}) %collective-permute-start.1) | collective-permute-done | bytes 1048608 | tf_op jit(solution)/shard_map/ppermute | solution.py:968
  56.2 6.7 project_kv.3
  69.1 13.2 %project_q.1 = (bf16[1024,2048]{1,0:T(8,128)(2,1)}, bf16[1024,2048]{1,0:T(8,128)(2,1)}, bf16[1024,1024]{1,0:T(8,128)(2,1)}, f32[1024,1024]{1,0:T(8,128)}) custom-call(s32[2]{0:T(128)} %pad_add_fusion.10.s_ref, bf16[512,2048]{1,0:T(8,128)(2,1)} %bitcast.118, bf16[512,2048]{1,0:T(8,128)(2,1)} %collective-permute-done.xb_ref.x_ref, f32[1,2048]{1,0:T(1,128)} %bitcast.128, ...), custom_call_target="tpu_custom_call" | custom-call | flops 9100000256 | tf_op jit(solution)/shard_map/project_q/pallas_call | solution.py:167
  82.3 15.0 %flash_fwd.4 = (f32[1024,1024]{1,0:T(8,128)}, f32[1024,512]{1,0:T(8,128)}) custom-call(s32[10]{0:T(128)} %concatenate.27.s_ref, bf16[1024,1024]{1,0:T(8,128)(2,1)} %get-tuple-element.88.q_ref, s32[1024,128]{1,0:T(8,128)} %broadcast_in_dim.29.st_ref, bf16[512,1024]{1,0:T(8,128)(2,1)} %get-tuple-element.89.rest_0_.rest_6_, ...), custom_call_target="tpu_custom_call" | custom-call | flops 13299999744 | tf_op jit(solution)/shard_map/flash_fwd/pallas_call | solution.py:278
  101.8 11.3 %flash_fwd.5 = (f32[1024,1024]{1,0:T(8,128)}, f32[1024,512]{1,0:T(8,128)}) custom-call(s32[10]{0:T(128)} %concatenate.26.s_ref, bf16[1024,1024]{1,0:T(8,128)(2,1)} %get-tuple-element.88.q_ref, s32[1024,128]{1,0:T(8,128)} %broadcast_in_dim.29.st_ref, bf16[512,1024]{1,0:T(8,128)(2,1)} %copy-done.29, bf16[512,1024]{1,0:T(8,128)(2,1)} %collective-permute-done.3.rest_1_.rest_9_, ...), custom_call_target="tpu_custom_call" | custom-call | flops 13299999744 | tf_op jit(solution)/shard_map/flash_fwd/pallas_call | solution.py:278
  113.2 8.0 %collective-permute-done.4.rest_1_.rest_11_ = bf16[512,1024]{1,0:T(8,128)(2,1)} collective-permute-done((bf16[512,1024]{1,0:T(8,128)(2,1)}, bf16[512,1024]{1,0:T(8,128)(2,1)}, u32[]{:S(2)}, u32[]{:S(2)}) %collective-permute-start.4) | collective-permute-done | bytes 1048608 | tf_op jit(solution)/shard_map/ppermute | solution.py:968
  121.2 6.7 flash_fwd.6
  133.4 6.6 flash_fwd.7
  140.0 6.2 convolution_convert_fusion.3.refs_1_
  148.6 18.7 %convolution_convert_fusion.refs_4_ = bf16[1024,3072]{1,0:T(8,128)(2,1)} fusion(bf16[1024,2048]{1,0:T(8,128)(2,1)S(1)} %pad_maximum_fusion.refs_6_.refs_1_.refs_3_, bf16[3072,2048]{1,0:T(8,128)(2,1)} %param.22), kind=kOutput, calls=%fused_computation | convolution fusion | flops 12888047616 | bytes 23068672 | tf_op jit(solution)/shard_map/dot_general | solution.py:73
  167.3 14.3 %collective-permute-done.5.refs_2_ = bf16[512,2048]{1,0:T(8,128)(2,1)} collective-permute-done((bf16[512,2048]{1,0:T(8,128)(2,1)S(1)}, bf16[512,2048]{1,0:T(8,128)(2,1)}, u32[]{:S(2)}, u32[]{:S(2)}) %collective-permute-start.5) | collective-permute-done | bytes 2097184 | tf_op jit(solution)/shard_map/ppermute | solution.py:915
  181.5 37.5 %mlp.2 = (bf16[512,2048]{1,0:T(8,128)(2,1)}, bf16[512,3072]{1,0:T(8,128)(2,1)}, bf16[512,3072]{1,0:T(8,128)(2,1)}, bf16[512,3072]{1,0:T(8,128)(2,1)}, bf16[512,2048]{1,0:T(8,128)(2,1)}) custom-call(bf16[1024,2048]{1,0:T(8,128)(2,1)} %get-tuple-element.87.refs_0_.refs_6_, bf16[512,2048]{1,0:T(8,128)(2,1)} %copy-done.8, ...), custom_call_target="tpu_custom_call" | custom-call | flops 26599999488 | tf_op jit(solution)/shard_map/mlp/pallas_call | solution.py:459
  219.7 6.8 collective-permute-done.7.refs_2_
  226.5 37.7 %mlp.3 = (bf16[512,2048]{1,0:T(8,128)(2,1)}, bf16[512,3072]{1,0:T(8,128)(2,1)}, bf16[512,3072]{1,0:T(8,128)(2,1)}, bf16[512,3072]{1,0:T(8,128)(2,1)}, bf16[512,2048]{1,0:T(8,128)(2,1)}) custom-call(bf16[1024,2048]{1,0:T(8,128)(2,1)} %get-tuple-element.87.refs_0_.refs_6_, bf16[512,2048]{1,0:T(8,128)(2,1)} %convolution_convert_fusion.3.refs_1_, ...), custom_call_target="tpu_custom_call" | custom-call | flops 26599999488 | tf_op jit(solution)/shard_map/mlp/pallas_call | solution.py:459
  264.8 14.8 %wgrad_send.11.refs_4_ = bf16[2,4,3072,128]{3,2,1,0:T(8,128)(2,1)} custom-call(bf16[512,3072]{1,0:T(8,128)(2,1)} %get-tuple-element.101.refs_0_, bf16[1024,2048]{1,0:T(8,128)(2,1)} %copy-done.3, bf16[512,3072]{1,0:T(8,128)(2,1)} %get-tuple-element.127.refs_2_, bf16[1024,2048]{1,0:T(8,128)(2,1)} %copy-done.3), custom_call_target="tpu_custom_call" | custom-call | flops 9066516480 | tf_op jit(solution)/shard_map/wgrad_send/pallas_call | solution.py:805
  279.6 8.2 %wgrad.22 = bf16[1,4,3072,128]{3,2,1,0:T(8,128)(2,1)} custom-call(s32[5]{0:T(128)} %get-tuple-element.184.s_ref, bf16[512,3072]{1,0:T(8,128)(2,1)} %get-tuple-element.101.refs_0_, bf16[1024,2048]{1,0:T(8,128)(2,1)} %copy-done.3, bf16[512,3072]{1,0:T(8,128)(2,1)} %get-tuple-element.127.refs_2_, bf16[1024,2048]{1,0:T(8,128)(2,1)} %copy-done.3, ...), custom_call_target="tpu_custom_call" | custom-call | flops 9417876480 | tf_op jit(solution)/shard_map/wgrad/pallas_call | solution.py:720
  290.6 11.3 %mid_backward.2 = (bf16[512,2048]{1,0:T(8,128)(2,1)}, bf16[512,1024]{1,0:T(8,128)(2,1)}, f32[8,2048]{1,0:T(8,128)}) custom-call(bf16[1024,2048]{1,0:T(8,128)(2,1)} %get-tuple-element.87.refs_0_.refs_6_, bf16[512,2048]{1,0:T(8,128)(2,1)} %copy-done.8, bf16[512,2048]{1,0:T(8,128)(2,1)} %collective-permute-done.5.refs_2_, ...), custom_call_target="tpu_custom_call" | custom-call | flops 7699999744 | tf_op jit(solution)/shard_map/mid_backward/pallas_call | solution.py:518
  301.9 15.3 %wgrad_send.6.refs_4_ = bf16[2,4,128,3072]{3,2,1,0:T(8,128)(2,1)} custom-call(bf16[512,2048]{1,0:T(8,128)(2,1)} %get-tuple-element.118.refs_0_, bf16[512,3072]{1,0:T(8,128)(2,1)} %get-tuple-element.103.refs_1_, bf16[512,2048]{1,0:T(8,128)(2,1)} %get-tuple-element.105.refs_2_, bf16[512,3072]{1,0:T(8,128)(2,1)} %get-tuple-element.106.refs_3_), custom_call_target="tpu_custom_call" | custom-call | flops 9066516480 | tf_op jit(solution)/shard_map/wgrad_send/pallas_call | solution.py:805
  317.2 8.7 %wgrad.12 = bf16[1,4,128,3072]{3,2,1,0:T(8,128)(2,1)} custom-call(s32[5]{0:T(128)} %stack.112.s_ref, bf16[512,2048]{1,0:T(8,128)(2,1)} %get-tuple-element.118.refs_0_, bf16[512,3072]{1,0:T(8,128)(2,1)} %get-tuple-element.103.refs_1_, bf16[512,2048]{1,0:T(8,128)(2,1)} %get-tuple-element.105.refs_2_, bf16[512,3072]{1,0:T(8,128)(2,1)} %get-tuple-element.106.refs_3_, ...), custom_call_target="tpu_custom_call" | custom-call | flops 9417876480 | tf_op jit(solution)/shard_map/wgrad/pallas_call | solution.py:720
  327.8 11.3 %mid_backward.3 = (bf16[512,2048]{1,0:T(8,128)(2,1)}, bf16[512,1024]{1,0:T(8,128)(2,1)}, f32[8,2048]{1,0:T(8,128)}) custom-call(bf16[1024,2048]{1,0:T(8,128)(2,1)} %get-tuple-element.87.refs_0_.refs_6_, bf16[512,2048]{1,0:T(8,128)(2,1)} %convolution_convert_fusion.3.refs_1_, bf16[512,2048]{1,0:T(8,128)(2,1)} %collective-permute-done.7.refs_2_, ...), custom_call_target="tpu_custom_call" | custom-call | flops 7699999744 | tf_op jit(solution)/shard_map/mid_backward/pallas_call | solution.py:518
  339.7 18.2 %flash_bwd.2 = (f32[1024,512]{1,0:T(8,128)}, bf16[1024,512]{1,0:T(8,128)(2,1)}, bf16[1024,512]{1,0:T(8,128)(2,1)}, bf16[1024,512]{1,0:T(8,128)(2,1)}) custom-call(s32[14]{0:T(128)} %concatenate.30.s_ref, bf16[1024,1024]{1,0:T(8,128)(2,1)} %get-tuple-element.88.q_ref, s32[8,1024]{1,0:T(8,128)} %broadcast_in_dim.32.st_ref, ...), custom_call_target="tpu_custom_call" | custom-call | flops 25200001024 | tf_op jit(solution)/shard_map/flash_bwd/pallas_call | solution.py:384
  360.9 9.0 %wgrad.23 = bf16[1,4,3072,128]{3,2,1,0:T(8,128)(2,1)} custom-call(s32[5]{0:T(128)} %get-tuple-element.185.s_ref, bf16[512,3072]{1,0:T(8,128)(2,1)} %get-tuple-element.101.refs_0_, bf16[1024,2048]{1,0:T(8,128)(2,1)} %copy-done.3, bf16[512,3072]{1,0:T(8,128)(2,1)} %get-tuple-element.127.refs_2_, bf16[1024,2048]{1,0:T(8,128)(2,1)} %copy-done.3, ...), custom_call_target="tpu_custom_call" | custom-call | flops 9417876480 | tf_op jit(solution)/shard_map/wgrad/pallas_call | solution.py:720
  369.9 15.0 %wgrad_send.7.refs_4_ = bf16[2,4,128,3072]{3,2,1,0:T(8,128)(2,1)} custom-call(bf16[512,2048]{1,0:T(8,128)(2,1)} %get-tuple-element.118.refs_0_, bf16[512,3072]{1,0:T(8,128)(2,1)} %get-tuple-element.119.refs_1_, bf16[512,2048]{1,0:T(8,128)(2,1)} %get-tuple-element.105.refs_2_, bf16[512,3072]{1,0:T(8,128)(2,1)} %get-tuple-element.120.refs_3_), custom_call_target="tpu_custom_call" | custom-call | flops 9066516480 | tf_op jit(solution)/shard_map/wgrad_send/pallas_call | solution.py:805
  384.9 8.7 %wgrad.13 = bf16[1,4,128,3072]{3,2,1,0:T(8,128)(2,1)} custom-call(s32[5]{0:T(128)} %stack.112.s_ref, bf16[512,2048]{1,0:T(8,128)(2,1)} %get-tuple-element.118.refs_0_, bf16[512,3072]{1,0:T(8,128)(2,1)} %get-tuple-element.119.refs_1_, bf16[512,2048]{1,0:T(8,128)(2,1)} %get-tuple-element.105.refs_2_, bf16[512,3072]{1,0:T(8,128)(2,1)} %get-tuple-element.120.refs_3_, ...), custom_call_target="tpu_custom_call" | custom-call | flops 9417876480 | tf_op jit(solution)/shard_map/wgrad/pallas_call | solution.py:720
  393.6 18.3 %flash_bwd.3 = (f32[1024,512]{1,0:T(8,128)}, bf16[1024,512]{1,0:T(8,128)(2,1)}, bf16[1024,512]{1,0:T(8,128)(2,1)}, bf16[1024,512]{1,0:T(8,128)(2,1)}) custom-call(s32[14]{0:T(128)} %concatenate.30.s_ref, bf16[1024,1024]{1,0:T(8,128)(2,1)} %get-tuple-element.88.q_ref, s32[8,1024]{1,0:T(8,128)} %broadcast_in_dim.32.st_ref, ...), custom_call_target="tpu_custom_call" | custom-call | flops 25200001024 | tf_op jit(solution)/shard_map/flash_bwd/pallas_call | solution.py:384
  418.8 55.9 %collective-permute-done.14 = bf16[1024,512]{1,0:T(8,128)(2,1)} collective-permute-done((bf16[1024,512]{1,0:T(8,128)(2,1)}, bf16[1024,512]{1,0:T(8,128)(2,1)}, u32[]{:S(2)}, u32[]{:S(2)}) %collective-permute-start.14) | collective-permute-done | bytes 1048608 | tf_op jit(solution)/shard_map/ppermute | solution.py:1050
  478.4 9.5 %wgrad.14 = bf16[1,4,128,3072]{3,2,1,0:T(8,128)(2,1)} custom-call(s32[5]{0:T(128)} %stack.114.s_ref, bf16[512,2048]{1,0:T(8,128)(2,1)} %get-tuple-element.118.refs_0_, bf16[512,3072]{1,0:T(8,128)(2,1)} %get-tuple-element.103.refs_1_, bf16[512,2048]{1,0:T(8,128)(2,1)} %get-tuple-element.105.refs_2_, bf16[512,3072]{1,0:T(8,128)(2,1)} %get-tuple-element.106.refs_3_, ...), custom_call_target="tpu_custom_call" | custom-call | flops 9417876480 | tf_op jit(solution)/shard_map/wgrad/pallas_call | solution.py:720
  488.0 8.3 %q_back.1 = (bf16[1024,1024]{1,0:T(8,128)(2,1)}, f32[8,128]{1,0:T(8,128)}) custom-call(f32[1024,512]{1,0:T(8,128)} %get-tuple-element.117.refs_0_, f32[1024,512]{1,0:T(8,128)} %get-tuple-element.122.refs_1_, f32[1024,1024]{1,0:T(8,128)} %get-tuple-element.123.refs_2_, f32[1024,128]{1,0:T(8,128)} %copy.43.cos_ref.refs_3_.refs_7_, ...), custom_call_target="tpu_custom_call" | custom-call | flops 5950000128 | tf_op jit(solution)/shard_map/q_back/pallas_call | solution.py:570
  496.4 10.7 %convolution_convert_fusion.2 = bf16[512,2048]{1,0:T(8,128)(2,1)S(1)} fusion(bf16[512,3072]{1,0:T(8,128)(2,1)} %get-tuple-element.101.refs_0_, bf16[3072,2048]{1,0:T(8,128)(2,1)} %param.22), kind=kOutput, calls=%fused_computation.4 | convolution fusion | flops 6443499520 | bytes 17825792 | tf_op jit(solution)/shard_map/dot_general | solution.py:73
  507.2 8.3 %broadcast_select_fusion = (bf16[512,2048]{1,0:T(8,128)(2,1)}, bf16[512,2048]{1,0:T(8,128)(2,1)}) fusion(bf16[512,2048]{1,0:T(8,128)(2,1)S(1)} %convolution_convert_fusion.2, pred[]{:T(512)S(6)} %eq.2, bf16[512,3072]{1,0:T(8,128)(2,1)S(1)} %copy-done.32, bf16[3072,2048]{1,0:T(8,128)(2,1)S(1)} %bitcast.136), kind=kOutput, calls=%fused_computation.10 | convolution fusion | flops 6444548096 | bytes 22020096 | tf_op jit(solution)/shard_map/dot_general | solution.py:73
  517.0 9.0 %wgrad_send.8.refs_4_ = bf16[2,4,1024,128]{3,2,1,0:T(8,128)(2,1)} custom-call(bf16[512,1024]{1,0:T(8,128)(2,1)} %get-tuple-element.136.rest_2_.refs_0_, bf16[512,2048]{1,0:T(8,128)(2,1)} %get-tuple-element.108.refs_1_.h0_ref, bf16[512,1024]{1,0:T(8,128)(2,1)} %get-tuple-element.99.rest_3_.refs_2_, bf16[512,2048]{1,0:T(8,128)(2,1)} %get-tuple-element.135.refs_3_.h1_ref), custom_call_target="tpu_custom_call" | custom-call | flops 3955505664 | tf_op jit(solution)/shard_map/wgrad_send/pallas_call | solution.py:805
  530.7 7.6 %wgrad_send.9.refs_4_ = bf16[2,4,128,1024]{3,2,1,0:T(8,128)(2,1)} custom-call(bf16[1024,2048]{1,0:T(8,128)(2,1)} %get-tuple-element.139.refs_0_.refs_2_, bf16[1024,1024]{1,0:T(8,128)(2,1)} %get-tuple-element.125.refs_1_.refs_3_.refs_5_, bf16[1024,2048]{1,0:T(8,128)(2,1)} %get-tuple-element.139.refs_0_.refs_2_, ...), custom_call_target="tpu_custom_call" | custom-call | flops 3955505664 | tf_op jit(solution)/shard_map/wgrad_send/pallas_call | solution.py:805
  538.3 4.9 wgrad.16
  545.2 9.4 %wgrad.17 = bf16[1,4,128,3072]{3,2,1,0:T(8,128)(2,1)} custom-call(s32[5]{0:T(128)} %stack.114.s_ref, bf16[512,2048]{1,0:T(8,128)(2,1)} %get-tuple-element.118.refs_0_, bf16[512,3072]{1,0:T(8,128)(2,1)} %get-tuple-element.119.refs_1_, bf16[512,2048]{1,0:T(8,128)(2,1)} %get-tuple-element.105.refs_2_, bf16[512,3072]{1,0:T(8,128)(2,1)} %get-tuple-element.120.refs_3_, ...), custom_call_target="tpu_custom_call" | custom-call | flops 9417876480 | tf_op jit(solution)/shard_map/wgrad/pallas_call | solution.py:720
  554.7 8.5 %collective-permute-done.11 = bf16[512,2048]{1,0:T(8,128)(2,1)} collective-permute-done((bf16[512,2048]{1,0:T(8,128)(2,1)}, bf16[512,2048]{1,0:T(8,128)(2,1)}, u32[]{:S(2)}, u32[]{:S(2)}) %collective-permute-start.11) | collective-permute-done | bytes 2097184 | tf_op jit(solution)/shard_map/ppermute | solution.py:915
  564.4 13.0 %in_back.3 = (bf16[512,1024]{1,0:T(8,128)(2,1)}, bf16[512,2048]{1,0:T(8,128)(2,1)}, f32[8,128]{1,0:T(8,128)}, f32[8,2048]{1,0:T(8,128)}) custom-call(s32[1]{0:T(128)} %bitcast.2.s_ref, bf16[1024,512]{1,0:T(8,128)(2,1)} %get-tuple-element.128.refs_0_, bf16[1024,512]{1,0:T(8,128)(2,1)} %copy-done.4, bf16[1024,512]{1,0:T(8,128)(2,1)} %get-tuple-element.131.refs_2_, ...), custom_call_target="tpu_custom_call" | custom-call | flops 2624999936 | tf_op jit(solution)/shard_map/in_back/pallas_call | solution.py:620
  577.4 12.5 %in_back.2 = (bf16[512,1024]{1,0:T(8,128)(2,1)}, bf16[512,2048]{1,0:T(8,128)(2,1)}, f32[8,128]{1,0:T(8,128)}, f32[8,2048]{1,0:T(8,128)}) custom-call(s32[1]{0:T(128)} %bitcast.1.s_ref, bf16[1024,512]{1,0:T(8,128)(2,1)} %get-tuple-element.128.refs_0_, bf16[1024,512]{1,0:T(8,128)(2,1)} %copy-done.4, bf16[1024,512]{1,0:T(8,128)(2,1)} %get-tuple-element.131.refs_2_, ...), custom_call_target="tpu_custom_call" | custom-call | flops 2624999936 | tf_op jit(solution)/shard_map/in_back/pallas_call | solution.py:620
  590.0 8.7 %wgrad_send.10.refs_4_ = bf16[2,4,128,1024]{3,2,1,0:T(8,128)(2,1)} custom-call(bf16[1024,2048]{1,0:T(8,128)(2,1)} %get-tuple-element.139.refs_0_.refs_2_, bf16[512,1024]{1,0:T(8,128)(2,1)} %get-tuple-element.146.refs_1_, bf16[1024,2048]{1,0:T(8,128)(2,1)} %get-tuple-element.139.refs_0_.refs_2_, bf16[512,1024]{1,0:T(8,128)(2,1)} %get-tuple-element.147.refs_3_), custom_call_target="tpu_custom_call" | custom-call | flops 3955505664 | tf_op jit(solution)/shard_map/wgrad_send/pallas_call | solution.py:805
  598.7 4.9 wgrad.18
  603.5 5.0 wgrad.19
  609.7 5.8 wgrad.20
  623.8 7.5 %fusion = bf16[1,512,2048]{2,1,0:T(8,128)(2,1)} fusion(bf16[512,2048]{1,0:T(8,128)(2,1)} %collective-permute-done.11, bf16[512,2048]{1,0:T(8,128)(2,1)} %collective-permute-done.5.refs_2_, bf16[512,2048]{1,0:T(8,128)(2,1)} %collective-permute-done.7.refs_2_, bf16[512,2048]{1,0:T(8,128)(2,1)S(1)} %copy-done.9, ...), kind=kLoop, calls=%fused_computation.7 | loop fusion | flops 13631488 | bytes 18874368 | tf_op jit(solution)/shard_map/broadcast_in_dim | solution.py:1130
  631.4 13.3 %collective-permute-done.25 = bf16[2,1024,128]{2,1,0:T(8,128)(2,1)S(1)} collective-permute-done((bf16[2,1024,128]{2,1,0:T(8,128)(2,1)S(1)}, bf16[2,1024,128]{2,1,0:T(8,128)(2,1)S(1)}, u32[]{:S(2)}, u32[]{:S(2)}) %collective-permute-start.25) | collective-permute-done | bytes 524320 | tf_op jit(solution)/shard_map/ppermute | solution.py:871
  648.4 5.1 wgrad.21
  657.7 5.9 collective-permute-done.20
  666.5 14.0 %collective-permute-done.23 = bf16[2,128,1024]{2,1,0:T(8,128)(2,1)S(1)} collective-permute-done((bf16[2,128,1024]{2,1,0:T(8,128)(2,1)S(1)}, bf16[2,128,1024]{2,1,0:T(8,128)(2,1)S(1)}, u32[]{:S(2)}, u32[]{:S(2)}) %collective-permute-start.23) | collective-permute-done | bytes 524320 | tf_op jit(solution)/shard_map/ppermute | solution.py:871
  683.4 7.9 %final.1 = bf16[512,2048]{1,0:T(8,128)(2,1)} custom-call(bf16[512,2048]{1,0:T(8,128)(2,1)} %bitcast.119, bf16[512,2048]{1,0:T(8,128)(2,1)} %get-tuple-element.142.ga_ref, bf16[512,2048]{1,0:T(8,128)(2,1)} %copy-done.7, bf16[512,2048]{1,0:T(8,128)(2,1)} %get-tuple-element.108.refs_1_.h0_ref, bf16[512,2048]{1,0:T(8,128)(2,1)} %get-tuple-element.135.refs_3_.h1_ref, ...), custom_call_target="tpu_custom_call" | custom-call | flops 1680000000 | tf_op jit(solution)/shard_map/final/pallas_call | solution.py:889
  (212 shorter events, 121.1 us)
Async XLA Ops:
  7.2 698.1 %reduce-scatter.8.cloned.1.call-start = ((), (), s32[]{:S(2)}) async-start(), calls=%async_computation.5 | async-start | bytes 3932160 | tf_op jit(solution)/shard_map/reduce_scatter | solution.py:859
  7.2 49.0 %collective-permute-start = (bf16[512,2048]{1,0:T(8,128)(2,1)}, bf16[512,2048]{1,0:T(8,128)(2,1)}, u32[]{:S(2)}, u32[]{:S(2)}) collective-permute-start(bf16[512,2048]{1,0:T(8,128)(2,1)} %bitcast.116), channel_id=1, source_target_pairs={{0,1},{1,0},{2,3},{3,2},{4,5},{5,4},{6,7},{7,6},{8,9},{9,8},{10,11... | collective-permute-start | bytes 6291464 | tf_op jit(solution)/shard_map/ppermute | solution.py:915
  11.2 19.5 %copy-start.19 = (s32[1024]{0:T(1024)}, s32[1024]{0:T(1024)S(1)}, u32[]{:S(2)}) copy-start(s32[1024]{0:T(1024)S(1)} %get-tuple-element.180) | copy-start | bytes 12292
  21.9 25.9 %collective-permute-start.1 = (bf16[512,1024]{1,0:T(8,128)(2,1)}, bf16[512,1024]{1,0:T(8,128)(2,1)S(1)}, u32[]{:S(2)}, u32[]{:S(2)}) collective-permute-start(bf16[512,1024]{1,0:T(8,128)(2,1)} %get-tuple-element.89.rest_0_.rest_6_), channel_id=1, source_target_pairs={{0,2},{2,4},{4,6},{1,3},{3,5},{5,7},{8,10},{10,12},{12,14},{9,11},... | collective-permute-start | bytes 3145736 | tf_op jit(solution)/shard_map/ppermute | solution.py:968
  47.8 15.1 %copy-start.29 = (bf16[512,1024]{1,0:T(8,128)(2,1)}, bf16[512,1024]{1,0:T(8,128)(2,1)S(1)}, u32[]{:S(2)}) copy-start(bf16[512,1024]{1,0:T(8,128)(2,1)S(1)} %collective-permute-done.1.rest_0_.rest_8_) | copy-start | bytes 3145732
  47.8 65.3 %collective-permute-start.2 = (bf16[512,1024]{1,0:T(8,128)(2,1)S(1)}, bf16[512,1024]{1,0:T(8,128)(2,1)S(1)}, u32[]{:S(2)}, u32[]{:S(2)}) collective-permute-start(bf16[512,1024]{1,0:T(8,128)(2,1)S(1)} %collective-permute-done.1.rest_0_.rest_8_), channel_id=1, source_target_pairs={{0,2},{2,4},{4,6},{1,3},{3,5},{5,7},{8,10},{10,12},{12,14},{9,11},... | collective-permute-start | bytes 3145736 | tf_op jit(solution)/shard_map/ppermute | solution.py:968
  62.9 34.4 %collective-permute-start.3 = (bf16[512,1024]{1,0:T(8,128)(2,1)}, bf16[512,1024]{1,0:T(8,128)(2,1)}, u32[]{:S(2)}, u32[]{:S(2)}) collective-permute-start(bf16[512,1024]{1,0:T(8,128)(2,1)} %get-tuple-element.91.rest_1_.rest_7_), channel_id=1, source_target_pairs={{0,2},{2,4},{4,6},{1,3},{3,5},{5,7},{8,10},{10,12},{12,14},{9,11},... | collective-permute-start | bytes 3145736 | tf_op jit(solution)/shard_map/ppermute | solution.py:968
  67.6 80.1 %collective-permute-start.6 = (bf16[512,2048]{1,0:T(8,128)(2,1)S(1)}, bf16[512,2048]{1,0:T(8,128)(2,1)S(1)}, u32[]{:S(2)}, u32[]{:S(2)}) collective-permute-start(bf16[512,2048]{1,0:T(8,128)(2,1)S(1)} %bitcast.124), channel_id=1, source_target_pairs={{0,1},{1,0},{2,3},{3,2},{4,5},{5,4},{6,7},{7,6},{8,9},{9,8},{10,11... | collective-permute-start | bytes 6291464 | tf_op jit(solution)/shard_map/ppermute | solution.py:915
  97.4 23.9 %collective-permute-start.4 = (bf16[512,1024]{1,0:T(8,128)(2,1)}, bf16[512,1024]{1,0:T(8,128)(2,1)}, u32[]{:S(2)}, u32[]{:S(2)}) collective-permute-start(bf16[512,1024]{1,0:T(8,128)(2,1)} %collective-permute-done.3.rest_1_.rest_9_), channel_id=1, source_target_pairs={{0,2},{2,4},{4,6},{1,3},{3,5},{5,7},{8,10},{10,12},{12,14},{9,11},... | collective-permute-start | bytes 3145736 | tf_op jit(solution)/shard_map/ppermute | solution.py:968
  132.8 48.7 %collective-permute-start.5 = (bf16[512,2048]{1,0:T(8,128)(2,1)S(1)}, bf16[512,2048]{1,0:T(8,128)(2,1)}, u32[]{:S(2)}, u32[]{:S(2)}) collective-permute-start(bf16[512,2048]{1,0:T(8,128)(2,1)S(1)} %convolution_convert_fusion.4.refs_1_), channel_id=1, source_target_pairs={{0,1},{1,0},{2,3},{3,2},{4,5},{5,4},{6,7},{7,6},{8,9},{9,8},{10,11... | collective-permute-start | bytes 6291464 | tf_op jit(solution)/shard_map/ppermute | solution.py:915
  146.2 80.3 %collective-permute-start.7 = (bf16[512,2048]{1,0:T(8,128)(2,1)}, bf16[512,2048]{1,0:T(8,128)(2,1)}, u32[]{:S(2)}, u32[]{:S(2)}) collective-permute-start(bf16[512,2048]{1,0:T(8,128)(2,1)} %convolution_convert_fusion.3.refs_1_), channel_id=1, source_target_pairs={{0,1},{1,0},{2,3},{3,2},{4,5},{5,4},{6,7},{7,6},{8,9},{9,8},{10,11... | collective-permute-start | bytes 6291464 | tf_op jit(solution)/shard_map/ppermute | solution.py:915
  148.6 18.7 %copy-start.3 = (bf16[1024,2048]{1,0:T(8,128)(2,1)}, bf16[1024,2048]{1,0:T(8,128)(2,1)S(1)}, u32[]{:S(2)}) copy-start(bf16[1024,2048]{1,0:T(8,128)(2,1)S(1)} %pad_maximum_fusion.refs_6_.refs_1_.refs_3_) | copy-start | bytes 12582916
  219.1 70.1 %collective-permute-start.8 = (bf16[512,2048]{1,0:T(8,128)(2,1)}, bf16[512,2048]{1,0:T(8,128)(2,1)S(1)}, u32[]{:S(2)}, u32[]{:S(2)}) collective-permute-start(bf16[512,2048]{1,0:T(8,128)(2,1)} %get-tuple-element.107.refs_3_), channel_id=1, source_target_pairs={{0,1},{1,0},{2,3},{3,2},{4,5},{5,4},{6,7},{7,6},{8,9},{9,8},{10,11... | collective-permute-start | bytes 6291464 | tf_op jit(solution)/shard_map/ppermute | solution.py:915
  264.2 62.3 %collective-permute-start.9 = (bf16[512,2048]{1,0:T(8,128)(2,1)}, bf16[512,2048]{1,0:T(8,128)(2,1)S(1)}, u32[]{:S(2)}, u32[]{:S(2)}) collective-permute-start(bf16[512,2048]{1,0:T(8,128)(2,1)} %get-tuple-element.112.refs_3_), channel_id=1, source_target_pairs={{0,1},{1,0},{2,3},{3,2},{4,5},{5,4},{6,7},{7,6},{8,9},{9,8},{10,11... | collective-permute-start | bytes 6291464 | tf_op jit(solution)/shard_map/ppermute | solution.py:915
  287.8 71.4 %collective-permute-start.27 = (bf16[1,4,3072,128]{3,2,1,0:T(8,128)(2,1)}, bf16[1,4,3072,128]{3,2,1,0:T(8,128)(2,1)S(1)}, u32[]{:S(2)}, u32[]{:S(2)}) collective-permute-start(bf16[1,4,3072,128]{3,2,1,0:T(8,128)(2,1)} %wgrad.22), channel_id=1, source_target_pairs={{0,16},{8,24},{16,0},{24,8},{1,17},{9,25},{17,1},{25,9},{2,18},{10... | collective-permute-start | bytes 9437192 | tf_op jit(solution)/shard_map/ppermute | solution.py:846
  325.9 152.6 %collective-permute-start.10 = (bf16[1,4,128,3072]{3,2,1,0:T(8,128)(2,1)}, bf16[1,4,128,3072]{3,2,1,0:T(8,128)(2,1)}, u32[]{:S(2)}, u32[]{:S(2)}) collective-permute-start(bf16[1,4,128,3072]{3,2,1,0:T(8,128)(2,1)} %wgrad.12), channel_id=1, source_target_pairs={{0,16},{8,24},{16,0},{24,8},{1,17},{9,25},{17,1},{25,9},{2,18},{10... | collective-permute-start | bytes 9437192 | tf_op jit(solution)/shard_map/ppermute | solution.py:846
  357.9 59.3 %collective-permute-start.12 = (bf16[1024,512]{1,0:T(8,128)(2,1)}, bf16[1024,512]{1,0:T(8,128)(2,1)S(1)}, u32[]{:S(2)}, u32[]{:S(2)}) collective-permute-start(bf16[1024,512]{1,0:T(8,128)(2,1)} %get-tuple-element.130), channel_id=1, source_target_pairs={{2,0},{4,2},{6,4},{3,1},{5,3},{7,5},{10,8},{12,10},{14,12},{11,9},... | collective-permute-start | bytes 3145736 | tf_op jit(solution)/shard_map/ppermute | solution.py:1050
  369.9 338.9 %reduce-scatter.4.cloned.1.call-start = ((), (), s32[]{:S(2)}) async-start(), calls=%async_computation.3 | async-start | bytes 3932160 | tf_op jit(solution)/shard_map/reduce_scatter | solution.py:859
  393.6 21.5 %copy-start.25 = (s32[2]{0:T(128)S(1)}, s32[2]{0:T(128)}, u32[]{:S(2)}) copy-start(s32[2]{0:T(128)} %copy-done.24) | copy-start | bytes 28
  393.6 23.6 %copy-start.15 = (f32[8,2048]{1,0:T(8,128)S(1)}, f32[8,2048]{1,0:T(8,128)}, u32[]{:S(2)}) copy-start(f32[8,2048]{1,0:T(8,128)} %get-tuple-element.153) | copy-start | bytes 196612
  393.6 23.6 %copy-start.16 = (f32[8,2048]{1,0:T(8,128)S(1)}, f32[8,2048]{1,0:T(8,128)}, u32[]{:S(2)}) copy-start(f32[8,2048]{1,0:T(8,128)} %get-tuple-element.154) | copy-start | bytes 196612
  393.6 23.6 %copy-start.12 = (bf16[1024,512]{1,0:T(8,128)(2,1)S(1)}, bf16[1024,512]{1,0:T(8,128)(2,1)}, u32[]{:S(2)}) copy-start(bf16[1024,512]{1,0:T(8,128)(2,1)} %get-tuple-element.129) | copy-start | bytes 3145732
  411.9 62.7 %collective-permute-start.14 = (bf16[1024,512]{1,0:T(8,128)(2,1)}, bf16[1024,512]{1,0:T(8,128)(2,1)}, u32[]{:S(2)}, u32[]{:S(2)}) collective-permute-start(bf16[1024,512]{1,0:T(8,128)(2,1)} %get-tuple-element.133), channel_id=1, source_target_pairs={{2,0},{4,2},{6,4},{3,1},{5,3},{7,5},{10,8},{12,10},{14,12},{11,9},... | collective-permute-start | bytes 3145736 | tf_op jit(solution)/shard_map/ppermute | solution.py:1050
  415.1 59.6 %copy-start.13 = (bf16[1024,512]{1,0:T(8,128)(2,1)S(1)}, bf16[1024,512]{1,0:T(8,128)(2,1)}, u32[]{:S(2)}) copy-start(bf16[1024,512]{1,0:T(8,128)(2,1)} %get-tuple-element.132) | copy-start | bytes 3145732
  415.7 128.7 %collective-permute-start.16 = (bf16[1,4,128,3072]{3,2,1,0:T(8,128)(2,1)}, bf16[1,4,128,3072]{3,2,1,0:T(8,128)(2,1)}, u32[]{:S(2)}, u32[]{:S(2)}) collective-permute-start(bf16[1,4,128,3072]{3,2,1,0:T(8,128)(2,1)} %wgrad.13), channel_id=1, source_target_pairs={{0,16},{8,24},{16,0},{24,8},{1,17},{9,25},{17,1},{25,9},{2,18},{10... | collective-permute-start | bytes 9437192 | tf_op jit(solution)/shard_map/ppermute | solution.py:846
  417.5 145.7 %collective-permute-start.13 = (bf16[1024,512]{1,0:T(8,128)(2,1)S(1)}, bf16[1024,512]{1,0:T(8,128)(2,1)S(1)}, u32[]{:S(2)}, u32[]{:S(2)}) collective-permute-start(bf16[1024,512]{1,0:T(8,128)(2,1)S(1)} %add_convert_fusion.2), channel_id=1, source_target_pairs={{2,0},{4,2},{6,4},{3,1},{5,3},{7,5},{10,8},{12,10},{14,12},{11,9},... | collective-permute-start | bytes 3145736 | tf_op jit(solution)/shard_map/ppermute | solution.py:1050
  477.1 86.0 %collective-permute-start.15 = (bf16[1024,512]{1,0:T(8,128)(2,1)}, bf16[1024,512]{1,0:T(8,128)(2,1)S(1)}, u32[]{:S(2)}, u32[]{:S(2)}) collective-permute-start(bf16[1024,512]{1,0:T(8,128)(2,1)} %add_convert_fusion.1), channel_id=1, source_target_pairs={{2,0},{4,2},{6,4},{3,1},{5,3},{7,5},{10,8},{12,10},{14,12},{11,9},... | collective-permute-start | bytes 3145736 | tf_op jit(solution)/shard_map/ppermute | solution.py:1050
  488.0 223.2 %reduce-scatter.6.cloned.1.call-start = ((), (), s32[]{:S(2)}) async-start(), calls=%async_computation.4 | async-start | bytes 3932160 | tf_op jit(solution)/shard_map/reduce_scatter | solution.py:859
  488.0 19.1 %slice-start = ((s8[12582912]{0:T(1024)(128)(4,1)}), s8[4194304]{0:T(1024)(128)(4,1)S(1)}, s32[]{:S(2)}) async-start(s8[12582912]{0:T(1024)(128)(4,1)} %bitcast.135), calls=%async_computation.6 | async-start | bytes 8388608
  515.5 47.6 %collective-permute-start.11 = (bf16[512,2048]{1,0:T(8,128)(2,1)}, bf16[512,2048]{1,0:T(8,128)(2,1)}, u32[]{:S(2)}, u32[]{:S(2)}) collective-permute-start(bf16[512,2048]{1,0:T(8,128)(2,1)} %get-tuple-element.192), channel_id=1, source_target_pairs={{0,1},{1,0},{2,3},{3,2},{4,5},{5,4},{6,7},{7,6},{8,9},{9,8},{10,11... | collective-permute-start | bytes 6291464 | tf_op jit(solution)/shard_map/ppermute | solution.py:915
  543.2 60.4 %collective-permute-start.18 = (bf16[1,4,1024,128]{3,2,1,0:T(8,128)(2,1)}, bf16[1,4,1024,128]{3,2,1,0:T(8,128)(2,1)}, u32[]{:S(2)}, u32[]{:S(2)}) collective-permute-start(bf16[1,4,1024,128]{3,2,1,0:T(8,128)(2,1)} %wgrad.15), channel_id=1, source_target_pairs={{0,16},{8,24},{16,0},{24,8},{1,17},{9,25},{17,1},{25,9},{2,18},{10... | collective-permute-start | bytes 3145736 | tf_op jit(solution)/shard_map/ppermute | solution.py:846
  544.4 65.3 %collective-permute-start.19 = (bf16[1,4,128,1024]{3,2,1,0:T(8,128)(2,1)}, bf16[1,4,128,1024]{3,2,1,0:T(8,128)(2,1)}, u32[]{:S(2)}, u32[]{:S(2)}) collective-permute-start(bf16[1,4,128,1024]{3,2,1,0:T(8,128)(2,1)} %wgrad.16), channel_id=1, source_target_pairs={{0,16},{8,24},{16,0},{24,8},{1,17},{9,25},{17,1},{25,9},{2,18},{10... | collective-permute-start | bytes 3145736 | tf_op jit(solution)/shard_map/ppermute | solution.py:846
  616.8 28.0 %collective-permute-start.25 = (bf16[2,1024,128]{2,1,0:T(8,128)(2,1)S(1)}, bf16[2,1024,128]{2,1,0:T(8,128)(2,1)S(1)}, u32[]{:S(2)}, u32[]{:S(2)}) collective-permute-start(bf16[2,1024,128]{2,1,0:T(8,128)(2,1)S(1)} %pad_maximum_fusion.4), channel_id=1, source_target_pairs={{0,2},{2,0},{4,6},{6,4},{1,3},{3,1},{5,7},{7,5},{8,10},{10,8},{12,... | collective-permute-start | bytes 1572872 | tf_op jit(solution)/shard_map/ppermute | solution.py:871
  621.9 41.7 %collective-permute-start.20 = (bf16[2,128,1024]{2,1,0:T(8,128)(2,1)}, bf16[2,128,1024]{2,1,0:T(8,128)(2,1)S(1)}, u32[]{:S(2)}, u32[]{:S(2)}) collective-permute-start(bf16[2,128,1024]{2,1,0:T(8,128)(2,1)} %pad_maximum_fusion.2), channel_id=1, source_target_pairs={{0,2},{2,0},{4,6},{6,4},{1,3},{3,1},{5,7},{7,5},{8,10},{10,8},{12,... | collective-permute-start | bytes 1572872 | tf_op jit(solution)/shard_map/ppermute | solution.py:871
  621.9 25.5 %collective-permute-start.22 = (bf16[1,4,128,1024]{3,2,1,0:T(8,128)(2,1)S(1)}, bf16[1,4,128,1024]{3,2,1,0:T(8,128)(2,1)S(1)}, u32[]{:S(2)}, u32[]{:S(2)}) collective-permute-start(bf16[1,4,128,1024]{3,2,1,0:T(8,128)(2,1)S(1)} %copy-done.31), channel_id=1, source_target_pairs={{0,16},{8,24},{16,0},{24,8},{1,17},{9,25},{17,1},{25,9},{2,18},{10... | collective-permute-start | bytes 3145736 | tf_op jit(solution)/shard_map/ppermute | solution.py:846
  622.2 59.9 %collective-permute-start.17 = (bf16[512,2048]{1,0:T(8,128)(2,1)}, bf16[512,2048]{1,0:T(8,128)(2,1)S(1)}, u32[]{:S(2)}, u32[]{:S(2)}) collective-permute-start(bf16[512,2048]{1,0:T(8,128)(2,1)} %get-tuple-element.144), channel_id=1, source_target_pairs={{0,1},{1,0},{2,3},{3,2},{4,5},{5,4},{6,7},{7,6},{8,9},{9,8},{10,11... | collective-permute-start | bytes 6291464 | tf_op jit(solution)/shard_map/ppermute | solution.py:915
  645.8 18.9 %collective-permute-start.26 = (bf16[1024,128]{1,0:T(8,128)(2,1)S(1)}, bf16[1024,128]{1,0:T(8,128)(2,1)S(1)}, u32[]{:S(2)}, u32[]{:S(2)}) collective-permute-start(bf16[1024,128]{1,0:T(8,128)(2,1)S(1)} %fusion.2), channel_id=1, source_target_pairs={{0,4},{2,6},{4,0},{6,2},{1,5},{3,7},{5,1},{7,3},{8,12},{10,14},{12... | collective-permute-start | bytes 786440 | tf_op jit(solution)/shard_map/ppermute | solution.py:873
  654.7 25.9 %copy-start.2 = (bf16[1,4,128,1024]{3,2,1,0:T(8,128)(2,1)S(1)}, bf16[1,4,128,1024]{3,2,1,0:T(8,128)(2,1)}, u32[]{:S(2)}) copy-start(bf16[1,4,128,1024]{3,2,1,0:T(8,128)(2,1)} %wgrad.21) | copy-start | bytes 3145732
  654.7 25.8 %collective-permute-start.23 = (bf16[2,128,1024]{2,1,0:T(8,128)(2,1)S(1)}, bf16[2,128,1024]{2,1,0:T(8,128)(2,1)S(1)}, u32[]{:S(2)}, u32[]{:S(2)}) collective-permute-start(bf16[2,128,1024]{2,1,0:T(8,128)(2,1)S(1)} %pad_maximum_fusion.3), channel_id=1, source_target_pairs={{0,2},{2,0},{4,6},{6,4},{1,3},{3,1},{5,7},{7,5},{8,10},{10,8},{12,... | collective-permute-start | bytes 1572872 | tf_op jit(solution)/shard_map/ppermute | solution.py:871
  663.8 17.4 %collective-permute-start.21 = (bf16[128,1024]{1,0:T(8,128)(2,1)S(1)}, bf16[128,1024]{1,0:T(8,128)(2,1)S(1)}, u32[]{:S(2)}, u32[]{:S(2)}) collective-permute-start(bf16[128,1024]{1,0:T(8,128)(2,1)S(1)} %fusion.10), channel_id=1, source_target_pairs={{0,4},{2,6},{4,0},{6,2},{1,5},{3,7},{5,1},{7,3},{8,12},{10,14},{12... | collective-permute-start | bytes 786440 | tf_op jit(solution)/shard_map/ppermute | solution.py:873
  680.7 14.5 %collective-permute-start.24 = (bf16[128,1024]{1,0:T(8,128)(2,1)S(1)}, bf16[128,1024]{1,0:T(8,128)(2,1)S(1)}, u32[]{:S(2)}, u32[]{:S(2)}) collective-permute-start(bf16[128,1024]{1,0:T(8,128)(2,1)S(1)} %fusion.6), channel_id=1, source_target_pairs={{0,4},{2,6},{4,0},{6,2},{1,5},{3,7},{5,1},{7,3},{8,12},{10,14},{12... | collective-permute-start | bytes 786440 | tf_op jit(solution)/shard_map/ppermute | solution.py:873
  691.3 3.9 collective-permute-start.30
  692.0 3.9 collective-permute-start.29
  692.8 3.1 collective-permute-start.28
  695.9 5.7 collective-permute-start.33
  698.1 4.7 collective-permute-start.32
  699.9 3.8 collective-permute-start.31
  703.7 3.9 collective-permute-start.34
  (26 other events, 191.4 us)
Sparse Core Ops, SparseCore 0:
  370.0 90.5 reduce-scatter.7
  488.1 84.6 reduce-scatter.3
  575.1 75.7 reduce-scatter.5
